TPU v7x, 32 devices: a whole 2x2x4 slice. The times are simulated.
32 devices in a mesh: dp: 4 (over z), expert: 8 (over y, x, core).
Axes of the slice: x: 2, y: 2, z: 4, core: 2. Of those that a mesh axis runs over, the one named last changes fastest.
Arguments:
- tokens: bfloat16 [8192, 1280], P(('dp', 'expert')), may hold values from -14 to 14
- ln_gain: float32 [1280], replicated, may hold values from 0.25 to 1.75
- router: bfloat16 [1280, 8], replicated, may hold values from -0.3125 to 0.3125
- w_in: bfloat16 [8, 5120, 1280], P('expert', 'dp'), may hold values from -0.15625 to 0.15625
- b_in: bfloat16 [8, 5120], P('expert', 'dp'), may hold values from -3 to 3
- w_out: bfloat16 [8, 5120, 1280], P('expert', 'dp'), may hold values from -0.078125 to 0.078125
- b_out: bfloat16 [8, 1280], P('expert'), may hold values from -3 to 3
- expert_choice: int32 [8192], P(('dp', 'expert')), may hold values from 0 to 7
- modality: int32 [8192], P(('dp', 'expert')), may hold values from 0 to 1, as said below
- slot: int32 [8192], P(('dp', 'expert')), may hold values from -1 to 15, as said below
Outputs:
- moe_out: bfloat16 [8192, 1280], P(('dp', 'expert'))
- aux_losses: float32 [2, 2], replicated
Inputs may be any that keep to these rules, and one draw needn't show every extreme that they name: Each source's tokens with one expert and a slot other than -1 have distinct slots, numbered from 0 in token order; one expert has all 16 slots filled in every source. `modality`: every source holds tokens of both modalities.
All inputs are finite; a program needn't handle non-finite values.
Results may differ from a plain program's by a relative error of at most 0.007.
Values may be sent and summed in bfloat16 or wider, within the bound.
No kernel may reach another device: no remote copies, remote signals or barrier semaphores. Data moves between devices by JAX's collectives and lax.ppermute only.
A program may use at most 128 MiB of HBM per device.

v0:
```python
import jax
import jax.numpy as jnp
from jax import lax
from jax.sharding import PartitionSpec as P

CAP = 16


def layer_norm(tokens, ln_gain):
    values = tokens.astype(jnp.float32)
    center = values - jnp.mean(values, axis=-1, keepdims=True)
    spread = jnp.mean(center * center, axis=-1, keepdims=True)
    return (center * lax.rsqrt(spread + 1e-06) * ln_gain).astype(jnp.bfloat16)


def expert_hidden(rows, first, first_bias, second):
    pre = lax.dot_general(rows, first, (((1,), (1,)), ((), ())), preferred_element_type=jnp.float32)
    hidden = jax.nn.gelu(pre + first_bias.astype(jnp.float32), approximate=False).astype(
        jnp.bfloat16
    )
    return jnp.dot(hidden, second, preferred_element_type=jnp.float32)


def on_device(tokens, ln_gain, router, w_in, b_in, w_out, b_out, expert_choice, modality, slot):
    normed = layer_norm(tokens, ln_gain)
    logits = jnp.dot(normed, router, preferred_element_type=jnp.float32)
    logp = jax.nn.log_softmax(logits, axis=-1)
    probs = jnp.exp(logp)
    gate = jnp.take_along_axis(probs, expert_choice[:, None], axis=1)[:, 0]
    experts_all = router.shape[1]
    width = normed.shape[1]
    columns = experts_all * CAP
    target = jnp.where(slot >= 0, expert_choice * CAP + slot, -1)
    table = (target[:, None] == jnp.arange(columns, dtype=jnp.int32)[None, :]).astype(jnp.bfloat16)
    buffer = jnp.einsum("tk,td->kd", table, normed, preferred_element_type=jnp.float32).astype(
        jnp.bfloat16
    )
    received = lax.all_to_all(
        buffer.reshape(experts_all, CAP, width), "expert", split_axis=0, concat_axis=0, tiled=True
    )
    senders = lax.axis_size("expert")
    local_count = w_in.shape[0]
    received = received.reshape(senders, local_count, CAP, width)
    rows = received[:, 0].reshape(senders * CAP, width)
    gathered = lax.all_gather(rows, "dp", axis=0, tiled=True)
    summed = lax.psum_scatter(
        expert_hidden(gathered, w_in[0], b_in[0], w_out[0]), "dp", scatter_dimension=0, tiled=True
    )
    results = [
        (summed + b_out[0].astype(jnp.float32)).astype(jnp.bfloat16).reshape(senders, CAP, width)
    ]
    outputs = jnp.stack(results, axis=1).reshape(experts_all, CAP, width)
    returned = lax.all_to_all(outputs, "expert", split_axis=0, concat_axis=0, tiled=True)
    fetched = jnp.dot(table, returned.reshape(columns, width), preferred_element_type=jnp.float32)
    moe_out = (gate[:, None] * fetched).astype(jnp.bfloat16)
    textual = (modality == 1).astype(jnp.float32)
    select = jnp.stack([1.0 - textual, textual], axis=0)
    entropy = -jnp.sum(probs * logp, axis=-1)
    prob_part = jnp.dot(select, probs, precision=lax.Precision.HIGHEST)
    ent_part = jnp.dot(select, entropy, precision=lax.Precision.HIGHEST)
    count_part = jnp.sum(select, axis=1)
    prob_sum, ent_sum, count = lax.psum((prob_part, ent_part, count_part), ("dp", "expert"))
    pbar = prob_sum / count[:, None]
    aux_losses = jnp.stack([ent_sum / count, jnp.sum(pbar * jnp.log(pbar), axis=1)], axis=1)
    return (moe_out, aux_losses)


def solution(mesh):
    return jax.shard_map(
        on_device,
        mesh=mesh,
        in_specs=(
            P(("dp", "expert"), None),
            P(),
            P(),
            P("expert", "dp", None),
            P("expert", "dp"),
            P("expert", "dp", None),
            P("expert", None),
            P(("dp", "expert")),
            P(("dp", "expert")),
            P(("dp", "expert")),
        ),
        out_specs=(P(("dp", "expert"), None), P()),
        check_vma=False,
    )
```

profile of v0, /device:TPU:0, one launch (start us, length us, event | category | flops | bytes accessed | tf_op | source)
XLA Modules:
  0.0 144.7 jit_solution(16310733744528008156)
XLA Ops:
  7.2 0.0 all-gather.2.cloned.1.call-start
  7.3 1.4 convert_reduce_fusion
  8.7 1.4 fusion.18
  10.1 1.4 fusion.20
  11.5 0.8 copy-done.1
  12.3 0.4 convolution_convert_fusion
  12.7 12.7 %all_to_all.10 = bf16[8,16,1280]{2,1,0:T(8,128)(2,1)} all-to-all(bf16[8,16,1280]{2,1,0:T(8,128)(2,1)S(1)} %bitcast.35), channel_id=1, replica_groups=mesh['dp'=4,'expert'=8] {'expert'}, dimensions={0} | all-to-all | bytes 655360 | tf_op jit(solution)/shard_map/all_to_all | solution.py:38
  25.4 0.0 reduce-scatter.2.cloned.1.call-start
  25.5 32.0 %all-gather.2.cloned.1.call-done = bf16[512,1280]{1,0:T(8,128)(2,1)} async-done(((bf16[128,1280]{1,0:T(8,128)(2,1)}), bf16[512,1280]{1,0:T(8,128)(2,1)}) %all-gather.2.cloned.1.call-update) | async-done | bytes 1310736 | tf_op jit(solution)/shard_map/all_gather | solution.py:45
  57.5 12.3 %fusion = f32[512,1280]{1,0:T(8,128)} fusion(bf16[1,1280,1280]{2,1,0:T(8,128)(2,1)S(1)} %copy-done, bf16[512,1280]{1,0:T(8,128)(2,1)} %all-gather.2.cloned.1.call-done, bf16[1,1280,1280]{2,1,0:T(8,128)(2,1)} %param.13, f32[1280]{0:T(1024)S(1)} %convert_reduce_fusion.2), kind=kOutput, calls=%fused_computation.3 | convolution fusion | flops 3398696960 | bytes 10490880 | tf_op jit(solution)/shard_map/dot_general | solution.py:21
  69.8 0.7 copy-done.2
  70.5 1.4 fusion.61
  72.0 0.1 convolution_bitcast_fusion
  72.1 0.1 fusion.29
  72.3 0.1 fusion.60
  72.4 41.3 %all-reduce = (f32[2,8]{1,0:T(2,128)S(1)}, f32[2]{0:T(128)S(1)}, f32[2]{0:T(128)S(1)}) all-reduce(f32[2,8]{1,0:T(2,128)S(1)} %fusion.29, f32[2]{0:T(128)S(1)} %fusion.60, f32[2]{0:T(128)S(1)} %convolution_bitcast_fusion), channel_id=1, replica_groups=mesh['dp'=4,'expert'=8] {'dp','expert'}, use_global_device_ids=true, to_apply=%region_9.10 | all-reduce | flops 20 | bytes 160 | tf_op jit(solution)/shard_map/psum | solution.py:62
  113.7 0.2 fusion.25
  114.0 8.2 %reduce-scatter.2.cloned.1.call-done = f32[128,1280]{1,0:T(8,128)} async-done(((f32[512,1280]{1,0:T(8,128)}), f32[128,1280]{1,0:T(8,128)}) %reduce-scatter.2.cloned.1.call-update) | async-done | bytes 655376 | tf_op jit(solution)/shard_map/reduce_scatter | solution.py:46
  122.1 1.9 %add_convert_fusion = bf16[128,1280]{1,0:T(8,128)(2,1)} fusion(f32[128,1280]{1,0:T(8,128)} %reduce-scatter.2.cloned.1.call-done, f32[1280]{0:T(1024)S(1)} %convert_reduce_fusion.1), kind=kLoop, calls=%fused_computation.35 | loop fusion | flops 327680 | bytes 988160 | tf_op jit(solution)/shard_map/convert_element_type | solution.py:50
  124.0 4.1 %all-to-all-start.1 = ((bf16[8,16,1280]{2,1,0:T(8,128)(2,1)}), bf16[8,16,1280]{2,1,0:T(8,128)(2,1)}, u32[]{:S(2)}, u32[]{:S(2)}) async-start(bf16[8,16,1280]{2,1,0:T(8,128)(2,1)} %bitcast.33), calls=%async_computation.2 | async-start | bytes 655360 | tf_op jit(solution)/shard_map/all_to_all | solution.py:53
  128.1 0.6 copy.14
  128.7 1.8 %gather_fusion = f32[256]{0:T(256)S(1)} fusion(f32[256,8]{0,1:T(8,128)S(1)} %get-tuple-element.12, s32[256]{0:T(256)S(1)} %bitcast.32), kind=kCustom, calls=%fused_computation | custom fusion | bytes 4096 | tf_op jit(solution)/shard_map/jit(take_along_axis)/gather | solution.py:29
  130.6 5.1 %all-to-all-done.1 = bf16[8,16,1280]{2,1,0:T(8,128)(2,1)} async-done(((bf16[8,16,1280]{2,1,0:T(8,128)(2,1)}), bf16[8,16,1280]{2,1,0:T(8,128)(2,1)}, u32[]{:S(2)}, u32[]{:S(2)}) %all-to-all-start.1) | async-done | bytes 327712 | tf_op jit(solution)/shard_map/all_to_all | solution.py:53
  135.7 2.2 %fusion.15 = bf16[256,1280]{1,0:T(8,128)(2,1)} fusion(bf16[128,1280]{1,0:T(8,128)(2,1)} %bitcast.8, f32[256]{0:T(256)S(1)} %and_select_fusion, s32[256]{0:T(256)S(1)} %get-tuple-element.14), kind=kOutput, calls=%fused_computation.25 | convolution fusion | flops 84574208 | bytes 985088 | tf_op jit(solution)/shard_map/dot_general | solution.py:54
  (33 shorter events, 0.2 us)
Async XLA Ops:
  7.2 50.3 %copy-start = (bf16[1,1280,1280]{2,1,0:T(8,128)(2,1)S(1)}, bf16[1,1280,1280]{2,1,0:T(8,128)(2,1)}, u32[]{:S(2)}) copy-start(bf16[1,1280,1280]{2,1,0:T(8,128)(2,1)} %param.15) | copy-start | bytes 9830404
  7.2 4.3 %copy-start.6 = (s32[256]{0:T(256)S(1)}, s32[256]{0:T(256)}, u32[]{:S(2)}) copy-start(s32[256]{0:T(256)} %param.17) | copy-start | bytes 3076
  7.2 4.3 %copy-start.7 = (s32[256]{0:T(256)S(1)}, s32[256]{0:T(256)}, u32[]{:S(2)}) copy-start(s32[256]{0:T(256)} %param.19) | copy-start | bytes 3076
  7.2 18.3 %copy-start.3 = (bf16[1,1280]{1,0:T(2,128)(2,1)S(1)}, bf16[1,1280]{1,0:T(2,128)(2,1)}, u32[]{:S(2)}) copy-start(bf16[1,1280]{1,0:T(2,128)(2,1)} %param.14) | copy-start | bytes 7684
  7.2 50.2 %all-gather.2.cloned.1.call-start = ((), (), s32[]{:S(2)}) async-start(), calls=%async_computation.3 | async-start | bytes 1638400 | tf_op jit(solution)/shard_map/all_gather | solution.py:45
  11.5 0.8 copy-start.1
  25.4 96.7 %reduce-scatter.2.cloned.1.call-start = ((), (), s32[]{:S(2)}) async-start(), calls=%async_computation.4 | async-start | bytes 3276800 | tf_op jit(solution)/shard_map/reduce_scatter | solution.py:46
  69.8 0.7 copy-start.2
  69.8 2.2 %copy-start.5 = (s32[256]{0:T(256)S(1)}, s32[256]{0:T(256)}, u32[]{:S(2)}) copy-start(s32[256]{0:T(256)} %param.18) | copy-start | bytes 3076
  69.8 44.0 %copy-start.4 = (bf16[1,1280]{1,0:T(2,128)(2,1)S(1)}, bf16[1,1280]{1,0:T(2,128)(2,1)}, u32[]{:S(2)}) copy-start(bf16[1,1280]{1,0:T(2,128)(2,1)} %param.16) | copy-start | bytes 7684
  124.0 11.7 %all-to-all-start.1 = ((bf16[8,16,1280]{2,1,0:T(8,128)(2,1)}), bf16[8,16,1280]{2,1,0:T(8,128)(2,1)}, u32[]{:S(2)}, u32[]{:S(2)}) async-start(bf16[8,16,1280]{2,1,0:T(8,128)(2,1)} %bitcast.33), calls=%async_computation.2 | async-start | bytes 655360 | tf_op jit(solution)/shard_map/all_to_all | solution.py:53
Sparse Core Ops, SparseCore 0:
  25.5 31.8 all-gather.1
  69.9 52.1 reduce-scatter.1
where the time goes:
time: 145 us
  blocking collectives  54 us (37%)
  waiting for transfers between devices  45.3 us (31%)
  matrix products  16.5 us (11%)
  between operations  14.3 us (10%)
  other arithmetic  6.49 us (4%)
  starting transfers between devices  4.15 us (3%)
  local copies, waits for them, and re-layouts  4.02 us (3%)
    psum x1, blocking collectives, on_device(): lax.psum((prob_part, ent_part, count_part), ('dp', 'expert'))  41.3 us
    all_gather x1, waiting for transfers between devices, on_device(): gathered = lax.all_gather(rows, 'dp', axis=0, tiled=True)  32 us
    all_to_all x1, blocking collectives, on_device(): lax.all_to_all(buffer.reshape(experts_all, CAP, width), 'expert', split_a...  12.7 us
    dot_general x1, matrix products, expert_hidden(): return jnp.dot(hidden, second, preferred_element_type=jnp.float32)  12.3 us
    reduce_scatter x1, waiting for transfers between devices, on_device(): lax.psum_scatter(expert_hidden(gathered, w_in[0], b_in[0], w_out[0]), 'dp...  8.17 us
    all_to_all x1, waiting for transfers between devices, on_device(): lax.all_to_all(outputs, 'expert', split_axis=0, concat_axis=0, tiled=True)  5.12 us
    all_to_all x1, starting transfers between devices, on_device(): lax.all_to_all(outputs, 'expert', split_axis=0, concat_axis=0, tiled=True)  4.07 us
  transfers between devices with their start and end apart: 3, of which 3 were waited for; matrix products, arithmetic and copies ran while one was open for 3% of the time, Pallas kernels for 0%

commit v1 on v0

v1 whole, which is shorter than its diff:
```python
import functools

import jax
import jax.numpy as jnp
from jax import lax
from jax.experimental import pallas as pl
from jax.experimental.pallas import tpu as pltpu
from jax.sharding import PartitionSpec as P

CAP = 16
CHUNKS = 2
AXES = ("dp", "expert")
VMEM = pl.BlockSpec(memory_space=pltpu.VMEM)


def dispatch_kernel(copies, chunk, tokens, gain, target, normed_out, *buffers):
    values = tokens[...].astype(jnp.float32)
    center = values - jnp.mean(values, axis=-1, keepdims=True)
    spread = jnp.mean(center * center, axis=-1, keepdims=True)
    normed = (center * lax.rsqrt(spread + 1e-06) * gain[...]).astype(jnp.bfloat16)
    normed_out[...] = normed
    for index, buffer in enumerate(buffers):
        rows = buffer.shape[1]
        row = lax.broadcasted_iota(jnp.int32, (rows, normed.shape[0]), 0)
        key = (row // chunk) * CAP + index * chunk + row % chunk
        table = (key == target[...]).astype(jnp.float32).astype(jnp.bfloat16)
        packed = jnp.dot(table, normed, preferred_element_type=jnp.float32).astype(jnp.bfloat16)
        for copy in range(copies):
            buffer[copy] = packed


def router_kernel(normed, router, choice, modality, gate_out, stats_out):
    logits = lax.dot_general(
        router[...], normed[...], (((1,), (1,)), ((), ())), preferred_element_type=jnp.float32
    )
    peak = jnp.max(logits, axis=0, keepdims=True)
    shifted = logits - peak
    logp = shifted - jnp.log(jnp.sum(jnp.exp(shifted), axis=0, keepdims=True))
    probs = jnp.exp(logp)
    expert = lax.broadcasted_iota(jnp.int32, probs.shape, 0)
    gate = jnp.sum(jnp.where(expert == choice[...], probs, 0.0), axis=0, keepdims=True)
    gate_out[...] = jnp.broadcast_to(gate, gate_out.shape)
    textual = (modality[...] == 1).astype(jnp.float32)
    entropy = -jnp.sum(probs * logp, axis=0, keepdims=True)
    lane = lax.broadcasted_iota(jnp.int32, stats_out.shape, 1)
    stats = jnp.zeros(stats_out.shape, jnp.float32)
    for kind, select in enumerate((1.0 - textual, textual)):
        prob_sum = jnp.sum(probs * select, axis=1, keepdims=True)
        ent_sum = jnp.sum(entropy * select, axis=1, keepdims=True)
        count = jnp.sum(select, axis=1, keepdims=True)
        for place, value in enumerate((prob_sum, ent_sum, count)):
            stats = jnp.where(lane == 2 * place + kind, value, stats)
    stats_out[...] = stats


def expert_kernel(rows, first, first_bias, second, last_bias, out, total):
    step = pl.program_id(0)

    @pl.when(step == 0)
    def _():
        total[...] = jnp.broadcast_to(last_bias[...], total.shape)

    pre = lax.dot_general(
        rows[...], first[...], (((1,), (1,)), ((), ())), preferred_element_type=jnp.float32
    )
    pre = pre + first_bias[...].astype(jnp.float32)
    hidden = (0.5 * pre * (1.0 + lax.erf(pre * (0.5**0.5)))).astype(jnp.bfloat16)
    total[...] += jnp.dot(hidden, second[...], preferred_element_type=jnp.float32)

    @pl.when(step == pl.num_programs(0) - 1)
    def _():
        out[...] = total[...].astype(jnp.bfloat16)


def combine_kernel(chunk, target, gate, stats, *refs):
    returned, (out, aux) = refs[:-2], refs[-2:]
    fetched = None
    experts = stats.shape[1]
    for index, part in enumerate(returned):
        row = lax.broadcasted_iota(jnp.int32, (part.shape[0], target.shape[1]), 0)
        row = row % (experts * chunk)
        key = (row // chunk) * CAP + index * chunk + row % chunk
        table = (key == target[...]).astype(jnp.float32).astype(jnp.bfloat16)
        term = lax.dot_general(
            table, part[...], (((0,), (0,)), ((), ())), preferred_element_type=jnp.float32
        )
        fetched = term if fetched is None else fetched + term
    scale = jnp.transpose(gate[...])[:, 0:1]
    out[...] = (scale * fetched).astype(jnp.bfloat16)
    sums = jnp.sum(stats[...], axis=0)
    row = lax.broadcasted_iota(jnp.int32, aux.shape, 0)
    column = lax.broadcasted_iota(jnp.int32, aux.shape, 1)
    result = jnp.zeros(aux.shape, jnp.float32)
    for kind in range(2):
        count = sums[0:1, 4 + kind : 5 + kind]
        local = sums[0:1, 2 + kind : 3 + kind] / count
        pbar = sums[:, kind : kind + 1] / sums[:, 4 + kind : 5 + kind]
        spread = jnp.sum(pbar * jnp.log(pbar), axis=0, keepdims=True)
        result = jnp.where((row == kind) & (column == 0), local, result)
        result = jnp.where((row == kind) & (column == 1), spread, result)
    aux[...] = result


def on_device(tokens, ln_gain, router, w_in, b_in, w_out, b_out, expert_choice, modality, slot):
    count, width = tokens.shape
    experts = router.shape[1]
    layers, senders = lax.axis_size("dp"), lax.axis_size("expert")
    assert w_in.shape[0] == 1 and experts == senders
    chunk = CAP // CHUNKS
    target = jnp.where(slot >= 0, expert_choice * CAP + slot, -1).reshape(1, count)
    normed, *buffers = pl.pallas_call(
        functools.partial(dispatch_kernel, layers, chunk),
        out_shape=[jax.ShapeDtypeStruct((count, width), jnp.bfloat16)]
        + [jax.ShapeDtypeStruct((layers, experts * chunk, width), jnp.bfloat16)] * CHUNKS,
        in_specs=[VMEM] * 3,
        out_specs=[VMEM] * (1 + CHUNKS),
        name="dispatch",
    )(tokens, ln_gain.reshape(1, width), target)
    devices = layers * senders

    def exchange(block):
        return lax.all_to_all(
            block.reshape(devices, chunk, width), AXES, split_axis=0, concat_axis=0, tiled=True
        ).reshape(devices * chunk, width)

    received = [exchange(buffer) for buffer in buffers]
    gate, stats = pl.pallas_call(
        router_kernel,
        out_shape=[
            jax.ShapeDtypeStruct((8, count), jnp.float32),
            jax.ShapeDtypeStruct((experts, 128), jnp.float32),
        ],
        in_specs=[VMEM] * 4,
        out_specs=[VMEM] * 2,
        name="router",
    )(normed, router.T, expert_choice.reshape(1, count), modality.reshape(1, count))
    stats = lax.all_to_all(
        jnp.broadcast_to(stats[None], (devices, experts, 128)), AXES, split_axis=0, concat_axis=0, tiled=True
    )
    hidden = w_in.shape[1]
    block = 256
    rows = devices * chunk
    last_bias = jnp.where(lax.axis_index("dp") == 0, b_out.astype(jnp.float32), 0.0)
    returned = []
    for part in received:
        partial = pl.pallas_call(
            expert_kernel,
            grid=(hidden // block,),
            out_shape=jax.ShapeDtypeStruct((rows, width), jnp.bfloat16),
            in_specs=[
                pl.BlockSpec((rows, width), lambda i: (0, 0)),
                pl.BlockSpec((None, block, width), lambda i: (0, i, 0)),
                pl.BlockSpec((1, block), lambda i: (0, i)),
                pl.BlockSpec((None, block, width), lambda i: (0, i, 0)),
                pl.BlockSpec((1, width), lambda i: (0, 0)),
            ],
            out_specs=pl.BlockSpec((rows, width), lambda i: (0, 0)),
            scratch_shapes=[pltpu.VMEM((rows, width), jnp.float32)],
            cost_estimate=pl.CostEstimate(
                flops=4 * rows * width * hidden,
                bytes_accessed=4 * width * (hidden + rows),
                transcendentals=rows * hidden,
            ),
            name="expert",
        )(part, w_in, b_in, w_out, last_bias)
        returned.append(exchange(partial))
    return pl.pallas_call(
        functools.partial(combine_kernel, chunk),
        out_shape=[
            jax.ShapeDtypeStruct((count, width), jnp.bfloat16),
            jax.ShapeDtypeStruct((2, 2), jnp.float32),
        ],
        in_specs=[VMEM] * (3 + CHUNKS),
        out_specs=[VMEM] * 2,
        name="combine",
    )(target, gate, stats, *returned)


def solution(mesh):
    return jax.shard_map(
        on_device,
        mesh=mesh,
        in_specs=(
            P(AXES, None),
            P(),
            P(),
            P("expert", "dp", None),
            P("expert", "dp"),
            P("expert", "dp", None),
            P("expert", None),
            P(AXES),
            P(AXES),
            P(AXES),
        ),
        out_specs=(P(AXES, None), P()),
        check_vma=False,
    )
```

time: 145 us -> 113 us (0.78)
  waiting for transfers between devices: 45.3 us -> 19.5 us
  Pallas kernels: 0 us -> 23.6 us
  matrix products: 16.5 us -> 0 us
  between operations: 14.3 us -> 0.69 us
  other arithmetic: 6.49 us -> 1.87 us
  blocking collectives: 54 us -> 58.3 us
  starting transfers between devices: 4.15 us -> 6.73 us
  local copies, waits for them, and re-layouts: 4.02 us -> 2 us
    all_to_all x1 -> x3, blocking collectives: 12.7 us -> 58.3 us  [the longest x2 42.8 us: exchange(): lax.all_to_all(block.reshape(devices, chunk, width), AXES, split_axis=0,...]
    psum x1 -> x0, blocking collectives: 41.3 us -> none  [on_device(): lax.psum((prob_part, ent_part, count_part), ('dp', 'expert'))]
    all_gather x1 -> x0, waiting for transfers between devices: 32 us -> none  [on_device(): gathered = lax.all_gather(rows, 'dp', axis=0, tiled=True)]
    pallas_call x0 -> x5, Pallas kernels: none -> 23.6 us  [the longest x2 15.9 us: on_device(): pl.pallas_call(expert_kernel, grid=(hidden // block,), out_shape=jax.Shap...]
    dot_general x6 -> x0, matrix products: 16.5 us -> none  [the longest x1 12.3 us: expert_hidden(): return jnp.dot(hidden, second, preferred_element_type=jnp.float32)]
    all_to_all x1 -> x2, waiting for transfers between devices: 5.12 us -> 19.5 us  [exchange(): lax.all_to_all(block.reshape(devices, chunk, width), AXES, split_axis=0,...]
    reduce_scatter x1 -> x0, waiting for transfers between devices: 8.17 us -> none  [on_device(): lax.psum_scatter(expert_hidden(gathered, w_in[0], b_in[0], w_out[0]), 'dp...]
    convert_element_type x3 -> x0, other arithmetic: 3.21 us -> none  [the longest x1 1.85 us: on_device(): (summed + b_out[0].astype(jnp.float32)).astype(jnp.bfloat16)]
  transfers between devices with their start and end apart: 3 -> 2, of which waited for: 3 -> 2; matrix products, arithmetic and copies ran while one was open for 3% -> 1% of each run, Pallas kernels for 0% -> 14%
where the time goes in v1:
time: 113 us
  blocking collectives  58.3 us (52%)
  Pallas kernels  23.6 us (21%)
  waiting for transfers between devices  19.5 us (17%)
  starting transfers between devices  6.73 us (6%)
  local copies, waits for them, and re-layouts  2 us (2%)
  other arithmetic  1.87 us (2%)
    all_to_all x2, blocking collectives, exchange(): lax.all_to_all(block.reshape(devices, chunk, width), AXES, split_axis=0,...  42.8 us
    all_to_all x2, waiting for transfers between devices, exchange(): lax.all_to_all(block.reshape(devices, chunk, width), AXES, split_axis=0,...  19.5 us
    pallas_call x2, Pallas kernels, on_device(): pl.pallas_call(expert_kernel, grid=(hidden // block,), out_shape=jax.Shap...  15.9 us
    all_to_all x1, blocking collectives, on_device(): lax.all_to_all(jnp.broadcast_to(stats[None], (devices, experts, 128)), AX...  15.4 us
    all_to_all x2, starting transfers between devices, exchange(): lax.all_to_all(block.reshape(devices, chunk, width), AXES, split_axis=0,...  6.73 us
    pallas_call x1, Pallas kernels, on_device(): pl.pallas_call(functools.partial(dispatch_kernel, layers, chunk), out_sha...  2.84 us
    pallas_call x1, Pallas kernels, on_device(): pl.pallas_call(functools.partial(combine_kernel, chunk), out_shape=[jax.S...  2.76 us
  transfers between devices with their start and end apart: 2, of which 2 were waited for; matrix products, arithmetic and copies ran while one was open for 1% of the time, Pallas kernels for 14%

profile of v1, /device:TPU:0, one launch (start us, length us, event | category | flops | bytes accessed | tf_op | source)
XLA Modules:
  0.0 112.6 jit_solution(9530007395403428762)
XLA Ops:
  0.6 0.0 copy-start.2
  0.6 1.3 %reshape.42.gain = f32[1,1280]{1,0:T(1,128)} reshape(f32[1280]{0:T(1024)} %param.11) | data formatting | bytes 10240 | tf_op jit(solution)/shard_map/reshape | solution.py:118
  1.9 1.3 %compare_select_fusion = s32[256]{0:T(256)} fusion(s32[256]{0:T(256)} %param.19, s32[256]{0:T(256)} %param.17), kind=kLoop, calls=%fused_computation.1 | loop fusion | flops 1024 | bytes 3072 | tf_op jit(solution)/shard_map/jit(_where)/select_n | solution.py:110
  3.2 2.8 %dispatch.1 = (bf16[256,1280]{1,0:T(8,128)(2,1)}, bf16[4,64,1280]{2,1,0:T(8,128)(2,1)}, bf16[4,64,1280]{2,1,0:T(8,128)(2,1)}) custom-call(bf16[256,1280]{1,0:T(8,128)(2,1)} %tokens.1, f32[1,1280]{1,0:T(1,128)} %reshape.42.gain, s32[1,256]{1,0:T(1,128)} %bitcast.21), custom_call_target="tpu_custom_call" | custom-call | tf_op jit(solution)/shard_map/dispatch/pallas_call | solution.py:111
  6.0 2.1 %router.1 = (f32[8,256]{1,0:T(8,128)}, f32[8,128]{1,0:T(8,128)}) custom-call(bf16[256,1280]{1,0:T(8,128)(2,1)} %get-tuple-element.7.normed, bf16[8,1280]{1,0:T(8,128)(2,1)} %bitcast.20, s32[1,256]{1,0:T(1,128)} %bitcast.23, s32[1,256]{1,0:T(1,128)} %bitcast.24), custom_call_target="tpu_custom_call" | custom-call | tf_op jit(solution)/shard_map/router/pallas_call | solution.py:127
  8.2 0.7 broadcast_in_dim.15
  8.9 15.4 %all_to_all.25.stats = f32[32,8,128]{2,1,0:T(8,128)} all-to-all(f32[32,8,128]{2,1,0:T(8,128)S(1)} %broadcast_in_dim.15), channel_id=1, replica_groups=mesh['dp'=4,'expert'=8] {'dp','expert'}, dimensions={0} | all-to-all | bytes 262144 | tf_op jit(solution)/shard_map/all_to_all | solution.py:137
  24.3 21.3 %all_to_all.26 = bf16[32,8,1280]{2,1,0:T(8,128)(2,1)} all-to-all(bf16[32,8,1280]{2,1,0:T(8,128)(2,1)} %bitcast.19), channel_id=1, replica_groups=mesh['dp'=4,'expert'=8] {'dp','expert'}, dimensions={0} | all-to-all | bytes 1310720 | tf_op jit(solution)/shard_map/all_to_all | solution.py:122
  45.6 3.3 %all-to-all-start.3 = ((bf16[32,8,1280]{2,1,0:T(8,128)(2,1)}), bf16[32,8,1280]{2,1,0:T(8,128)(2,1)S(1)}, u32[]{:S(2)}, u32[]{:S(2)}) async-start(bf16[32,8,1280]{2,1,0:T(8,128)(2,1)} %bitcast.18), calls=%async_computation.3 | async-start | bytes 1310720 | tf_op jit(solution)/shard_map/all_to_all | solution.py:122
  49.0 0.0 copy-done.2
  49.0 0.6 broadcast_select_fusion.last_bias
  49.6 7.9 %expert.2 = bf16[256,1280]{1,0:T(8,128)(2,1)} custom-call(bf16[256,1280]{1,0:T(8,128)(2,1)} %bitcast.13, bf16[1,1280,1280]{2,1,0:T(8,128)(2,1)} %first.3, bf16[1,1280]{1,0:T(2,128)(2,1)} %first_bias.3, bf16[1,1280,1280]{2,1,0:T(8,128)(2,1)} %second.3, f32[1,1280]{1,0:T(1,128)} %broadcast_select_fusion.last_bias), custom_call_target="tpu_custom_call" | custom-call | flops 1677721600 | bytes 7864320 | tf_op jit(solution)/shard_map/expert/pallas_call | solution.py:146
  57.5 9.5 %all-to-all-done.3 = bf16[32,8,1280]{2,1,0:T(8,128)(2,1)S(1)} async-done(((bf16[32,8,1280]{2,1,0:T(8,128)(2,1)}), bf16[32,8,1280]{2,1,0:T(8,128)(2,1)S(1)}, u32[]{:S(2)}, u32[]{:S(2)}) %all-to-all-start.3) | async-done | bytes 655392 | tf_op jit(solution)/shard_map/all_to_all | solution.py:122
  66.9 0.0 copy-start
  66.9 3.4 %all-to-all-start.2 = ((bf16[32,8,1280]{2,1,0:T(8,128)(2,1)}), bf16[32,8,1280]{2,1,0:T(8,128)(2,1)S(1)}, u32[]{:S(2)}, u32[]{:S(2)}) async-start(bf16[32,8,1280]{2,1,0:T(8,128)(2,1)} %bitcast.14), calls=%async_computation.2 | async-start | bytes 1310720 | tf_op jit(solution)/shard_map/all_to_all | solution.py:122
  70.4 0.0 copy-done
  70.4 7.9 %expert.3 = bf16[256,1280]{1,0:T(8,128)(2,1)} custom-call(bf16[256,1280]{1,0:T(8,128)(2,1)} %bitcast.12, bf16[1,1280,1280]{2,1,0:T(8,128)(2,1)} %first.3, bf16[1,1280]{1,0:T(2,128)(2,1)} %first_bias.3, bf16[1,1280,1280]{2,1,0:T(8,128)(2,1)} %second.3, f32[1,1280]{1,0:T(1,128)} %broadcast_select_fusion.last_bias), custom_call_target="tpu_custom_call" | custom-call | flops 1677721600 | bytes 7864320 | tf_op jit(solution)/shard_map/expert/pallas_call | solution.py:146
  78.3 10.0 %all-to-all-done.2 = bf16[32,8,1280]{2,1,0:T(8,128)(2,1)S(1)} async-done(((bf16[32,8,1280]{2,1,0:T(8,128)(2,1)}), bf16[32,8,1280]{2,1,0:T(8,128)(2,1)S(1)}, u32[]{:S(2)}, u32[]{:S(2)}) %all-to-all-start.2) | async-done | bytes 655392 | tf_op jit(solution)/shard_map/all_to_all | solution.py:122
  88.3 0.0 copy-start.1
  88.3 21.5 %all_to_all.27 = bf16[32,8,1280]{2,1,0:T(8,128)(2,1)} all-to-all(bf16[32,8,1280]{2,1,0:T(8,128)(2,1)} %bitcast.15), channel_id=1, replica_groups=mesh['dp'=4,'expert'=8] {'dp','expert'}, dimensions={0} | all-to-all | bytes 1310720 | tf_op jit(solution)/shard_map/all_to_all | solution.py:122
  109.9 0.0 copy-done.1
  109.9 2.8 %combine.1 = (bf16[256,1280]{1,0:T(8,128)(2,1)}, f32[2,2]{1,0:T(2,128)}) custom-call(s32[1,256]{1,0:T(1,128)} %bitcast.22, f32[8,256]{1,0:T(8,128)} %get-tuple-element.8.gate, f32[32,8,128]{2,1,0:T(8,128)} %all_to_all.25.stats, bf16[256,1280]{1,0:T(8,128)(2,1)} %bitcast.16, bf16[256,1280]{1,0:T(8,128)(2,1)} %bitcast.17), custom_call_target="tpu_custom_call" | custom-call | tf_op jit(solution)/shard_map/combine/pallas_call | solution.py:167
Async XLA Ops:
  0.6 48.3 %copy-start.2 = (bf16[1,1280]{1,0:T(2,128)(2,1)S(1)}, bf16[1,1280]{1,0:T(2,128)(2,1)}, u32[]{:S(2)}) copy-start(bf16[1,1280]{1,0:T(2,128)(2,1)} %param.16) | copy-start | bytes 7684
  45.6 21.3 %all-to-all-start.3 = ((bf16[32,8,1280]{2,1,0:T(8,128)(2,1)}), bf16[32,8,1280]{2,1,0:T(8,128)(2,1)S(1)}, u32[]{:S(2)}, u32[]{:S(2)}) async-start(bf16[32,8,1280]{2,1,0:T(8,128)(2,1)} %bitcast.18), calls=%async_computation.3 | async-start | bytes 1310720 | tf_op jit(solution)/shard_map/all_to_all | solution.py:122
  66.9 3.4 %copy-start = (bf16[32,8,1280]{2,1,0:T(8,128)(2,1)}, bf16[32,8,1280]{2,1,0:T(8,128)(2,1)S(1)}, u32[]{:S(2)}) copy-start(bf16[32,8,1280]{2,1,0:T(8,128)(2,1)S(1)} %all-to-all-done.3) | copy-start | bytes 1966084
  66.9 21.4 %all-to-all-start.2 = ((bf16[32,8,1280]{2,1,0:T(8,128)(2,1)}), bf16[32,8,1280]{2,1,0:T(8,128)(2,1)S(1)}, u32[]{:S(2)}, u32[]{:S(2)}) async-start(bf16[32,8,1280]{2,1,0:T(8,128)(2,1)} %bitcast.14), calls=%async_computation.2 | async-start | bytes 1310720 | tf_op jit(solution)/shard_map/all_to_all | solution.py:122
  88.3 21.5 %copy-start.1 = (bf16[32,8,1280]{2,1,0:T(8,128)(2,1)}, bf16[32,8,1280]{2,1,0:T(8,128)(2,1)S(1)}, u32[]{:S(2)}) copy-start(bf16[32,8,1280]{2,1,0:T(8,128)(2,1)S(1)} %all-to-all-done.2) | copy-start | bytes 1966084

commit v2 on v1

v2 whole, which is shorter than its diff:
```python
import functools

import jax
import jax.numpy as jnp
from jax import lax
from jax.experimental import pallas as pl
from jax.experimental.pallas import tpu as pltpu
from jax.sharding import PartitionSpec as P

CAP = 16
CHUNKS = 2
LANES = 128
AXES = ("dp", "expert")
VMEM = pl.BlockSpec(memory_space=pltpu.VMEM)


def role(layer):
    return (layer ^ (layer >> 1)) & 1


def one_hot(chunk, index, experts, rows, target):
    row = lax.broadcasted_iota(jnp.int32, (rows, target.shape[1]), 0)
    row = row % (experts * chunk)
    key = (row // chunk) * CAP + index * chunk + row % chunk
    return (key == target).astype(jnp.float32).astype(jnp.bfloat16)


def dispatch_kernel(copies, chunk, experts, tokens, gain, choice, slot, normed_out, target_out, *buffers):
    values = tokens[...].astype(jnp.float32)
    center = values - jnp.mean(values, axis=-1, keepdims=True)
    spread = jnp.mean(center * center, axis=-1, keepdims=True)
    normed = (center * lax.rsqrt(spread + 1e-06) * gain[...]).astype(jnp.bfloat16)
    normed_out[...] = normed
    target = jnp.where(slot[...] >= 0, choice[...] * CAP + slot[...], -1)
    target_out[...] = target
    for index, buffer in enumerate(buffers):
        table = one_hot(chunk, index, experts, experts * chunk, target)
        packed = jnp.dot(table, normed, preferred_element_type=jnp.float32).astype(jnp.bfloat16)
        for copy in range(copies):
            buffer[copy] = packed


def router_kernel(normed, router, choice, modality, gate_out, stats_out):
    logits = lax.dot_general(
        router[...], normed[...], (((1,), (1,)), ((), ())), preferred_element_type=jnp.float32
    )
    shifted = logits - jnp.max(logits, axis=0, keepdims=True)
    logp = shifted - jnp.log(jnp.sum(jnp.exp(shifted), axis=0, keepdims=True))
    probs = jnp.exp(logp)
    experts = probs.shape[0]
    expert = lax.broadcasted_iota(jnp.int32, probs.shape, 0)
    gate = jnp.sum(jnp.where(expert == choice[...], probs, 0.0), axis=0, keepdims=True)
    gate_out[...] = jnp.broadcast_to(gate, gate_out.shape)
    textual = (modality[...] == 1).astype(jnp.float32)
    entropy = -jnp.sum(probs * logp, axis=0, keepdims=True)
    lane = lax.broadcasted_iota(jnp.int32, (experts, LANES), 1)
    row = lax.broadcasted_iota(jnp.int32, (experts, LANES), 0)
    line = lane[0:1]
    stats = jnp.zeros((1, LANES), jnp.float32)
    for kind, select in enumerate((1.0 - textual, textual)):
        prob_sum = jnp.sum(probs * select, axis=1, keepdims=True)
        spread = jnp.where(lane == row + kind * experts, prob_sum, 0.0)
        stats = stats + jnp.sum(spread, axis=0, keepdims=True)
        ent_sum = jnp.sum(entropy * select, axis=1, keepdims=True)
        count = jnp.sum(select, axis=1, keepdims=True)
        stats = jnp.where(line == 2 * experts + kind, ent_sum, stats)
        stats = jnp.where(line == 2 * experts + 2 + kind, count, stats)
    stats_out[...] = jnp.broadcast_to(stats, stats_out.shape)


def expert_kernel(rows, first, first_bias, second, last_bias, out):
    pre = lax.dot_general(
        rows[...], first[...], (((1,), (1,)), ((), ())), preferred_element_type=jnp.float32
    )
    pre = pre + first_bias[...].astype(jnp.float32)
    hidden = (0.5 * pre * (1.0 + lax.erf(pre * (0.5**0.5)))).astype(jnp.bfloat16)
    result = jnp.dot(hidden, second[...], preferred_element_type=jnp.float32)
    out[...] = (result + last_bias[...]).astype(out.dtype)


def sum_kernel(chunk, carry, own, other, stats, other_stats, out):
    width = own.shape[1]
    out[:, :width] = (own[...] + other[...].astype(jnp.float32)).astype(jnp.bfloat16)
    if carry:
        total = stats[0:1] + other_stats[0:1]
        row = lax.broadcasted_iota(jnp.int32, (own.shape[0], LANES), 0) % chunk
        extra = jnp.zeros(row.shape, jnp.float32)
        for piece in range(3):
            part = total.astype(jnp.bfloat16).astype(jnp.float32)
            extra = jnp.where(row == piece, part, extra)
            total = total - part
        out[:, width:] = extra.astype(jnp.bfloat16)


def combine_kernel(chunk, experts, target, gate, *refs):
    returned, (out, aux) = refs[:-2], refs[-2:]
    width = out.shape[1]
    fetched = None
    for index, part in enumerate(returned):
        table = one_hot(chunk, index, experts, part.shape[0], target[...])
        term = lax.dot_general(
            table, part[:, :width], (((0,), (0,)), ((), ())), preferred_element_type=jnp.float32
        )
        fetched = term if fetched is None else fetched + term
    scale = jnp.transpose(gate[...])[:, 0:1]
    out[...] = (scale * fetched).astype(jnp.bfloat16)
    sums = jnp.sum(returned[-1][:, width:].astype(jnp.float32), axis=0, keepdims=True)
    lane = lax.broadcasted_iota(jnp.int32, sums.shape, 1)

    def pick(at):
        return jnp.sum(jnp.where(lane == at, sums, 0.0), axis=1, keepdims=True)

    row = lax.broadcasted_iota(jnp.int32, aux.shape, 0)
    column = lax.broadcasted_iota(jnp.int32, aux.shape, 1)
    result = jnp.zeros(aux.shape, jnp.float32)
    for kind in range(2):
        count = pick(2 * experts + 2 + kind)
        local = pick(2 * experts + kind) / count
        pbar = sums / count
        inside = (lane >= kind * experts) & (lane < (kind + 1) * experts)
        terms = jnp.where(inside, pbar * jnp.log(pbar), 0.0)
        spread = jnp.sum(terms, axis=1, keepdims=True)
        result = jnp.where((row == kind) & (column == 0), local, result)
        result = jnp.where((row == kind) & (column == 1), spread, result)
    aux[...] = result


def on_device(tokens, ln_gain, router, w_in, b_in, w_out, b_out, expert_choice, modality, slot):
    count, width = tokens.shape
    experts = router.shape[1]
    layers, senders = lax.axis_size("dp"), lax.axis_size("expert")
    assert w_in.shape[0] == 1 and experts == senders and layers % 4 == 0
    assert 2 * experts + 4 <= LANES
    hidden = w_in.shape[1]
    chunk = CAP // CHUNKS
    half = layers // 2
    peers = half * experts
    rows = peers * chunk
    groups = [
        [z * experts + e for z in range(layers) if role(z) == r for e in range(experts)] for r in range(2)
    ]
    pairs = [(z, z ^ 1) for z in range(layers)]
    choice = expert_choice.reshape(1, count)
    normed, target, *buffers = pl.pallas_call(
        functools.partial(dispatch_kernel, half, chunk, experts),
        out_shape=[
            jax.ShapeDtypeStruct((count, width), jnp.bfloat16),
            jax.ShapeDtypeStruct((1, count), jnp.int32),
        ]
        + [jax.ShapeDtypeStruct((half, experts * chunk, width), jnp.bfloat16)] * CHUNKS,
        in_specs=[VMEM] * 4,
        out_specs=[VMEM] * (2 + CHUNKS),
        name="dispatch",
    )(tokens, ln_gain.reshape(1, width), choice, slot.reshape(1, count))

    def exchange(block):
        return lax.all_to_all(
            block.reshape(peers, chunk, block.shape[-1]),
            AXES,
            split_axis=0,
            concat_axis=0,
            axis_index_groups=groups,
            tiled=True,
        ).reshape(rows, block.shape[-1])

    def swap(block):
        return lax.ppermute(block, "dp", pairs)

    gate, stats = pl.pallas_call(
        router_kernel,
        out_shape=[
            jax.ShapeDtypeStruct((8, count), jnp.float32),
            jax.ShapeDtypeStruct((8, LANES), jnp.float32),
        ],
        in_specs=[VMEM] * 4,
        out_specs=[VMEM] * 2,
        name="router",
    )(normed, router.T, choice, modality.reshape(1, count))
    other_stats = swap(stats)

    height = rows if rows <= 512 else 256

    def run_expert(part, bias, dtype, name):
        return pl.pallas_call(
            expert_kernel,
            grid=(rows // height,),
            out_shape=jax.ShapeDtypeStruct((rows, width), dtype),
            in_specs=[
                pl.BlockSpec((height, width), lambda i: (i, 0)),
                pl.BlockSpec((None, hidden, width), lambda i: (0, 0, 0)),
                pl.BlockSpec((1, hidden), lambda i: (0, 0)),
                pl.BlockSpec((None, hidden, width), lambda i: (0, 0, 0)),
                pl.BlockSpec((1, width), lambda i: (0, 0)),
            ],
            out_specs=pl.BlockSpec((height, width), lambda i: (i, 0)),
            cost_estimate=pl.CostEstimate(
                flops=4 * rows * width * hidden,
                bytes_accessed=4 * width * (hidden + rows),
                transcendentals=rows * hidden,
            ),
            name=name,
        )(part, w_in, b_in, w_out, bias)

    last_bias = jnp.where(lax.axis_index("dp") < 2, b_out.astype(jnp.float32), 0.0)
    no_bias = jnp.zeros((1, width), jnp.float32)
    returned = []
    for index, buffer in enumerate(buffers):
        carry = index == CHUNKS - 1
        mine = exchange(buffer)
        theirs = swap(mine)
        own = run_expert(mine, last_bias, jnp.float32, "own")
        back = swap(run_expert(theirs, no_bias, jnp.bfloat16, "theirs"))
        full = width + LANES if carry else width
        summed = pl.pallas_call(
            functools.partial(sum_kernel, chunk, carry),
            grid=(rows // height,),
            out_shape=jax.ShapeDtypeStruct((rows, full), jnp.bfloat16),
            in_specs=[pl.BlockSpec((height, width), lambda i: (i, 0))] * 2
            + [pl.BlockSpec((8, LANES), lambda i: (0, 0))] * 2,
            out_specs=pl.BlockSpec((height, full), lambda i: (i, 0)),
            name="sum",
        )(own, back, stats, other_stats)
        returned.append(exchange(summed))
    return pl.pallas_call(
        functools.partial(combine_kernel, chunk, experts),
        out_shape=[
            jax.ShapeDtypeStruct((count, width), jnp.bfloat16),
            jax.ShapeDtypeStruct((2, 2), jnp.float32),
        ],
        in_specs=[VMEM] * (2 + CHUNKS),
        out_specs=[VMEM] * 2,
        name="combine",
    )(target, gate, *returned)


def solution(mesh):
    return jax.shard_map(
        on_device,
        mesh=mesh,
        in_specs=(
            P(AXES, None),
            P(),
            P(),
            P("expert", "dp", None),
            P("expert", "dp"),
            P("expert", "dp", None),
            P("expert", None),
            P(AXES),
            P(AXES),
            P(AXES),
        ),
        out_specs=(P(AXES, None), P()),
        check_vma=False,
    )
```

time: 113 us -> 104 us (0.920)
  blocking collectives: 58.3 us -> 36 us
  Pallas kernels: 23.6 us -> 33.2 us
  starting transfers between devices: 6.73 us -> 14.6 us
  waiting for transfers between devices: 19.5 us -> 14.4 us
  local copies, waits for them, and re-layouts: 2 us -> 4.2 us
  other arithmetic: 1.87 us -> 0.6 us
    all_to_all x3 -> x2, blocking collectives: 58.3 us -> 36 us  [exchange(): lax.all_to_all(block.reshape(peers, chunk, block.shape[-1]), AXES, split_...]
    all_to_all x2, waiting for transfers between devices: 19.5 us -> 6.56 us  [exchange(): lax.all_to_all(block.reshape(peers, chunk, block.shape[-1]), AXES, split_...]
    pallas_call x4 -> x8, Pallas kernels: 21.5 us -> 31 us  [the longest x4 21.9 us: run_expert(): pl.pallas_call(expert_kernel, grid=(rows // height,), out_shape=jax.Shape...]
    ppermute x0 -> x5, waiting for transfers between devices: none -> 7.85 us  [swap(): return lax.ppermute(block, 'dp', pairs)]
    ppermute x0 -> x5, starting transfers between devices: none -> 4.64 us  [swap(): return lax.ppermute(block, 'dp', pairs)]
    all_to_all x2, starting transfers between devices: 6.73 us -> 9.98 us  [exchange(): lax.all_to_all(block.reshape(peers, chunk, block.shape[-1]), AXES, split_...]
    unnamed x6 -> x18, local copies, waits for them, and re-layouts: 0.01 us -> 2.27 us
    select_n x2 -> x1, other arithmetic: 1.87 us -> 0.6 us  [on_device(): jnp.where(lax.axis_index('dp') < 2, b_out.astype(jnp.float32), 0.0)]
  transfers between devices with their start and end apart: 2 -> 7, of which waited for: 2 -> 4; matrix products, arithmetic and copies ran while one was open for 1% -> 1% of each run, Pallas kernels for 14% -> 27%
where the time goes in v2:
time: 104 us
  blocking collectives  36 us (35%)
  Pallas kernels  33.2 us (32%)
  starting transfers between devices  14.6 us (14%)
  waiting for transfers between devices  14.4 us (14%)
  local copies, waits for them, and re-layouts  4.2 us (4%)
    all_to_all x2, blocking collectives, exchange(): lax.all_to_all(block.reshape(peers, chunk, block.shape[-1]), AXES, split_...  36 us
    pallas_call x4, Pallas kernels, run_expert(): pl.pallas_call(expert_kernel, grid=(rows // height,), out_shape=jax.Shape...  21.9 us
    all_to_all x2, starting transfers between devices, exchange(): lax.all_to_all(block.reshape(peers, chunk, block.shape[-1]), AXES, split_...  9.98 us
    ppermute x5, waiting for transfers between devices, swap(): return lax.ppermute(block, 'dp', pairs)  7.85 us
    all_to_all x2, waiting for transfers between devices, exchange(): lax.all_to_all(block.reshape(peers, chunk, block.shape[-1]), AXES, split_...  6.56 us
    ppermute x5, starting transfers between devices, swap(): return lax.ppermute(block, 'dp', pairs)  4.64 us
    pallas_call x2, Pallas kernels, on_device(): pl.pallas_call(functools.partial(sum_kernel, chunk, carry), grid=(rows //...  3.98 us
    pallas_call x1, Pallas kernels, on_device(): pl.pallas_call(functools.partial(dispatch_kernel, half, chunk, experts),...  2.65 us
  transfers between devices with their start and end apart: 7, of which 4 were waited for; matrix products, arithmetic and copies ran while one was open for 1% of the time, Pallas kernels for 27%

profile of v2, /device:TPU:0, one launch (start us, length us, event | category | flops | bytes accessed | tf_op | source)
XLA Modules:
  0.0 103.7 jit_solution(14974678339760852114)
XLA Ops:
  0.6 1.3 %reshape.40.gain = f32[1,1280]{1,0:T(1,128)} reshape(f32[1280]{0:T(1024)} %param.11) | data formatting | bytes 10240 | tf_op jit(solution)/shard_map/reshape | solution.py:154
  1.9 2.6 %dispatch.1 = (bf16[256,1280]{1,0:T(8,128)(2,1)}, s32[1,256]{1,0:T(1,128)}, bf16[2,64,1280]{2,1,0:T(8,128)(2,1)}, bf16[2,64,1280]{2,1,0:T(8,128)(2,1)}) custom-call(bf16[256,1280]{1,0:T(8,128)(2,1)} %tokens.1, f32[1,1280]{1,0:T(1,128)} %reshape.40.gain, s32[1,256]{1,0:T(1,128)} %bitcast.23, s32[1,256]{1,0:T(1,128)} %bitcast.26), custom_call_target="tpu_custom_call" | custom-call | tf_op jit(solution)/shard_map/dispatch/pallas_call | solution.py:144
  4.6 18.6 %all_to_all.20 = bf16[16,8,1280]{2,1,0:T(8,128)(2,1)S(1)} all-to-all(bf16[16,8,1280]{2,1,0:T(8,128)(2,1)} %bitcast.21), channel_id=1, replica_groups={{0,1,2,3,4,5,6,7,24,25,26,27,28,29,30,31},{8,9,10,11,12,13,14,15,16,17,..., dimensions={0} | all-to-all | bytes 655360 | tf_op jit(solution)/shard_map/all_to_all | solution.py:157
  23.2 3.5 %all-to-all-start.2 = ((bf16[16,8,1280]{2,1,0:T(8,128)(2,1)}), bf16[16,8,1280]{2,1,0:T(8,128)(2,1)S(1)}, u32[]{:S(2)}, u32[]{:S(2)}) async-start(bf16[16,8,1280]{2,1,0:T(8,128)(2,1)} %bitcast.20), calls=%async_computation.2 | async-start | bytes 655360 | tf_op jit(solution)/shard_map/all_to_all | solution.py:157
  26.8 1.2 %collective-permute-start = (bf16[128,1280]{1,0:T(8,128)(2,1)S(1)}, bf16[128,1280]{1,0:T(8,128)(2,1)S(1)}, u32[]{:S(2)}, u32[]{:S(2)}) collective-permute-start(bf16[128,1280]{1,0:T(8,128)(2,1)S(1)} %bitcast.16), channel_id=1, source_target_pairs={{0,8},{8,0},{16,24},{24,16},{1,9},{9,1},{17,25},{25,17},{2,10},{10... | collective-permute-start | bytes 983048 | tf_op jit(solution)/shard_map/ppermute | solution.py:167
  28.0 2.1 %router.1 = (f32[8,256]{1,0:T(8,128)}, f32[8,128]{1,0:T(8,128)}) custom-call(bf16[256,1280]{1,0:T(8,128)(2,1)} %get-tuple-element.9.normed, bf16[8,1280]{1,0:T(8,128)(2,1)} %bitcast.22, s32[1,256]{1,0:T(1,128)} %bitcast.24, s32[1,256]{1,0:T(1,128)} %bitcast.25), custom_call_target="tpu_custom_call" | custom-call | tf_op jit(solution)/shard_map/router/pallas_call | solution.py:169
  30.1 0.9 collective-permute-start.2
  31.0 6.6 %all-to-all-done.2 = bf16[16,8,1280]{2,1,0:T(8,128)(2,1)S(1)} async-done(((bf16[16,8,1280]{2,1,0:T(8,128)(2,1)}), bf16[16,8,1280]{2,1,0:T(8,128)(2,1)S(1)}, u32[]{:S(2)}, u32[]{:S(2)}) %all-to-all-start.2) | async-done | bytes 327712 | tf_op jit(solution)/shard_map/all_to_all | solution.py:157
  37.6 2.3 %collective-permute-start.3 = (bf16[128,1280]{1,0:T(8,128)(2,1)S(1)}, bf16[128,1280]{1,0:T(8,128)(2,1)S(1)}, u32[]{:S(2)}, u32[]{:S(2)}) collective-permute-start(bf16[128,1280]{1,0:T(8,128)(2,1)S(1)} %bitcast.14), channel_id=1, source_target_pairs={{0,8},{8,0},{16,24},{24,16},{1,9},{9,1},{17,25},{25,17},{2,10},{10... | collective-permute-start | bytes 983048 | tf_op jit(solution)/shard_map/ppermute | solution.py:167
  39.8 0.7 collective-permute-done.rows
  41.3 5.4 %theirs.2 = bf16[128,1280]{1,0:T(8,128)(2,1)} custom-call(bf16[128,1280]{1,0:T(8,128)(2,1)} %copy-done.3, bf16[1,1280,1280]{2,1,0:T(8,128)(2,1)} %first.7, bf16[1,1280]{1,0:T(2,128)(2,1)} %first_bias.7, bf16[1,1280,1280]{2,1,0:T(8,128)(2,1)} %second.7, f32[1,1280]{1,0:T(1,128)} %broadcast_in_dim.5.last_bias), custom_call_target="tpu_custom_call" | custom-call | flops 838860800 | bytes 7208960 | tf_op jit(solution)/shard_map/theirs/pallas_call | solution.py:184
  47.5 5.5 %own.2 = f32[128,1280]{1,0:T(8,128)} custom-call(bf16[128,1280]{1,0:T(8,128)(2,1)} %bitcast.17, bf16[1,1280,1280]{2,1,0:T(8,128)(2,1)} %first.7, bf16[1,1280]{1,0:T(2,128)(2,1)} %first_bias.7, bf16[1,1280,1280]{2,1,0:T(8,128)(2,1)} %second.7, f32[1,1280]{1,0:T(1,128)} %broadcast_select_fusion.last_bias), custom_call_target="tpu_custom_call" | custom-call | flops 838860800 | bytes 7208960 | tf_op jit(solution)/shard_map/own/pallas_call | solution.py:184
  53.0 2.5 %collective-permute-done.1.other = bf16[128,1280]{1,0:T(8,128)(2,1)S(1)} collective-permute-done((bf16[128,1280]{1,0:T(8,128)(2,1)}, bf16[128,1280]{1,0:T(8,128)(2,1)S(1)}, u32[]{:S(2)}, u32[]{:S(2)}) %collective-permute-start.1) | collective-permute-done | bytes 327712 | tf_op jit(solution)/shard_map/ppermute | solution.py:167
  55.5 0.7 copy-done.5
  56.3 2.0 %sum.2 = bf16[128,1280]{1,0:T(8,128)(2,1)} custom-call(f32[128,1280]{1,0:T(8,128)} %own.2, bf16[128,1280]{1,0:T(8,128)(2,1)} %copy-done.5, f32[8,128]{1,0:T(8,128)} %get-tuple-element.12.stats, f32[8,128]{1,0:T(8,128)} %copy-done.7), custom_call_target="tpu_custom_call" | custom-call | tf_op jit(solution)/shard_map/sum/pallas_call | solution.py:214
  58.2 6.4 %all-to-all-start.1 = ((bf16[16,8,1280]{2,1,0:T(8,128)(2,1)}), bf16[16,8,1280]{2,1,0:T(8,128)(2,1)S(1)}, u32[]{:S(2)}, u32[]{:S(2)}) async-start(bf16[16,8,1280]{2,1,0:T(8,128)(2,1)} %bitcast.18), calls=%async_computation.1 | async-start | bytes 655360 | tf_op jit(solution)/shard_map/all_to_all | solution.py:157
  64.7 0.7 copy-done.4
  65.4 5.4 %theirs.3 = bf16[128,1280]{1,0:T(8,128)(2,1)} custom-call(bf16[128,1280]{1,0:T(8,128)(2,1)} %copy-done.4, bf16[1,1280,1280]{2,1,0:T(8,128)(2,1)} %first.7, bf16[1,1280]{1,0:T(2,128)(2,1)} %first_bias.7, bf16[1,1280,1280]{2,1,0:T(8,128)(2,1)} %second.7, f32[1,1280]{1,0:T(1,128)} %broadcast_in_dim.5.last_bias), custom_call_target="tpu_custom_call" | custom-call | flops 838860800 | bytes 7208960 | tf_op jit(solution)/shard_map/theirs/pallas_call | solution.py:184
  70.9 5.5 %own.3 = f32[128,1280]{1,0:T(8,128)} custom-call(bf16[128,1280]{1,0:T(8,128)(2,1)} %bitcast.15, bf16[1,1280,1280]{2,1,0:T(8,128)(2,1)} %first.7, bf16[1,1280]{1,0:T(2,128)(2,1)} %first_bias.7, bf16[1,1280,1280]{2,1,0:T(8,128)(2,1)} %second.7, f32[1,1280]{1,0:T(1,128)} %broadcast_select_fusion.last_bias), custom_call_target="tpu_custom_call" | custom-call | flops 838860800 | bytes 7208960 | tf_op jit(solution)/shard_map/own/pallas_call | solution.py:184
  76.4 4.6 %collective-permute-done.4.other = bf16[128,1280]{1,0:T(8,128)(2,1)S(1)} collective-permute-done((bf16[128,1280]{1,0:T(8,128)(2,1)}, bf16[128,1280]{1,0:T(8,128)(2,1)S(1)}, u32[]{:S(2)}, u32[]{:S(2)}) %collective-permute-start.4) | collective-permute-done | bytes 327712 | tf_op jit(solution)/shard_map/ppermute | solution.py:167
  81.1 0.7 copy-done.6
  81.8 2.0 %sum.3 = bf16[128,1408]{1,0:T(8,128)(2,1)} custom-call(f32[128,1280]{1,0:T(8,128)} %own.3, bf16[128,1280]{1,0:T(8,128)(2,1)} %copy-done.6, f32[8,128]{1,0:T(8,128)} %get-tuple-element.12.stats, f32[8,128]{1,0:T(8,128)} %copy-done.7), custom_call_target="tpu_custom_call" | custom-call | tf_op jit(solution)/shard_map/sum/pallas_call | solution.py:214
  83.8 17.4 %all_to_all.21 = bf16[16,8,1408]{2,1,0:T(8,128)(2,1)} all-to-all(bf16[16,8,1408]{2,1,0:T(8,128)(2,1)} %bitcast.13), channel_id=1, replica_groups={{0,1,2,3,4,5,6,7,24,25,26,27,28,29,30,31},{8,9,10,11,12,13,14,15,16,17,..., dimensions={0} | all-to-all | bytes 720896 | tf_op jit(solution)/shard_map/all_to_all | solution.py:157
  101.2 2.5 %combine.1 = (bf16[256,1280]{1,0:T(8,128)(2,1)}, f32[2,2]{1,0:T(2,128)}) custom-call(s32[1,256]{1,0:T(1,128)} %get-tuple-element.8.target, f32[8,256]{1,0:T(8,128)} %get-tuple-element.10.gate, bf16[128,1280]{1,0:T(8,128)(2,1)} %bitcast.19, bf16[128,1408]{1,0:T(8,128)(2,1)} %bitcast.12), custom_call_target="tpu_custom_call" | custom-call | tf_op jit(solution)/shard_map/combine/pallas_call | solution.py:224
  (22 shorter events, 1.6 us)
Async XLA Ops:
  23.2 23.5 %copy-start.1 = (bf16[16,8,1280]{2,1,0:T(8,128)(2,1)}, bf16[16,8,1280]{2,1,0:T(8,128)(2,1)S(1)}, u32[]{:S(2)}) copy-start(bf16[16,8,1280]{2,1,0:T(8,128)(2,1)S(1)} %all_to_all.20) | copy-start | bytes 983044
  23.2 14.3 %all-to-all-start.2 = ((bf16[16,8,1280]{2,1,0:T(8,128)(2,1)}), bf16[16,8,1280]{2,1,0:T(8,128)(2,1)S(1)}, u32[]{:S(2)}, u32[]{:S(2)}) async-start(bf16[16,8,1280]{2,1,0:T(8,128)(2,1)} %bitcast.20), calls=%async_computation.2 | async-start | bytes 655360 | tf_op jit(solution)/shard_map/all_to_all | solution.py:157
  26.8 13.8 %collective-permute-start = (bf16[128,1280]{1,0:T(8,128)(2,1)S(1)}, bf16[128,1280]{1,0:T(8,128)(2,1)S(1)}, u32[]{:S(2)}, u32[]{:S(2)}) collective-permute-start(bf16[128,1280]{1,0:T(8,128)(2,1)S(1)} %bitcast.16), channel_id=1, source_target_pairs={{0,8},{8,0},{16,24},{24,16},{1,9},{9,1},{17,25},{25,17},{2,10},{10... | collective-permute-start | bytes 983048 | tf_op jit(solution)/shard_map/ppermute | solution.py:167
  30.1 22.9 %collective-permute-start.2 = (f32[8,128]{1,0:T(8,128)}, f32[8,128]{1,0:T(8,128)S(1)}, u32[]{:S(2)}, u32[]{:S(2)}) collective-permute-start(f32[8,128]{1,0:T(8,128)} %get-tuple-element.12.stats), channel_id=1, source_target_pairs={{0,8},{8,0},{16,24},{24,16},{1,9},{9,1},{17,25},{25,17},{2,10},{10... | collective-permute-start | bytes 12296 | tf_op jit(solution)/shard_map/ppermute | solution.py:167
  37.6 9.1 %copy-start = (bf16[16,8,1280]{2,1,0:T(8,128)(2,1)}, bf16[16,8,1280]{2,1,0:T(8,128)(2,1)S(1)}, u32[]{:S(2)}) copy-start(bf16[16,8,1280]{2,1,0:T(8,128)(2,1)S(1)} %all-to-all-done.2) | copy-start | bytes 983044
  37.6 27.1 %collective-permute-start.3 = (bf16[128,1280]{1,0:T(8,128)(2,1)S(1)}, bf16[128,1280]{1,0:T(8,128)(2,1)S(1)}, u32[]{:S(2)}, u32[]{:S(2)}) collective-permute-start(bf16[128,1280]{1,0:T(8,128)(2,1)S(1)} %bitcast.14), channel_id=1, source_target_pairs={{0,8},{8,0},{16,24},{24,16},{1,9},{9,1},{17,25},{25,17},{2,10},{10... | collective-permute-start | bytes 983048 | tf_op jit(solution)/shard_map/ppermute | solution.py:167
  40.5 0.7 copy-start.3
  41.3 5.7 %copy-start.8 = (bf16[1,1280]{1,0:T(2,128)(2,1)S(1)}, bf16[1,1280]{1,0:T(2,128)(2,1)}, u32[]{:S(2)}) copy-start(bf16[1,1280]{1,0:T(2,128)(2,1)} %param.16) | copy-start | bytes 7684
  46.7 8.8 %collective-permute-start.1 = (bf16[128,1280]{1,0:T(8,128)(2,1)}, bf16[128,1280]{1,0:T(8,128)(2,1)S(1)}, u32[]{:S(2)}, u32[]{:S(2)}) collective-permute-start(bf16[128,1280]{1,0:T(8,128)(2,1)} %theirs.2), channel_id=1, source_target_pairs={{0,8},{8,0},{16,24},{24,16},{1,9},{9,1},{17,25},{25,17},{2,10},{10... | collective-permute-start | bytes 983048 | tf_op jit(solution)/shard_map/ppermute | solution.py:167
  53.0 2.5 %copy-start.7 = (f32[8,128]{1,0:T(8,128)}, f32[8,128]{1,0:T(8,128)S(1)}, u32[]{:S(2)}) copy-start(f32[8,128]{1,0:T(8,128)S(1)} %collective-permute-done.2.other_stats) | copy-start | bytes 12292
  55.5 0.7 copy-start.5
  58.2 25.6 %all-to-all-start.1 = ((bf16[16,8,1280]{2,1,0:T(8,128)(2,1)}), bf16[16,8,1280]{2,1,0:T(8,128)(2,1)S(1)}, u32[]{:S(2)}, u32[]{:S(2)}) async-start(bf16[16,8,1280]{2,1,0:T(8,128)(2,1)} %bitcast.18), calls=%async_computation.1 | async-start | bytes 655360 | tf_op jit(solution)/shard_map/all_to_all | solution.py:157
  64.7 0.7 copy-start.4
  70.8 10.2 %collective-permute-start.4 = (bf16[128,1280]{1,0:T(8,128)(2,1)}, bf16[128,1280]{1,0:T(8,128)(2,1)S(1)}, u32[]{:S(2)}, u32[]{:S(2)}) collective-permute-start(bf16[128,1280]{1,0:T(8,128)(2,1)} %theirs.3), channel_id=1, source_target_pairs={{0,8},{8,0},{16,24},{24,16},{1,9},{9,1},{17,25},{25,17},{2,10},{10... | collective-permute-start | bytes 983048 | tf_op jit(solution)/shard_map/ppermute | solution.py:167
  81.1 0.7 copy-start.6
  83.8 17.4 %copy-start.2 = (bf16[16,8,1280]{2,1,0:T(8,128)(2,1)}, bf16[16,8,1280]{2,1,0:T(8,128)(2,1)S(1)}, u32[]{:S(2)}) copy-start(bf16[16,8,1280]{2,1,0:T(8,128)(2,1)S(1)} %all-to-all-done.1) | copy-start | bytes 983044

commit v3 on v2

--- a/solution.py
+++ b/solution.py
@@ -8,10 +8,12 @@
 from jax.sharding import PartitionSpec as P
 
 CAP = 16
-CHUNKS = 2
+CHUNKS = 1
+SPLIT = 2
 LANES = 128
 AXES = ("dp", "expert")
 VMEM = pl.BlockSpec(memory_space=pltpu.VMEM)
+PARAMS = pltpu.CompilerParams(vmem_limit_bytes=24 << 20)
 
 
 def role(layer):
@@ -29,7 +31,7 @@
     values = tokens[...].astype(jnp.float32)
     center = values - jnp.mean(values, axis=-1, keepdims=True)
     spread = jnp.mean(center * center, axis=-1, keepdims=True)
-    normed = (center * lax.rsqrt(spread + 1e-06) * gain[...]).astype(jnp.bfloat16)
+    normed = (center * lax.rsqrt(spread + 1e-06) * gain[...].reshape(1, values.shape[1])).astype(jnp.bfloat16)
     normed_out[...] = normed
     target = jnp.where(slot[...] >= 0, choice[...] * CAP + slot[...], -1)
     target_out[...] = target
@@ -68,27 +70,35 @@
     stats_out[...] = jnp.broadcast_to(stats, stats_out.shape)
 
 
-def expert_kernel(rows, first, first_bias, second, last_bias, out):
+def expert_kernel(biased, rows, first, first_bias, second, last_bias, out):
     pre = lax.dot_general(
         rows[...], first[...], (((1,), (1,)), ((), ())), preferred_element_type=jnp.float32
     )
     pre = pre + first_bias[...].astype(jnp.float32)
     hidden = (0.5 * pre * (1.0 + lax.erf(pre * (0.5**0.5)))).astype(jnp.bfloat16)
     result = jnp.dot(hidden, second[...], preferred_element_type=jnp.float32)
-    out[...] = (result + last_bias[...]).astype(out.dtype)
-
-
-def sum_kernel(chunk, carry, own, other, stats, other_stats, out):
+    if biased:
+        once = (lax.axis_index("dp") < 2).astype(jnp.float32)
+        result = result + once * last_bias[...].astype(jnp.float32)
+    out[...] = result.astype(out.dtype)
+
+
+def sum_kernel(chunk, carry, steps, own, *refs):
+    others, (stats, other_stats, out) = refs[:-3], refs[-3:]
     width = own.shape[1]
-    out[:, :width] = (own[...] + other[...].astype(jnp.float32)).astype(jnp.bfloat16)
+    part = pl.program_id(0) // steps
+    other = others[0][...]
+    for index in range(1, len(others)):
+        other = jnp.where(part == index, others[index][...], other)
+    out[:, :width] = (own[...] + other.astype(jnp.float32)).astype(jnp.bfloat16)
     if carry:
         total = stats[0:1] + other_stats[0:1]
         row = lax.broadcasted_iota(jnp.int32, (own.shape[0], LANES), 0) % chunk
         extra = jnp.zeros(row.shape, jnp.float32)
         for piece in range(3):
-            part = total.astype(jnp.bfloat16).astype(jnp.float32)
-            extra = jnp.where(row == piece, part, extra)
-            total = total - part
+            rounded = total.astype(jnp.bfloat16).astype(jnp.float32)
+            extra = jnp.where(row == piece, rounded, extra)
+            total = total - rounded
         out[:, width:] = extra.astype(jnp.bfloat16)
 
 
@@ -151,7 +161,7 @@
         in_specs=[VMEM] * 4,
         out_specs=[VMEM] * (2 + CHUNKS),
         name="dispatch",
-    )(tokens, ln_gain.reshape(1, width), choice, slot.reshape(1, count))
+    )(tokens, ln_gain, choice, slot.reshape(1, count))
 
     def exchange(block):
         return lax.all_to_all(
@@ -174,52 +184,63 @@
         ],
         in_specs=[VMEM] * 4,
         out_specs=[VMEM] * 2,
+        compiler_params=PARAMS,
         name="router",
     )(normed, router.T, choice, modality.reshape(1, count))
     other_stats = swap(stats)
 
-    height = rows if rows <= 512 else 256
-
-    def run_expert(part, bias, dtype, name):
+    first = pltpu.with_memory_space_constraint(w_in.reshape(hidden, width), pltpu.VMEM)
+    second = pltpu.with_memory_space_constraint(w_out.reshape(hidden, width), pltpu.VMEM)
+
+    def run_expert(part, biased, dtype, name):
+        tall = part.shape[0]
+        height = min(tall, 256)
         return pl.pallas_call(
-            expert_kernel,
-            grid=(rows // height,),
-            out_shape=jax.ShapeDtypeStruct((rows, width), dtype),
+            functools.partial(expert_kernel, biased),
+            grid=(tall // height,),
+            out_shape=jax.ShapeDtypeStruct((tall, width), dtype),
             in_specs=[
                 pl.BlockSpec((height, width), lambda i: (i, 0)),
-                pl.BlockSpec((None, hidden, width), lambda i: (0, 0, 0)),
+                VMEM,
                 pl.BlockSpec((1, hidden), lambda i: (0, 0)),
-                pl.BlockSpec((None, hidden, width), lambda i: (0, 0, 0)),
+                VMEM,
                 pl.BlockSpec((1, width), lambda i: (0, 0)),
             ],
             out_specs=pl.BlockSpec((height, width), lambda i: (i, 0)),
             cost_estimate=pl.CostEstimate(
-                flops=4 * rows * width * hidden,
-                bytes_accessed=4 * width * (hidden + rows),
-                transcendentals=rows * hidden,
+                flops=4 * tall * width * hidden,
+                bytes_accessed=4 * width * (hidden + tall),
+                transcendentals=tall * hidden,
             ),
+            compiler_params=PARAMS,
             name=name,
-        )(part, w_in, b_in, w_out, bias)
-
-    last_bias = jnp.where(lax.axis_index("dp") < 2, b_out.astype(jnp.float32), 0.0)
-    no_bias = jnp.zeros((1, width), jnp.float32)
+        )(part, first, b_in, second, b_out)
+
     returned = []
     for index, buffer in enumerate(buffers):
         carry = index == CHUNKS - 1
         mine = exchange(buffer)
-        theirs = swap(mine)
-        own = run_expert(mine, last_bias, jnp.float32, "own")
-        back = swap(run_expert(theirs, no_bias, jnp.bfloat16, "theirs"))
+        tall = rows // SPLIT
+        theirs = [swap(mine[at : at + tall]) for at in range(0, rows, tall)]
+        own = run_expert(mine, True, jnp.float32, "own")
+        back = [swap(run_expert(part, False, jnp.bfloat16, "theirs")) for part in theirs]
         full = width + LANES if carry else width
+        height = min(tall, 256)
+        steps = tall // height
         summed = pl.pallas_call(
-            functools.partial(sum_kernel, chunk, carry),
+            functools.partial(sum_kernel, chunk, carry, steps),
             grid=(rows // height,),
             out_shape=jax.ShapeDtypeStruct((rows, full), jnp.bfloat16),
-            in_specs=[pl.BlockSpec((height, width), lambda i: (i, 0))] * 2
+            in_specs=[pl.BlockSpec((height, width), lambda i: (i, 0))]
+            + [
+                pl.BlockSpec((height, width), lambda i, p=p: (jnp.clip(i - p * steps, 0, steps - 1), 0))
+                for p in range(SPLIT)
+            ]
             + [pl.BlockSpec((8, LANES), lambda i: (0, 0))] * 2,
             out_specs=pl.BlockSpec((height, full), lambda i: (i, 0)),
+            compiler_params=PARAMS,
             name="sum",
-        )(own, back, stats, other_stats)
+        )(own, *back, stats, other_stats)
         returned.append(exchange(summed))
     return pl.pallas_call(
         functools.partial(combine_kernel, chunk, experts),
@@ -229,6 +250,7 @@
         ],
         in_specs=[VMEM] * (2 + CHUNKS),
         out_specs=[VMEM] * 2,
+        compiler_params=PARAMS,
         name="combine",
     )(target, gate, *returned)
 

time: 104 us -> 82.3 us (0.79)
  the two profiles are of different devices: /device:TPU:0 before, /device:TPU:8 now
where the time goes in v3:
time: 82.3 us; the launch traced here: 82 us
  blocking collectives  46.7 us (57%)
  waiting for transfers between devices  17.9 us (22%)
  Pallas kernels  10.3 us (13%)
  starting transfers between devices  4.28 us (5%)
  local copies, waits for them, and re-layouts  2.02 us (2%)
    all_to_all x2, blocking collectives, exchange(): lax.all_to_all(block.reshape(peers, chunk, block.shape[-1]), AXES, split_...  46.7 us
    ppermute x5, waiting for transfers between devices, swap(): return lax.ppermute(block, 'dp', pairs)  17.9 us
    pallas_call x3, Pallas kernels, run_expert(): pl.pallas_call(functools.partial(expert_kernel, biased), grid=(tall // he...  5.6 us
    ppermute x5, starting transfers between devices, swap(): return lax.ppermute(block, 'dp', pairs)  4.28 us
    pallas_call x1, Pallas kernels, on_device(): pl.pallas_call(functools.partial(dispatch_kernel, half, chunk, experts),...  2.81 us
    unnamed x20, local copies, waits for them, and re-layouts  1.97 us
  transfers between devices with their start and end apart: 5, of which 3 were waited for; matrix products, arithmetic and copies ran while one was open for 0% of the time, Pallas kernels for 7%

profile of v3, /device:TPU:8, one launch (start us, length us, event | category | flops | bytes accessed | tf_op | source)
XLA Modules:
  0.0 82.0 jit_solution(15362110032525419025)
XLA Ops:
  0.7 2.8 %dispatch.1 = (bf16[256,1280]{1,0:T(8,128)(2,1)}, s32[1,256]{1,0:T(1,128)}, bf16[2,128,1280]{2,1,0:T(8,128)(2,1)}) custom-call(bf16[256,1280]{1,0:T(8,128)(2,1)} %tokens.1, f32[1280]{0:T(1024)} %gain.1, s32[1,256]{1,0:T(1,128)} %bitcast.22, s32[1,256]{1,0:T(1,128)} %bitcast.28), custom_call_target="tpu_custom_call" | custom-call | tf_op jit(solution)/shard_map/dispatch/pallas_call | solution.py:154
  3.5 23.8 %all_to_all.10 = bf16[16,16,1280]{2,1,0:T(8,128)(2,1)S(1)} all-to-all(bf16[16,16,1280]{2,1,0:T(8,128)(2,1)} %bitcast.25), channel_id=1, replica_groups={{0,1,2,3,4,5,6,7,24,25,26,27,28,29,30,31},{8,9,10,11,12,13,14,15,16,17,..., dimensions={0} | all-to-all | bytes 1310720 | tf_op jit(solution)/shard_map/all_to_all | solution.py:167
  27.3 0.1 collective-permute-start
  27.4 2.0 %collective-permute-start.2 = (bf16[128,1280]{1,0:T(8,128)(2,1)S(1)}, bf16[128,1280]{1,0:T(8,128)(2,1)S(1)}, u32[]{:S(2)}, u32[]{:S(2)}) collective-permute-start(bf16[128,1280]{1,0:T(8,128)(2,1)S(1)} %bitcast.26), channel_id=1, source_target_pairs={{0,8},{8,0},{16,24},{24,16},{1,9},{9,1},{17,25},{25,17},{2,10},{10... | collective-permute-start | bytes 983048 | tf_op jit(solution)/shard_map/ppermute | solution.py:177
  29.4 8.6 %collective-permute-done.rows = bf16[128,1280]{1,0:T(8,128)(2,1)S(1)} collective-permute-done((bf16[128,1280]{1,0:T(8,128)(2,1)S(1)}, bf16[128,1280]{1,0:T(8,128)(2,1)S(1)}, u32[]{:S(2)}, u32[]{:S(2)}) %collective-permute-start) | collective-permute-done | bytes 327712 | tf_op jit(solution)/shard_map/ppermute | solution.py:177
  38.0 0.0 copy-start.1
  38.0 1.9 %copy-done.1 = bf16[1,1280,1280]{2,1,0:T(8,128)(2,1)S(1)} copy-done((bf16[1,1280,1280]{2,1,0:T(8,128)(2,1)S(1)}, bf16[1,1280,1280]{2,1,0:T(8,128)(2,1)}, u32[]{:S(2)}) %copy-start.1) | copy-done | bytes 3276824
  39.9 1.8 %theirs.2 = bf16[128,1280]{1,0:T(8,128)(2,1)S(1)} custom-call(bf16[128,1280]{1,0:T(8,128)(2,1)S(1)} %collective-permute-done.rows, bf16[1280,1280]{1,0:T(8,128)(2,1)S(1)} %bitcast.12, bf16[1,1280]{1,0:T(2,128)(2,1)S(1)} %copy-done.4, bf16[1280,1280]{1,0:T(8,128)(2,1)S(1)} %bitcast.15, bf16[1,1280]{1,0:T(2,128)(2,1)S(1)} %copy-done.5), custom_call_target="tpu_custom_call" | custom-call | flops 838860800 | bytes 7208960 | tf_op jit(solution)/shard_map/theirs/pallas_call | solution.py:198
  41.7 0.0 copy-start.3
  41.7 0.0 copy-start.6
  41.7 0.0 copy-start.7
  41.7 0.0 copy-start.8
  41.7 0.0 copy-start.2
  41.7 0.1 collective-permute-start.1
  41.8 3.2 %collective-permute-done.2.rows = bf16[128,1280]{1,0:T(8,128)(2,1)S(1)} collective-permute-done((bf16[128,1280]{1,0:T(8,128)(2,1)S(1)}, bf16[128,1280]{1,0:T(8,128)(2,1)S(1)}, u32[]{:S(2)}, u32[]{:S(2)}) %collective-permute-start.2) | collective-permute-done | bytes 327712 | tf_op jit(solution)/shard_map/ppermute | solution.py:177
  45.0 1.8 %theirs.3 = bf16[128,1280]{1,0:T(8,128)(2,1)S(1)} custom-call(bf16[128,1280]{1,0:T(8,128)(2,1)S(1)} %collective-permute-done.2.rows, bf16[1280,1280]{1,0:T(8,128)(2,1)S(1)} %bitcast.13, bf16[1,1280]{1,0:T(2,128)(2,1)S(1)} %copy-done.4, bf16[1280,1280]{1,0:T(8,128)(2,1)S(1)} %bitcast.16, bf16[1,1280]{1,0:T(2,128)(2,1)S(1)} %copy-done.5), custom_call_target="tpu_custom_call" | custom-call | flops 838860800 | bytes 7208960 | tf_op jit(solution)/shard_map/theirs/pallas_call | solution.py:198
  46.7 0.1 collective-permute-start.3
  46.9 0.4 router.1
  47.3 2.1 %collective-permute-start.4 = (f32[8,128]{1,0:T(8,128)S(1)}, f32[8,128]{1,0:T(8,128)S(1)}, u32[]{:S(2)}, u32[]{:S(2)}) collective-permute-start(f32[8,128]{1,0:T(8,128)S(1)} %get-tuple-element.11.refs_2_), channel_id=1, source_target_pairs={{0,8},{8,0},{16,24},{24,16},{1,9},{9,1},{17,25},{25,17},{2,10},{10... | collective-permute-start | bytes 12296 | tf_op jit(solution)/shard_map/ppermute | solution.py:177
  49.4 2.1 %own.1 = f32[256,1280]{1,0:T(8,128)S(1)} custom-call(bf16[256,1280]{1,0:T(8,128)(2,1)S(1)} %bitcast.18, bf16[1280,1280]{1,0:T(8,128)(2,1)S(1)} %bitcast.14, bf16[1,1280]{1,0:T(2,128)(2,1)S(1)} %copy-done.4, bf16[1280,1280]{1,0:T(8,128)(2,1)S(1)} %bitcast.17, bf16[1,1280]{1,0:T(2,128)(2,1)S(1)} %copy-done.5), custom_call_target="tpu_custom_call" | custom-call | flops 1677721600 | bytes 7864320 | tf_op jit(solution)/shard_map/own/pallas_call | solution.py:198
  51.5 6.1 %collective-permute-done.4.refs_3_ = f32[8,128]{1,0:T(8,128)S(1)} collective-permute-done((f32[8,128]{1,0:T(8,128)S(1)}, f32[8,128]{1,0:T(8,128)S(1)}, u32[]{:S(2)}, u32[]{:S(2)}) %collective-permute-start.4) | collective-permute-done | bytes 4128 | tf_op jit(solution)/shard_map/ppermute | solution.py:177
  57.6 0.2 sum.1
  57.8 22.9 %all_to_all.11 = bf16[16,16,1408]{2,1,0:T(8,128)(2,1)S(1)} all-to-all(bf16[16,16,1408]{2,1,0:T(8,128)(2,1)S(1)} %bitcast.20), channel_id=1, replica_groups={{0,1,2,3,4,5,6,7,24,25,26,27,28,29,30,31},{8,9,10,11,12,13,14,15,16,17,..., dimensions={0} | all-to-all | bytes 1441792 | tf_op jit(solution)/shard_map/all_to_all | solution.py:167
  80.8 1.3 %combine.1 = (bf16[256,1280]{1,0:T(8,128)(2,1)}, f32[2,2]{1,0:T(2,128)}) custom-call(s32[1,256]{1,0:T(1,128)S(1)} %copy-done.9, f32[8,256]{1,0:T(8,128)S(1)} %get-tuple-element.9.gate, bf16[256,1408]{1,0:T(8,128)(2,1)S(1)} %bitcast.19), custom_call_target="tpu_custom_call" | custom-call | tf_op jit(solution)/shard_map/combine/pallas_call | solution.py:245
  (16 shorter events, 0.1 us)
Async XLA Ops:
  0.6 37.3 %copy-start.5 = (bf16[1,1280]{1,0:T(2,128)(2,1)S(1)}, bf16[1,1280]{1,0:T(2,128)(2,1)}, u32[]{:S(2)}) copy-start(bf16[1,1280]{1,0:T(2,128)(2,1)} %last_bias.5) | copy-start | bytes 7684
  0.6 37.3 %copy-start.4 = (bf16[1,1280]{1,0:T(2,128)(2,1)S(1)}, bf16[1,1280]{1,0:T(2,128)(2,1)}, u32[]{:S(2)}) copy-start(bf16[1,1280]{1,0:T(2,128)(2,1)} %first_bias.5) | copy-start | bytes 7684
  0.7 37.3 %copy-start = (bf16[1,1280,1280]{2,1,0:T(8,128)(2,1)S(1)}, bf16[1,1280,1280]{2,1,0:T(8,128)(2,1)}, u32[]{:S(2)}) copy-start(bf16[1,1280,1280]{2,1,0:T(8,128)(2,1)} %param.13) | copy-start | bytes 9830404
  27.3 10.6 %collective-permute-start = (bf16[128,1280]{1,0:T(8,128)(2,1)S(1)}, bf16[128,1280]{1,0:T(8,128)(2,1)S(1)}, u32[]{:S(2)}, u32[]{:S(2)}) collective-permute-start(bf16[128,1280]{1,0:T(8,128)(2,1)S(1)} %bitcast.27), channel_id=1, source_target_pairs={{0,8},{8,0},{16,24},{24,16},{1,9},{9,1},{17,25},{25,17},{2,10},{10... | collective-permute-start | bytes 983048 | tf_op jit(solution)/shard_map/ppermute | solution.py:177
  27.4 17.6 %collective-permute-start.2 = (bf16[128,1280]{1,0:T(8,128)(2,1)S(1)}, bf16[128,1280]{1,0:T(8,128)(2,1)S(1)}, u32[]{:S(2)}, u32[]{:S(2)}) collective-permute-start(bf16[128,1280]{1,0:T(8,128)(2,1)S(1)} %bitcast.26), channel_id=1, source_target_pairs={{0,8},{8,0},{16,24},{24,16},{1,9},{9,1},{17,25},{25,17},{2,10},{10... | collective-permute-start | bytes 983048 | tf_op jit(solution)/shard_map/ppermute | solution.py:177
  38.0 1.9 %copy-start.1 = (bf16[1,1280,1280]{2,1,0:T(8,128)(2,1)S(1)}, bf16[1,1280,1280]{2,1,0:T(8,128)(2,1)}, u32[]{:S(2)}) copy-start(bf16[1,1280,1280]{2,1,0:T(8,128)(2,1)} %param.15) | copy-start | bytes 9830404
  41.7 5.2 %copy-start.3 = (bf16[256,1280]{1,0:T(8,128)(2,1)S(1)}, bf16[256,1280]{1,0:T(8,128)(2,1)}, u32[]{:S(2)}) copy-start(bf16[256,1280]{1,0:T(8,128)(2,1)} %get-tuple-element.8.normed) | copy-start | bytes 1966084
  41.7 5.2 %copy-start.6 = (bf16[1280,8]{0,1:T(8,128)(2,1)S(1)}, bf16[1280,8]{0,1:T(8,128)(2,1)}, u32[]{:S(2)}) copy-start(bf16[1280,8]{0,1:T(8,128)(2,1)} %param.12) | copy-start | bytes 61444
  41.7 5.2 %copy-start.7 = (s32[256]{0:T(256)S(1)}, s32[256]{0:T(256)}, u32[]{:S(2)}) copy-start(s32[256]{0:T(256)} %param.17) | copy-start | bytes 3076
  41.7 5.2 %copy-start.8 = (s32[256]{0:T(256)S(1)}, s32[256]{0:T(256)}, u32[]{:S(2)}) copy-start(s32[256]{0:T(256)} %param.18) | copy-start | bytes 3076
  41.7 7.7 %copy-start.2 = (bf16[1,1280,1280]{2,1,0:T(8,128)(2,1)S(1)}, bf16[1,1280,1280]{2,1,0:T(8,128)(2,1)}, u32[]{:S(2)}) copy-start(bf16[1,1280,1280]{2,1,0:T(8,128)(2,1)} %param.15) | copy-start | bytes 9830404
  41.7 15.9 %collective-permute-start.1 = (bf16[128,1280]{1,0:T(8,128)(2,1)S(1)}, bf16[128,1280]{1,0:T(8,128)(2,1)S(1)}, u32[]{:S(2)}, u32[]{:S(2)}) collective-permute-start(bf16[128,1280]{1,0:T(8,128)(2,1)S(1)} %theirs.2), channel_id=1, source_target_pairs={{0,8},{8,0},{16,24},{24,16},{1,9},{9,1},{17,25},{25,17},{2,10},{10... | collective-permute-start | bytes 983048 | tf_op jit(solution)/shard_map/ppermute | solution.py:177
  46.7 10.9 %collective-permute-start.3 = (bf16[128,1280]{1,0:T(8,128)(2,1)S(1)}, bf16[128,1280]{1,0:T(8,128)(2,1)S(1)}, u32[]{:S(2)}, u32[]{:S(2)}) collective-permute-start(bf16[128,1280]{1,0:T(8,128)(2,1)S(1)} %theirs.3), channel_id=1, source_target_pairs={{0,8},{8,0},{16,24},{24,16},{1,9},{9,1},{17,25},{25,17},{2,10},{10... | collective-permute-start | bytes 983048 | tf_op jit(solution)/shard_map/ppermute | solution.py:177
  47.3 10.3 %collective-permute-start.4 = (f32[8,128]{1,0:T(8,128)S(1)}, f32[8,128]{1,0:T(8,128)S(1)}, u32[]{:S(2)}, u32[]{:S(2)}) collective-permute-start(f32[8,128]{1,0:T(8,128)S(1)} %get-tuple-element.11.refs_2_), channel_id=1, source_target_pairs={{0,8},{8,0},{16,24},{24,16},{1,9},{9,1},{17,25},{25,17},{2,10},{10... | collective-permute-start | bytes 12296 | tf_op jit(solution)/shard_map/ppermute | solution.py:177
  51.4 29.3 %copy-start.9 = (s32[1,256]{1,0:T(1,128)S(1)}, s32[1,256]{1,0:T(1,128)}, u32[]{:S(2)}) copy-start(s32[1,256]{1,0:T(1,128)} %get-tuple-element.7.target) | copy-start | bytes 3076

commit v4 on v2

v4 whole, which is shorter than its diff:
```python
import functools

import jax
import jax.numpy as jnp
from jax import lax
from jax.experimental import pallas as pl
from jax.experimental.pallas import tpu as pltpu
from jax.sharding import PartitionSpec as P

CAP = 16
PARTS = 2
LANES = 128
AXES = ("dp", "expert")
VMEM = pl.BlockSpec(memory_space=pltpu.VMEM)
PARAMS = pltpu.CompilerParams(vmem_limit_bytes=24 << 20)


def one_hot(rows, target):
    row = lax.broadcasted_iota(jnp.int32, (rows, target.shape[1]), 0)
    return (row == target).astype(jnp.float32).astype(jnp.bfloat16)


def spread_stats(total, rows, period):
    row = lax.broadcasted_iota(jnp.int32, (rows, LANES), 0) % period
    out = jnp.zeros((rows, LANES), jnp.float32)
    for piece in range(3):
        rounded = total.astype(jnp.bfloat16).astype(jnp.float32)
        out = jnp.where(row == piece, rounded, out)
        total = total - rounded
    return out.astype(jnp.bfloat16)


def join_stats(block):
    return jnp.sum(block.astype(jnp.float32), axis=0, keepdims=True)


def dispatch_kernel(tokens, gain, choice, slot, normed_out, target_out, buffer):
    values = tokens[...].astype(jnp.float32)
    center = values - jnp.mean(values, axis=-1, keepdims=True)
    spread = jnp.mean(center * center, axis=-1, keepdims=True)
    scaled = center * lax.rsqrt(spread + 1e-06) * gain[...].reshape(1, values.shape[1])
    normed = scaled.astype(jnp.bfloat16)
    normed_out[...] = normed
    target = jnp.where(slot[...] >= 0, choice[...] * CAP + slot[...], -1)
    target_out[...] = target
    table = one_hot(buffer.shape[0], target)
    buffer[...] = jnp.dot(table, normed, preferred_element_type=jnp.float32).astype(jnp.bfloat16)


def router_kernel(normed, router, choice, modality, first, second, gate_out, stats_out):
    logits = lax.dot_general(
        router[...], normed[...], (((1,), (1,)), ((), ())), preferred_element_type=jnp.float32
    )
    shifted = logits - jnp.max(logits, axis=0, keepdims=True)
    logp = shifted - jnp.log(jnp.sum(jnp.exp(shifted), axis=0, keepdims=True))
    probs = jnp.exp(logp)
    experts = probs.shape[0]
    expert = lax.broadcasted_iota(jnp.int32, probs.shape, 0)
    gate = jnp.sum(jnp.where(expert == choice[...], probs, 0.0), axis=0, keepdims=True)
    gate_out[...] = jnp.broadcast_to(gate, gate_out.shape)
    textual = (modality[...] == 1).astype(jnp.float32)
    entropy = -jnp.sum(probs * logp, axis=0, keepdims=True)
    lane = lax.broadcasted_iota(jnp.int32, (experts, LANES), 1)
    row = lax.broadcasted_iota(jnp.int32, (experts, LANES), 0)
    line = lane[0:1]
    stats = jnp.zeros((1, LANES), jnp.float32)
    for kind, select in enumerate((1.0 - textual, textual)):
        prob_sum = jnp.sum(probs * select, axis=1, keepdims=True)
        spread = jnp.where(lane == row + kind * experts, prob_sum, 0.0)
        stats = stats + jnp.sum(spread, axis=0, keepdims=True)
        ent_sum = jnp.sum(entropy * select, axis=1, keepdims=True)
        count = jnp.sum(select, axis=1, keepdims=True)
        stats = jnp.where(line == 2 * experts + kind, ent_sum, stats)
        stats = jnp.where(line == 2 * experts + 2 + kind, count, stats)
    stats_out[...] = jnp.broadcast_to(stats, stats_out.shape)


def expert_kernel(carry, rows, first, first_bias, second, *refs):
    stats, out = refs if carry else (None, refs[0])
    pre = lax.dot_general(
        rows[...], first[...], (((1,), (1,)), ((), ())), preferred_element_type=jnp.float32
    )
    pre = pre + first_bias[...].astype(jnp.float32)
    hidden = (0.5 * pre * (1.0 + lax.erf(pre * (0.5**0.5)))).astype(jnp.bfloat16)
    result = jnp.dot(hidden, second[...], preferred_element_type=jnp.float32)
    if carry:
        width = result.shape[1]
        out[:, :width] = result.astype(out.dtype)
        out[:, width:] = spread_stats(stats[0:1], out.shape[0], out.shape[0])
    else:
        out[...] = result.astype(out.dtype)


def far_kernel(carry, own, other, *refs):
    out = refs[-1]
    width = own.shape[1]
    out[:, :width] = (own[...] + other[:, :width].astype(jnp.float32)).astype(jnp.bfloat16)
    if carry:
        stats, other_stats = refs[0], refs[1]
        total = stats[0:1] + join_stats(other_stats[:, width:])
        out[:, width:] = spread_stats(total, out.shape[0], out.shape[0])


def near_kernel(parts, own, other, bias, stats, other_stats, *refs):
    far, out = refs[:-1], refs[-1]
    width = own.shape[1]
    result = own[...] + other[...].astype(jnp.float32) + bias[...].astype(jnp.float32)
    total = stats[0:1] + join_stats(other_stats[:, width:])
    tall = own.shape[0] // parts
    for part in range(parts):
        rows = slice(part * tall, (part + 1) * tall)
        piece = result[rows]
        for block in far[part::parts]:
            piece = piece + block[:, :width].astype(jnp.float32)
        out[rows, :width] = piece.astype(jnp.bfloat16)
    for block in far[::parts]:
        total = total + join_stats(block[:, width:])
    out[:, width:] = spread_stats(total, out.shape[0], CAP)


def combine_kernel(experts, target, gate, returned, out, aux):
    width = out.shape[1]
    table = one_hot(returned.shape[0], target[...])
    fetched = lax.dot_general(
        table, returned[:, :width], (((0,), (0,)), ((), ())), preferred_element_type=jnp.float32
    )
    scale = jnp.transpose(gate[...])[:, 0:1]
    out[...] = (scale * fetched).astype(jnp.bfloat16)
    sums = join_stats(returned[:, width:])
    lane = lax.broadcasted_iota(jnp.int32, sums.shape, 1)

    def pick(at):
        return jnp.sum(jnp.where(lane == at, sums, 0.0), axis=1, keepdims=True)

    row = lax.broadcasted_iota(jnp.int32, aux.shape, 0)
    column = lax.broadcasted_iota(jnp.int32, aux.shape, 1)
    result = jnp.zeros(aux.shape, jnp.float32)
    for kind in range(2):
        count = pick(2 * experts + 2 + kind)
        local = pick(2 * experts + kind) / count
        pbar = sums / count
        inside = (lane >= kind * experts) & (lane < (kind + 1) * experts)
        terms = jnp.where(inside, pbar * jnp.log(pbar), 0.0)
        spread = jnp.sum(terms, axis=1, keepdims=True)
        result = jnp.where((row == kind) & (column == 0), local, result)
        result = jnp.where((row == kind) & (column == 1), spread, result)
    aux[...] = result


def on_device(tokens, ln_gain, router, w_in, b_in, w_out, b_out, expert_choice, modality, slot):
    count, width = tokens.shape
    experts = router.shape[1]
    layers, senders = lax.axis_size("dp"), lax.axis_size("expert")
    assert w_in.shape[0] == 1 and experts == senders and layers % 4 == 0
    assert 2 * experts + 4 <= LANES
    hidden = w_in.shape[1]
    rows = experts * CAP
    tall = rows // PARTS
    full = width + LANES
    far_steps = [m ^ ((m >> 1) & 1) for m in range(2, layers, 2)]
    choice = expert_choice.reshape(1, count)
    normed, target, buffer = pl.pallas_call(
        dispatch_kernel,
        out_shape=[
            jax.ShapeDtypeStruct((count, width), jnp.bfloat16),
            jax.ShapeDtypeStruct((1, count), jnp.int32),
            jax.ShapeDtypeStruct((rows, width), jnp.bfloat16),
        ],
        in_specs=[VMEM] * 4,
        out_specs=[VMEM] * 3,
        name="dispatch",
    )(tokens, ln_gain, choice, slot.reshape(1, count))

    def exchange(block):
        return lax.all_to_all(
            block.reshape(experts, CAP, block.shape[-1]), "expert", split_axis=0, concat_axis=0, tiled=True
        ).reshape(rows, block.shape[-1])

    def swap(block, step):
        return lax.ppermute(block, "dp", [(z, z ^ step) for z in range(layers)])

    home = exchange(buffer)
    halves = [home[at : at + tall] for at in range(0, rows, tall)]
    visitors = [swap(part, step) for step in far_steps for part in halves]
    beside = swap(home, 1)
    first = pltpu.with_memory_space_constraint(w_in.reshape(hidden, width), pltpu.VMEM)
    second = pltpu.with_memory_space_constraint(w_out.reshape(hidden, width), pltpu.VMEM)
    gate, stats = pl.pallas_call(
        router_kernel,
        out_shape=[
            jax.ShapeDtypeStruct((8, count), jnp.float32),
            jax.ShapeDtypeStruct((8, LANES), jnp.float32),
        ],
        in_specs=[VMEM] * 6,
        out_specs=[VMEM] * 2,
        compiler_params=PARAMS,
        name="router",
    )(normed, router.T, choice, modality.reshape(1, count), first, second)

    def run_expert(part, dtype, carry=False):
        size = part.shape[0]
        columns = full if carry else width
        return pl.pallas_call(
            functools.partial(expert_kernel, carry),
            out_shape=jax.ShapeDtypeStruct((size, columns), dtype),
            in_specs=[VMEM] * (5 if carry else 4),
            out_specs=VMEM,
            cost_estimate=pl.CostEstimate(
                flops=4 * size * width * hidden,
                bytes_accessed=4 * width * (hidden + size),
                transcendentals=size * hidden,
            ),
            compiler_params=PARAMS,
        )(*((part, first, b_in, second) + ((stats,) if carry else ())))

    forwarded = [swap(part, 1) for part in visitors]
    answers = [
        swap(run_expert(part, jnp.bfloat16, index % PARTS == 0), 1)
        for index, part in enumerate(forwarded)
    ]
    answer = swap(run_expert(beside, jnp.bfloat16), 1)
    returned = []
    for index, part in enumerate(visitors):
        carry = index % PARTS == 0
        own = run_expert(part, jnp.float32)
        operands = (own, answers[index]) + ((stats, answers[0]) if carry else ())
        summed = pl.pallas_call(
            functools.partial(far_kernel, carry),
            out_shape=jax.ShapeDtypeStruct((tall, full if carry else width), jnp.bfloat16),
            in_specs=[VMEM] * len(operands),
            out_specs=VMEM,
            compiler_params=PARAMS,
            name="far_sum",
        )(*operands)
        returned.append(swap(summed, far_steps[index // PARTS]))
    own = run_expert(home, jnp.float32)
    summed = pl.pallas_call(
        functools.partial(near_kernel, PARTS),
        out_shape=jax.ShapeDtypeStruct((rows, full), jnp.bfloat16),
        in_specs=[VMEM] * (5 + len(returned)),
        out_specs=VMEM,
        compiler_params=PARAMS,
        name="near_sum",
    )(own, answer, b_out, stats, answers[0], *returned)
    return pl.pallas_call(
        functools.partial(combine_kernel, experts),
        out_shape=[
            jax.ShapeDtypeStruct((count, width), jnp.bfloat16),
            jax.ShapeDtypeStruct((2, 2), jnp.float32),
        ],
        in_specs=[VMEM] * 3,
        out_specs=[VMEM] * 2,
        compiler_params=PARAMS,
        name="combine",
    )(target, gate, exchange(summed))


def solution(mesh):
    return jax.shard_map(
        on_device,
        mesh=mesh,
        in_specs=(
            P(AXES, None),
            P(),
            P(),
            P("expert", "dp", None),
            P("expert", "dp"),
            P("expert", "dp", None),
            P("expert", None),
            P(AXES),
            P(AXES),
            P(AXES),
        ),
        out_specs=(P(AXES, None), P()),
        check_vma=False,
    )
```

time: 104 us -> 82.2 us (0.79)
  Pallas kernels: 33.2 us -> 15.1 us
  blocking collectives: 36 us -> 23.1 us
  local copies, waits for them, and re-layouts: 4.2 us -> 9.53 us
  starting transfers between devices: 14.6 us -> 19.8 us
    pallas_call x8 -> x11, Pallas kernels: 31 us -> 14.6 us  [the longest x6 10.6 us: run_expert(): pl.pallas_call(functools.partial(expert_kernel, carry), out_shape=jax.Sha...]
    ppermute x5 -> x10, starting transfers between devices: 4.64 us -> 19.8 us  [swap(): return lax.ppermute(block, 'dp', [(z, z ^ step) for z in range(layers)])]
    all_to_all x2, blocking collectives: 36 us -> 23.1 us  [exchange(): lax.all_to_all(block.reshape(experts, CAP, block.shape[-1]), 'expert', sp...]
    all_to_all x2 -> x0, starting transfers between devices: 9.98 us -> none  [exchange(): lax.all_to_all(block.reshape(peers, chunk, block.shape[-1]), AXES, split_...]
    unnamed x18 -> x22, local copies, waits for them, and re-layouts: 2.27 us -> 9.5 us
    all_to_all x2 -> x0, waiting for transfers between devices: 6.56 us -> none  [exchange(): lax.all_to_all(block.reshape(peers, chunk, block.shape[-1]), AXES, split_...]
    ppermute x5 -> x10, waiting for transfers between devices: 7.85 us -> 13.5 us  [swap(): return lax.ppermute(block, 'dp', [(z, z ^ step) for z in range(layers)])]
    pallas_call x1, Pallas kernels: 2.14 us -> 0.44 us  [on_device(): pl.pallas_call(router_kernel, out_shape=[jax.ShapeDtypeStruct((8, count),...]
  transfers between devices with their start and end apart: 7 -> 10, of which waited for: 4 -> 3; matrix products, arithmetic and copies ran while one was open for 1% -> 0% of each run, Pallas kernels for 27% -> 14%
where the time goes in v4:
time: 82.2 us; the launch traced here: 81.7 us
  blocking collectives  23.1 us (28%)
  starting transfers between devices  19.8 us (24%)
  Pallas kernels  15.1 us (18%)
  waiting for transfers between devices  13.5 us (16%)
  local copies, waits for them, and re-layouts  9.53 us (12%)
    all_to_all x2, blocking collectives, exchange(): lax.all_to_all(block.reshape(experts, CAP, block.shape[-1]), 'expert', sp...  23.1 us
    ppermute x10, starting transfers between devices, swap(): return lax.ppermute(block, 'dp', [(z, z ^ step) for z in range(layers)])  19.8 us
    ppermute x10, waiting for transfers between devices, swap(): return lax.ppermute(block, 'dp', [(z, z ^ step) for z in range(layers)])  13.5 us
    pallas_call x6, Pallas kernels, run_expert(): pl.pallas_call(functools.partial(expert_kernel, carry), out_shape=jax.Sha...  10.6 us
    unnamed x22, local copies, waits for them, and re-layouts  9.5 us
    pallas_call x1, Pallas kernels, on_device(): pl.pallas_call(dispatch_kernel, out_shape=[jax.ShapeDtypeStruct((count, w...  2.52 us
  transfers between devices with their start and end apart: 10, of which 3 were waited for; matrix products, arithmetic and copies ran while one was open for 0% of the time, Pallas kernels for 14%

profile of v4, /device:TPU:0, one launch (start us, length us, event | category | flops | bytes accessed | tf_op | source)
XLA Modules:
  0.0 81.7 jit_solution(3221583420404349759)
XLA Ops:
  0.6 2.5 %dispatch.1 = (bf16[256,1280]{1,0:T(8,128)(2,1)}, s32[1,256]{1,0:T(1,128)}, bf16[128,1280]{1,0:T(8,128)(2,1)}) custom-call(bf16[256,1280]{1,0:T(8,128)(2,1)} %tokens.1, f32[1280]{0:T(1024)} %gain.1, s32[1,256]{1,0:T(1,128)} %bitcast.31, s32[1,256]{1,0:T(1,128)} %bitcast.37), custom_call_target="tpu_custom_call" | custom-call | tf_op jit(solution)/shard_map/dispatch/pallas_call | solution.py:162
  3.2 12.8 %all_to_all.10 = bf16[8,16,1280]{2,1,0:T(8,128)(2,1)S(1)} all-to-all(bf16[8,16,1280]{2,1,0:T(8,128)(2,1)} %bitcast.34), channel_id=1, replica_groups=mesh['dp'=4,'expert'=8] {'expert'}, dimensions={0} | all-to-all | bytes 655360 | tf_op jit(solution)/shard_map/all_to_all | solution.py:175
  16.0 3.7 %collective-permute-start.6 = (bf16[64,1280]{1,0:T(8,128)(2,1)S(1)}, bf16[64,1280]{1,0:T(8,128)(2,1)S(1)}, u32[]{:S(2)}, u32[]{:S(2)}) collective-permute-start(bf16[64,1280]{1,0:T(8,128)(2,1)S(1)} %bitcast.36), channel_id=1, source_target_pairs={{0,24},{8,16},{16,8},{24,0},{1,25},{9,17},{17,9},{25,1},{2,26},{10... | collective-permute-start | bytes 491528 | tf_op jit(solution)/shard_map/ppermute | solution.py:180
  19.9 4.4 %collective-permute-done.6.rows = bf16[64,1280]{1,0:T(8,128)(2,1)S(1)} collective-permute-done((bf16[64,1280]{1,0:T(8,128)(2,1)S(1)}, bf16[64,1280]{1,0:T(8,128)(2,1)S(1)}, u32[]{:S(2)}, u32[]{:S(2)}) %collective-permute-start.6) | collective-permute-done | bytes 163872 | tf_op jit(solution)/shard_map/ppermute | solution.py:180
  24.3 7.2 %collective-permute-start.7 = (bf16[64,1280]{1,0:T(8,128)(2,1)S(1)}, bf16[64,1280]{1,0:T(8,128)(2,1)S(1)}, u32[]{:S(2)}, u32[]{:S(2)}) collective-permute-start(bf16[64,1280]{1,0:T(8,128)(2,1)S(1)} %collective-permute-done.6.rows), channel_id=1, source_target_pairs={{0,8},{8,0},{16,24},{24,16},{1,9},{9,1},{17,25},{25,17},{2,10},{10... | collective-permute-start | bytes 491528 | tf_op jit(solution)/shard_map/ppermute | solution.py:180
  31.5 2.6 %collective-permute-start.3 = (bf16[64,1280]{1,0:T(8,128)(2,1)S(1)}, bf16[64,1280]{1,0:T(8,128)(2,1)S(1)}, u32[]{:S(2)}, u32[]{:S(2)}) collective-permute-start(bf16[64,1280]{1,0:T(8,128)(2,1)S(1)} %collective-permute-done.2.rows), channel_id=1, source_target_pairs={{0,8},{8,0},{16,24},{24,16},{1,9},{9,1},{17,25},{25,17},{2,10},{10... | collective-permute-start | bytes 491528 | tf_op jit(solution)/shard_map/ppermute | solution.py:180
  34.0 1.9 %copy-done = bf16[1,1280,1280]{2,1,0:T(8,128)(2,1)S(1)} copy-done((bf16[1,1280,1280]{2,1,0:T(8,128)(2,1)S(1)}, bf16[1,1280,1280]{2,1,0:T(8,128)(2,1)}, u32[]{:S(2)}) %copy-start) | copy-done | bytes 3276824
  36.0 1.9 %copy-done.2 = bf16[1,1280,1280]{2,1,0:T(8,128)(2,1)S(1)} copy-done((bf16[1,1280,1280]{2,1,0:T(8,128)(2,1)S(1)}, bf16[1,1280,1280]{2,1,0:T(8,128)(2,1)}, u32[]{:S(2)}) %copy-start.2) | copy-done | bytes 3276824
  37.9 1.1 %copy-done.4 = bf16[256,1280]{1,0:T(8,128)(2,1)S(1)} copy-done((bf16[256,1280]{1,0:T(8,128)(2,1)S(1)}, bf16[256,1280]{1,0:T(8,128)(2,1)}, u32[]{:S(2)}) %copy-start.4) | copy-done | bytes 655384
  41.5 1.5 %copy-done.1 = bf16[1,1280,1280]{2,1,0:T(8,128)(2,1)S(1)} copy-done((bf16[1,1280,1280]{2,1,0:T(8,128)(2,1)S(1)}, bf16[1,1280,1280]{2,1,0:T(8,128)(2,1)}, u32[]{:S(2)}) %copy-start.1) | copy-done | bytes 3276824
  43.0 1.0 %copy-done.3 = bf16[1,1280,1280]{2,1,0:T(8,128)(2,1)S(1)} copy-done((bf16[1,1280,1280]{2,1,0:T(8,128)(2,1)S(1)}, bf16[1,1280,1280]{2,1,0:T(8,128)(2,1)}, u32[]{:S(2)}) %copy-start.3) | copy-done | bytes 3276824
  44.0 1.8 %shard_map.118 = bf16[64,1280]{1,0:T(8,128)(2,1)S(1)} custom-call(bf16[64,1280]{1,0:T(8,128)(2,1)S(1)} %collective-permute-done.7.rows, bf16[1280,1280]{1,0:T(8,128)(2,1)S(1)} %bitcast.13, bf16[1,1280]{1,0:T(2,128)(2,1)S(1)} %copy-done.5, bf16[1280,1280]{1,0:T(8,128)(2,1)S(1)} %bitcast.20), custom_call_target="tpu_custom_call" | custom-call | flops 419430400 | bytes 6881280 | tf_op jit(solution)/shard_map/pallas_call | solution.py:203
  45.8 1.8 %shard_map.115 = bf16[64,1408]{1,0:T(8,128)(2,1)S(1)} custom-call(bf16[64,1280]{1,0:T(8,128)(2,1)S(1)} %collective-permute-done.3.rows, bf16[1280,1280]{1,0:T(8,128)(2,1)S(1)} %bitcast.14, bf16[1,1280]{1,0:T(2,128)(2,1)S(1)} %copy-done.5, bf16[1280,1280]{1,0:T(8,128)(2,1)S(1)} %bitcast.21, f32[8,128]{1,0:T(8,128)S(1)} %get-tuple-element.11.refs_0_.stats), custom_call_target="tpu_custom_call" | custom-call | flops 419430400 | bytes 6881280 | tf_op jit(solution)/shard_map/pallas_call | solution.py:203
  47.6 2.1 %collective-permute-start.4 = (bf16[64,1408]{1,0:T(8,128)(2,1)S(1)}, bf16[64,1408]{1,0:T(8,128)(2,1)S(1)}, u32[]{:S(2)}, u32[]{:S(2)}) collective-permute-start(bf16[64,1408]{1,0:T(8,128)(2,1)S(1)} %shard_map.115), channel_id=1, source_target_pairs={{0,8},{8,0},{16,24},{24,16},{1,9},{9,1},{17,25},{25,17},{2,10},{10... | collective-permute-start | bytes 540680 | tf_op jit(solution)/shard_map/ppermute | solution.py:180
  49.7 1.8 %shard_map.114 = bf16[128,1280]{1,0:T(8,128)(2,1)S(1)} custom-call(bf16[128,1280]{1,0:T(8,128)(2,1)S(1)} %collective-permute-done.rows, bf16[1280,1280]{1,0:T(8,128)(2,1)S(1)} %bitcast.15, bf16[1,1280]{1,0:T(2,128)(2,1)S(1)} %copy-done.5, bf16[1280,1280]{1,0:T(8,128)(2,1)S(1)} %bitcast.22), custom_call_target="tpu_custom_call" | custom-call | flops 838860800 | bytes 7208960 | tf_op jit(solution)/shard_map/pallas_call | solution.py:203
  51.5 1.8 %shard_map.116.own = f32[64,1280]{1,0:T(8,128)S(1)} custom-call(bf16[64,1280]{1,0:T(8,128)(2,1)S(1)} %collective-permute-done.2.rows, bf16[1280,1280]{1,0:T(8,128)(2,1)S(1)} %bitcast.16, bf16[1,1280]{1,0:T(2,128)(2,1)S(1)} %copy-done.5, bf16[1280,1280]{1,0:T(8,128)(2,1)S(1)} %bitcast.23), custom_call_target="tpu_custom_call" | custom-call | flops 419430400 | bytes 6881280 | tf_op jit(solution)/shard_map/pallas_call | solution.py:203
  53.3 3.5 %collective-permute-done.4.other.refs_1_.other_stats = bf16[64,1408]{1,0:T(8,128)(2,1)S(1)} collective-permute-done((bf16[64,1408]{1,0:T(8,128)(2,1)S(1)}, bf16[64,1408]{1,0:T(8,128)(2,1)S(1)}, u32[]{:S(2)}, u32[]{:S(2)}) %collective-permute-start.4) | collective-permute-done | bytes 180256 | tf_op jit(solution)/shard_map/ppermute | solution.py:180
  56.8 2.5 %collective-permute-start.5 = (bf16[64,1408]{1,0:T(8,128)(2,1)S(1)}, bf16[64,1408]{1,0:T(8,128)(2,1)S(1)}, u32[]{:S(2)}, u32[]{:S(2)}) collective-permute-start(bf16[64,1408]{1,0:T(8,128)(2,1)S(1)} %far_sum.2), channel_id=1, source_target_pairs={{0,24},{8,16},{16,8},{24,0},{1,25},{9,17},{17,9},{25,1},{2,26},{10... | collective-permute-start | bytes 540680 | tf_op jit(solution)/shard_map/ppermute | solution.py:180
  59.3 1.8 %shard_map.117.own = f32[64,1280]{1,0:T(8,128)S(1)} custom-call(bf16[64,1280]{1,0:T(8,128)(2,1)S(1)} %collective-permute-done.6.rows, bf16[1280,1280]{1,0:T(8,128)(2,1)S(1)} %bitcast.17, bf16[1,1280]{1,0:T(2,128)(2,1)S(1)} %copy-done.5, bf16[1280,1280]{1,0:T(8,128)(2,1)S(1)} %bitcast.24), custom_call_target="tpu_custom_call" | custom-call | flops 419430400 | bytes 6881280 | tf_op jit(solution)/shard_map/pallas_call | solution.py:203
  61.2 1.4 %collective-permute-start.9 = (bf16[64,1280]{1,0:T(8,128)(2,1)S(1)}, bf16[64,1280]{1,0:T(8,128)(2,1)S(1)}, u32[]{:S(2)}, u32[]{:S(2)}) collective-permute-start(bf16[64,1280]{1,0:T(8,128)(2,1)S(1)} %far_sum.3), channel_id=1, source_target_pairs={{0,24},{8,16},{16,8},{24,0},{1,25},{9,17},{17,9},{25,1},{2,26},{10... | collective-permute-start | bytes 491528 | tf_op jit(solution)/shard_map/ppermute | solution.py:180
  62.6 1.8 %shard_map.113.own = f32[128,1280]{1,0:T(8,128)S(1)} custom-call(bf16[128,1280]{1,0:T(8,128)(2,1)S(1)} %bitcast.27, bf16[1280,1280]{1,0:T(8,128)(2,1)S(1)} %bitcast.18, bf16[1,1280]{1,0:T(2,128)(2,1)S(1)} %copy-done.5, bf16[1280,1280]{1,0:T(8,128)(2,1)S(1)} %bitcast.25), custom_call_target="tpu_custom_call" | custom-call | flops 838860800 | bytes 7208960 | tf_op jit(solution)/shard_map/pallas_call | solution.py:203
  64.4 5.6 %collective-permute-done.9.refs_1_ = bf16[64,1280]{1,0:T(8,128)(2,1)S(1)} collective-permute-done((bf16[64,1280]{1,0:T(8,128)(2,1)S(1)}, bf16[64,1280]{1,0:T(8,128)(2,1)S(1)}, u32[]{:S(2)}, u32[]{:S(2)}) %collective-permute-start.9) | collective-permute-done | bytes 163872 | tf_op jit(solution)/shard_map/ppermute | solution.py:180
  70.1 10.3 %all_to_all.11 = bf16[8,16,1408]{2,1,0:T(8,128)(2,1)S(1)} all-to-all(bf16[8,16,1408]{2,1,0:T(8,128)(2,1)S(1)} %bitcast.28), channel_id=1, replica_groups=mesh['dp'=4,'expert'=8] {'expert'}, dimensions={0} | all-to-all | bytes 720896 | tf_op jit(solution)/shard_map/all_to_all | solution.py:175
  80.5 1.2 %combine.1 = (bf16[256,1280]{1,0:T(8,128)(2,1)}, f32[2,2]{1,0:T(2,128)}) custom-call(s32[1,256]{1,0:T(1,128)S(1)} %copy-done.9, f32[8,256]{1,0:T(8,128)S(1)} %get-tuple-element.9.gate, bf16[128,1408]{1,0:T(8,128)(2,1)S(1)} %bitcast.29), custom_call_target="tpu_custom_call" | custom-call | tf_op jit(solution)/shard_map/combine/pallas_call | solution.py:245
  (33 shorter events, 3.2 us)
Async XLA Ops:
  16.0 8.3 %collective-permute-start.6 = (bf16[64,1280]{1,0:T(8,128)(2,1)S(1)}, bf16[64,1280]{1,0:T(8,128)(2,1)S(1)}, u32[]{:S(2)}, u32[]{:S(2)}) collective-permute-start(bf16[64,1280]{1,0:T(8,128)(2,1)S(1)} %bitcast.36), channel_id=1, source_target_pairs={{0,24},{8,16},{16,8},{24,0},{1,25},{9,17},{17,9},{25,1},{2,26},{10... | collective-permute-start | bytes 491528 | tf_op jit(solution)/shard_map/ppermute | solution.py:180
  19.6 11.8 %collective-permute-start.2 = (bf16[64,1280]{1,0:T(8,128)(2,1)S(1)}, bf16[64,1280]{1,0:T(8,128)(2,1)S(1)}, u32[]{:S(2)}, u32[]{:S(2)}) collective-permute-start(bf16[64,1280]{1,0:T(8,128)(2,1)S(1)} %bitcast.35), channel_id=1, source_target_pairs={{0,24},{8,16},{16,8},{24,0},{1,25},{9,17},{17,9},{25,1},{2,26},{10... | collective-permute-start | bytes 491528 | tf_op jit(solution)/shard_map/ppermute | solution.py:180
  19.9 29.8 %collective-permute-start = (bf16[128,1280]{1,0:T(8,128)(2,1)S(1)}, bf16[128,1280]{1,0:T(8,128)(2,1)S(1)}, u32[]{:S(2)}, u32[]{:S(2)}) collective-permute-start(bf16[128,1280]{1,0:T(8,128)(2,1)S(1)} %bitcast.26), channel_id=1, source_target_pairs={{0,8},{8,0},{16,24},{24,16},{1,9},{9,1},{17,25},{25,17},{2,10},{10... | collective-permute-start | bytes 983048 | tf_op jit(solution)/shard_map/ppermute | solution.py:180
  24.3 17.2 %collective-permute-start.7 = (bf16[64,1280]{1,0:T(8,128)(2,1)S(1)}, bf16[64,1280]{1,0:T(8,128)(2,1)S(1)}, u32[]{:S(2)}, u32[]{:S(2)}) collective-permute-start(bf16[64,1280]{1,0:T(8,128)(2,1)S(1)} %collective-permute-done.6.rows), channel_id=1, source_target_pairs={{0,8},{8,0},{16,24},{24,16},{1,9},{9,1},{17,25},{25,17},{2,10},{10... | collective-permute-start | bytes 491528 | tf_op jit(solution)/shard_map/ppermute | solution.py:180
  31.5 14.4 %collective-permute-start.3 = (bf16[64,1280]{1,0:T(8,128)(2,1)S(1)}, bf16[64,1280]{1,0:T(8,128)(2,1)S(1)}, u32[]{:S(2)}, u32[]{:S(2)}) collective-permute-start(bf16[64,1280]{1,0:T(8,128)(2,1)S(1)} %collective-permute-done.2.rows), channel_id=1, source_target_pairs={{0,8},{8,0},{16,24},{24,16},{1,9},{9,1},{17,25},{25,17},{2,10},{10... | collective-permute-start | bytes 491528 | tf_op jit(solution)/shard_map/ppermute | solution.py:180
  34.0 1.9 %copy-start = (bf16[1,1280,1280]{2,1,0:T(8,128)(2,1)S(1)}, bf16[1,1280,1280]{2,1,0:T(8,128)(2,1)}, u32[]{:S(2)}) copy-start(bf16[1,1280,1280]{2,1,0:T(8,128)(2,1)} %param.13) | copy-start | bytes 9830404
  36.0 1.9 %copy-start.2 = (bf16[1,1280,1280]{2,1,0:T(8,128)(2,1)S(1)}, bf16[1,1280,1280]{2,1,0:T(8,128)(2,1)}, u32[]{:S(2)}) copy-start(bf16[1,1280,1280]{2,1,0:T(8,128)(2,1)} %param.15) | copy-start | bytes 9830404
  37.9 1.1 %copy-start.4 = (bf16[256,1280]{1,0:T(8,128)(2,1)S(1)}, bf16[256,1280]{1,0:T(8,128)(2,1)}, u32[]{:S(2)}) copy-start(bf16[256,1280]{1,0:T(8,128)(2,1)} %get-tuple-element.8.normed) | copy-start | bytes 1966084
  39.0 0.7 copy-start.6
  39.7 0.7 copy-start.8
  40.4 0.7 copy-start.10
  41.1 1.9 %copy-start.1 = (bf16[1,1280,1280]{2,1,0:T(8,128)(2,1)S(1)}, bf16[1,1280,1280]{2,1,0:T(8,128)(2,1)}, u32[]{:S(2)}) copy-start(bf16[1,1280,1280]{2,1,0:T(8,128)(2,1)} %param.13) | copy-start | bytes 9830404
  41.1 2.9 %copy-start.3 = (bf16[1,1280,1280]{2,1,0:T(8,128)(2,1)S(1)}, bf16[1,1280,1280]{2,1,0:T(8,128)(2,1)}, u32[]{:S(2)}) copy-start(bf16[1,1280,1280]{2,1,0:T(8,128)(2,1)} %param.15) | copy-start | bytes 9830404
  41.1 2.9 %copy-start.5 = (bf16[1,1280]{1,0:T(2,128)(2,1)S(1)}, bf16[1,1280]{1,0:T(2,128)(2,1)}, u32[]{:S(2)}) copy-start(bf16[1,1280]{1,0:T(2,128)(2,1)} %first_bias.11) | copy-start | bytes 7684
  45.8 15.3 %collective-permute-start.8 = (bf16[64,1280]{1,0:T(8,128)(2,1)S(1)}, bf16[64,1280]{1,0:T(8,128)(2,1)S(1)}, u32[]{:S(2)}, u32[]{:S(2)}) collective-permute-start(bf16[64,1280]{1,0:T(8,128)(2,1)S(1)} %shard_map.118), channel_id=1, source_target_pairs={{0,8},{8,0},{16,24},{24,16},{1,9},{9,1},{17,25},{25,17},{2,10},{10... | collective-permute-start | bytes 491528 | tf_op jit(solution)/shard_map/ppermute | solution.py:180
  47.6 9.1 %collective-permute-start.4 = (bf16[64,1408]{1,0:T(8,128)(2,1)S(1)}, bf16[64,1408]{1,0:T(8,128)(2,1)S(1)}, u32[]{:S(2)}, u32[]{:S(2)}) collective-permute-start(bf16[64,1408]{1,0:T(8,128)(2,1)S(1)} %shard_map.115), channel_id=1, source_target_pairs={{0,8},{8,0},{16,24},{24,16},{1,9},{9,1},{17,25},{25,17},{2,10},{10... | collective-permute-start | bytes 540680 | tf_op jit(solution)/shard_map/ppermute | solution.py:180
  51.4 18.5 %collective-permute-start.1 = (bf16[128,1280]{1,0:T(8,128)(2,1)S(1)}, bf16[128,1280]{1,0:T(8,128)(2,1)S(1)}, u32[]{:S(2)}, u32[]{:S(2)}) collective-permute-start(bf16[128,1280]{1,0:T(8,128)(2,1)S(1)} %shard_map.114), channel_id=1, source_target_pairs={{0,8},{8,0},{16,24},{24,16},{1,9},{9,1},{17,25},{25,17},{2,10},{10... | collective-permute-start | bytes 983048 | tf_op jit(solution)/shard_map/ppermute | solution.py:180
  56.8 13.1 %collective-permute-start.5 = (bf16[64,1408]{1,0:T(8,128)(2,1)S(1)}, bf16[64,1408]{1,0:T(8,128)(2,1)S(1)}, u32[]{:S(2)}, u32[]{:S(2)}) collective-permute-start(bf16[64,1408]{1,0:T(8,128)(2,1)S(1)} %far_sum.2), channel_id=1, source_target_pairs={{0,24},{8,16},{16,8},{24,0},{1,25},{9,17},{17,9},{25,1},{2,26},{10... | collective-permute-start | bytes 540680 | tf_op jit(solution)/shard_map/ppermute | solution.py:180
  61.1 8.8 %copy-start.7 = (bf16[1,1280]{1,0:T(2,128)(2,1)S(1)}, bf16[1,1280]{1,0:T(2,128)(2,1)}, u32[]{:S(2)}) copy-start(bf16[1,1280]{1,0:T(2,128)(2,1)} %bias.1) | copy-start | bytes 7684
  61.2 19.3 %copy-start.9 = (s32[1,256]{1,0:T(1,128)S(1)}, s32[1,256]{1,0:T(1,128)}, u32[]{:S(2)}) copy-start(s32[1,256]{1,0:T(1,128)} %get-tuple-element.7.target) | copy-start | bytes 3076
  61.2 8.8 %collective-permute-start.9 = (bf16[64,1280]{1,0:T(8,128)(2,1)S(1)}, bf16[64,1280]{1,0:T(8,128)(2,1)S(1)}, u32[]{:S(2)}, u32[]{:S(2)}) collective-permute-start(bf16[64,1280]{1,0:T(8,128)(2,1)S(1)} %far_sum.3), channel_id=1, source_target_pairs={{0,24},{8,16},{16,8},{24,0},{1,25},{9,17},{17,9},{25,1},{2,26},{10... | collective-permute-start | bytes 491528 | tf_op jit(solution)/shard_map/ppermute | solution.py:180

commit v5 on v4

v5 whole, which is shorter than its diff:
```python
import functools

import jax
import jax.numpy as jnp
from jax import lax
from jax.experimental import pallas as pl
from jax.experimental.pallas import tpu as pltpu
from jax.sharding import PartitionSpec as P

CAP = 16
PARTS = 2
LANES = 128
AXES = ("dp", "expert")
VMEM = pl.BlockSpec(memory_space=pltpu.VMEM)
PARAMS = pltpu.CompilerParams(vmem_limit_bytes=24 << 20)


def one_hot(rows, target):
    row = lax.broadcasted_iota(jnp.int32, (rows, target.shape[1]), 0)
    return (row == target).astype(jnp.float32).astype(jnp.bfloat16)


def spread_stats(total, rows, period):
    row = lax.broadcasted_iota(jnp.int32, (rows, LANES), 0) % period
    out = jnp.zeros((rows, LANES), jnp.float32)
    for piece in range(3):
        rounded = total.astype(jnp.bfloat16).astype(jnp.float32)
        out = jnp.where(row == piece, rounded, out)
        total = total - rounded
    return out.astype(jnp.bfloat16)


def join_stats(block):
    return jnp.sum(block.astype(jnp.float32), axis=0, keepdims=True)


def dispatch_kernel(tokens, gain, choice, slot, normed_out, target_out, *slabs):
    values = tokens[...].astype(jnp.float32)
    center = values - jnp.mean(values, axis=-1, keepdims=True)
    spread = jnp.mean(center * center, axis=-1, keepdims=True)
    scaled = center * lax.rsqrt(spread + 1e-06) * gain[...].reshape(1, values.shape[1])
    normed = scaled.astype(jnp.bfloat16)
    normed_out[...] = normed
    distance = choice[...] ^ lax.axis_index("expert")
    target = jnp.where(slot[...] >= 0, distance * CAP + slot[...], -1)
    target_out[...] = target
    table = one_hot(len(slabs) * CAP, target)
    packed = jnp.dot(table, normed, preferred_element_type=jnp.float32).astype(jnp.bfloat16)
    for index, slab in enumerate(slabs):
        slab[...] = packed[index * CAP : (index + 1) * CAP]


def pack_kernel(*refs):
    slabs, out = refs[:-1], refs[-1]
    for index, slab in enumerate(slabs):
        out[index * CAP : (index + 1) * CAP] = slab[...]


def router_kernel(normed, router, choice, modality, first, second, gate_out, stats_out):
    logits = lax.dot_general(
        router[...], normed[...], (((1,), (1,)), ((), ())), preferred_element_type=jnp.float32
    )
    shifted = logits - jnp.max(logits, axis=0, keepdims=True)
    logp = shifted - jnp.log(jnp.sum(jnp.exp(shifted), axis=0, keepdims=True))
    probs = jnp.exp(logp)
    experts = probs.shape[0]
    expert = lax.broadcasted_iota(jnp.int32, probs.shape, 0)
    gate = jnp.sum(jnp.where(expert == choice[...], probs, 0.0), axis=0, keepdims=True)
    gate_out[...] = jnp.broadcast_to(gate, gate_out.shape)
    textual = (modality[...] == 1).astype(jnp.float32)
    entropy = -jnp.sum(probs * logp, axis=0, keepdims=True)
    lane = lax.broadcasted_iota(jnp.int32, (experts, LANES), 1)
    row = lax.broadcasted_iota(jnp.int32, (experts, LANES), 0)
    line = lane[0:1]
    stats = jnp.zeros((1, LANES), jnp.float32)
    for kind, select in enumerate((1.0 - textual, textual)):
        prob_sum = jnp.sum(probs * select, axis=1, keepdims=True)
        spread = jnp.where(lane == row + kind * experts, prob_sum, 0.0)
        stats = stats + jnp.sum(spread, axis=0, keepdims=True)
        ent_sum = jnp.sum(entropy * select, axis=1, keepdims=True)
        count = jnp.sum(select, axis=1, keepdims=True)
        stats = jnp.where(line == 2 * experts + kind, ent_sum, stats)
        stats = jnp.where(line == 2 * experts + 2 + kind, count, stats)
    stats_out[...] = jnp.broadcast_to(stats, stats_out.shape)


def expert_kernel(count, carry, *refs):
    parts, (first, first_bias, second), rest = refs[:count], refs[count : count + 3], refs[count + 3 :]
    out = rest[-1]
    rows = parts[0][...] if count == 1 else jnp.concatenate([part[...] for part in parts], axis=0)
    pre = lax.dot_general(
        rows, first[...], (((1,), (1,)), ((), ())), preferred_element_type=jnp.float32
    )
    pre = pre + first_bias[...].astype(jnp.float32)
    hidden = (0.5 * pre * (1.0 + lax.erf(pre * (0.5**0.5)))).astype(jnp.bfloat16)
    result = jnp.dot(hidden, second[...], preferred_element_type=jnp.float32)
    width = result.shape[1]
    out[:, :width] = result.astype(out.dtype)
    if carry:
        out[:, width:] = spread_stats(rest[0][0:1], out.shape[0], out.shape[0])


def far_kernel(index, carry, own, other, *refs):
    out = refs[-1]
    tall, width = out.shape[0], own.shape[1]
    mine = own[index * tall : (index + 1) * tall]
    out[:, :width] = (mine + other[:, :width].astype(jnp.float32)).astype(jnp.bfloat16)
    if carry:
        total = refs[0][0:1] + join_stats(refs[1][:, width:])
        out[:, width:] = spread_stats(total, tall, tall)


def near_kernel(index, far_count, own, other, bias, *refs):
    far, refs = refs[:far_count], refs[far_count:]
    tall, width = far[0].shape[0], own.shape[1]
    rows = slice(index * tall, (index + 1) * tall)
    result = own[rows] + other[rows].astype(jnp.float32) + bias[...].astype(jnp.float32)
    for block in far:
        result = result + block[:, :width].astype(jnp.float32)
    result = result.astype(jnp.bfloat16)
    if index == 0:
        stats, other_stats, extra_out = refs[:3]
        total = stats[0:1] + join_stats(other_stats[:, width:])
        for block in far:
            total = total + join_stats(block[:, width:])
        extra = spread_stats(total, CAP, CAP)
        extra_out[...] = extra
        slabs = refs[3:]
    else:
        extra = refs[0][...]
        slabs = refs[1:]
    for place, slab in enumerate(slabs):
        slab[:, :width] = result[place * CAP : (place + 1) * CAP]
        slab[:, width:] = extra


def combine_kernel(experts, target, gate, *refs):
    slabs, (out, aux) = refs[:-2], refs[-2:]
    width = out.shape[1]
    returned = jnp.concatenate([slab[...] for slab in slabs], axis=0)
    table = one_hot(returned.shape[0], target[...])
    fetched = lax.dot_general(
        table, returned[:, :width], (((0,), (0,)), ((), ())), preferred_element_type=jnp.float32
    )
    scale = jnp.transpose(gate[...])[:, 0:1]
    out[...] = (scale * fetched).astype(jnp.bfloat16)
    sums = join_stats(slabs[0][:, width:])
    have = {0: sums}
    for index in range(1, experts):
        have[index] = join_stats(slabs[index][:, width:])
    while len(have) > 1:
        have = {at // 2: have[at] + have[at + 1] for at in range(0, len(have), 2)}
    sums = have[0]
    lane = lax.broadcasted_iota(jnp.int32, sums.shape, 1)

    def pick(at):
        return jnp.sum(jnp.where(lane == at, sums, 0.0), axis=1, keepdims=True)

    row = lax.broadcasted_iota(jnp.int32, aux.shape, 0)
    column = lax.broadcasted_iota(jnp.int32, aux.shape, 1)
    result = jnp.zeros(aux.shape, jnp.float32)
    for kind in range(2):
        count = pick(2 * experts + 2 + kind)
        local = pick(2 * experts + kind) / count
        pbar = sums / count
        inside = (lane >= kind * experts) & (lane < (kind + 1) * experts)
        terms = jnp.where(inside, pbar * jnp.log(pbar), 0.0)
        spread = jnp.sum(terms, axis=1, keepdims=True)
        result = jnp.where((row == kind) & (column == 0), local, result)
        result = jnp.where((row == kind) & (column == 1), spread, result)
    aux[...] = result


def on_device(tokens, ln_gain, router, w_in, b_in, w_out, b_out, expert_choice, modality, slot):
    count, width = tokens.shape
    experts = router.shape[1]
    layers, senders = lax.axis_size("dp"), lax.axis_size("expert")
    assert w_in.shape[0] == 1 and experts == senders and layers % 4 == 0
    assert 2 * experts + 4 <= LANES
    hidden = w_in.shape[1]
    rows = experts * CAP
    tall = rows // PARTS
    full = width + LANES
    far_steps = [m ^ ((m >> 1) & 1) for m in range(2, layers, 2)]
    choice = expert_choice.reshape(1, count)
    normed, target, *slabs = pl.pallas_call(
        dispatch_kernel,
        out_shape=[
            jax.ShapeDtypeStruct((count, width), jnp.bfloat16),
            jax.ShapeDtypeStruct((1, count), jnp.int32),
        ]
        + [jax.ShapeDtypeStruct((CAP, width), jnp.bfloat16)] * experts,
        in_specs=[VMEM] * 4,
        out_specs=[VMEM] * (2 + experts),
        name="dispatch",
    )(tokens, ln_gain, choice, slot.reshape(1, count))

    def kernel(body, shapes, *operands, cost=None):
        many = isinstance(shapes, list)
        return pl.pallas_call(
            body,
            out_shape=shapes,
            in_specs=[VMEM] * len(operands),
            out_specs=[VMEM] * len(shapes) if many else VMEM,
            cost_estimate=cost,
            compiler_params=PARAMS,
        )(*operands)

    def bf16(*shape):
        return jax.ShapeDtypeStruct(shape, jnp.bfloat16)

    def f32(*shape):
        return jax.ShapeDtypeStruct(shape, jnp.float32)

    def hop(block, axis, step):
        size = lax.axis_size(axis)
        return lax.ppermute(block, axis, [(i, i ^ step) for i in range(size)])

    each = experts // PARTS
    homes, visitors, beside = [], {}, []
    slabs = [slabs[0]] + [hop(slabs[k], "expert", k) for k in range(1, experts)]
    for part in range(PARTS):
        home = kernel(pack_kernel, bf16(tall, width), *slabs[part * each : (part + 1) * each])
        homes.append(home)
        for step in far_steps:
            visitors[step, part] = hop(home, "dp", step)
        beside.append(hop(home, "dp", 1))
    first = pltpu.with_memory_space_constraint(w_in.reshape(hidden, width), pltpu.VMEM)
    second = pltpu.with_memory_space_constraint(w_out.reshape(hidden, width), pltpu.VMEM)
    gate, stats = kernel(
        router_kernel,
        [f32(8, count), f32(8, LANES)],
        normed,
        router.T,
        choice,
        modality.reshape(1, count),
        first,
        second,
    )

    def run_expert(parts, dtype, carry=False):
        size = sum(part.shape[0] for part in parts)
        return kernel(
            functools.partial(expert_kernel, len(parts), carry),
            jax.ShapeDtypeStruct((size, full if carry else width), dtype),
            *parts,
            first,
            b_in,
            second,
            *((stats,) if carry else ()),
            cost=pl.CostEstimate(
                flops=4 * size * width * hidden,
                bytes_accessed=4 * width * (hidden + size),
                transcendentals=size * hidden,
            ),
        )

    order = [(step, part) for part in range(PARTS) for step in far_steps]
    forwarded = {at: hop(visitors[at], "dp", 1) for at in order}
    answers = {}
    for at in order:
        theirs = run_expert([forwarded[at]], jnp.bfloat16, at[1] == 0)
        answers[at] = hop(theirs, "dp", 1)
    theirs = run_expert(beside, jnp.bfloat16)
    answer = hop(theirs, "dp", 1)
    owns = {}
    for step in far_steps:
        owns[step] = run_expert([visitors[step, part] for part in range(PARTS)], jnp.float32)
    returned = {}
    shared = answers[far_steps[0], 0]
    for step, part in order:
        carry = part == 0
        summed = kernel(
            functools.partial(far_kernel, part, carry),
            bf16(tall, full if carry else width),
            owns[step],
            answers[step, part],
            *((stats, shared) if carry else ()),
        )
        returned[step, part] = hop(summed, "dp", step)
    own = run_expert(homes, jnp.float32)
    back, extra = [], None
    for part in range(PARTS):
        far = [returned[step, part] for step in far_steps]
        shapes = [bf16(CAP, full)] * each
        body = functools.partial(near_kernel, part, len(far))
        if part == 0:
            out = kernel(body, [bf16(CAP, LANES)] + shapes, own, answer, b_out, *far, stats, shared)
            extra, out = out[0], out[1:]
        else:
            out = kernel(body, shapes, own, answer, b_out, *far, extra)
        for place, slab in enumerate(out):
            k = part * each + place
            back.append(hop(slab, "expert", k) if k else slab)
    return tuple(
        kernel(
            functools.partial(combine_kernel, experts),
            [bf16(count, width), f32(2, 2)],
            target,
            gate,
            *back,
        )
    )


def solution(mesh):
    return jax.shard_map(
        on_device,
        mesh=mesh,
        in_specs=(
            P(AXES, None),
            P(),
            P(),
            P("expert", "dp", None),
            P("expert", "dp"),
            P("expert", "dp", None),
            P("expert", None),
            P(AXES),
            P(AXES),
            P(AXES),
        ),
        out_specs=(P(AXES, None), P()),
        check_vma=False,
    )
```

time: 82.2 us -> 82.2 us (level)
  blocking collectives: 23.1 us -> 0 us
  waiting for transfers between devices: 13.5 us -> 32.7 us
  starting transfers between devices: 19.8 us -> 24.7 us
  Pallas kernels: 15.1 us -> 13.3 us
    all_to_all x2 -> x0, blocking collectives: 23.1 us -> none  [exchange(): lax.all_to_all(block.reshape(experts, CAP, block.shape[-1]), 'expert', sp...]
    ppermute x10 -> x25, waiting for transfers between devices: 13.5 us -> 32.7 us  [hop(): return lax.ppermute(block, axis, [(i, i ^ step) for i in range(size)])]
    ppermute x10 -> x25, starting transfers between devices: 19.8 us -> 24.7 us  [hop(): return lax.ppermute(block, axis, [(i, i ^ step) for i in range(size)])]
    pallas_call x11 -> x13, Pallas kernels: 12.5 us -> 10.8 us  [kernel(): pl.pallas_call(body, out_shape=shapes, in_specs=[VMEM] * len(operands), o...]
    unnamed x22 -> x24, local copies, waits for them, and re-layouts: 9.5 us -> 10.3 us
  transfers between devices with their start and end apart: 10 -> 25, of which waited for: 3 -> 10; matrix products, arithmetic and copies ran while one was open for 0% -> 0% of each run, Pallas kernels for 14% -> 12%
where the time goes in v5:
time: 82.2 us; the launch traced here: 81.8 us
  waiting for transfers between devices  32.7 us (40%)
  starting transfers between devices  24.7 us (30%)
  Pallas kernels  13.3 us (16%)
  local copies, waits for them, and re-layouts  10.3 us (13%)
    ppermute x25, waiting for transfers between devices, hop(): return lax.ppermute(block, axis, [(i, i ^ step) for i in range(size)])  32.7 us
    ppermute x25, starting transfers between devices, hop(): return lax.ppermute(block, axis, [(i, i ^ step) for i in range(size)])  24.7 us
    pallas_call x13, Pallas kernels, kernel(): pl.pallas_call(body, out_shape=shapes, in_specs=[VMEM] * len(operands), o...  10.8 us
    unnamed x24, local copies, waits for them, and re-layouts  10.3 us
    pallas_call x1, Pallas kernels, on_device(): pl.pallas_call(dispatch_kernel, out_shape=[jax.ShapeDtypeStruct((count, w...  2.51 us
  transfers between devices with their start and end apart: 25, of which 10 were waited for; matrix products, arithmetic and copies ran while one was open for 0% of the time, Pallas kernels for 12%

profile of v5, /device:TPU:0, one launch (start us, length us, event | category | flops | bytes accessed | tf_op | source)
XLA Modules:
  0.0 81.8 jit_solution(15826706408697446119)
XLA Ops:
  0.6 2.5 %dispatch.1 = (bf16[256,1280]{1,0:T(8,128)(2,1)}, s32[1,256]{1,0:T(1,128)}, bf16[16,1280]{1,0:T(8,128)(2,1)}, bf16[16,1280]{1,0:T(8,128)(2,1)}, bf16[16,1280]{1,...) custom-call(bf16[256,1280]{1,0:T(8,128)(2,1)} %tokens.1, ...), custom_call_target="tpu_custom_call" | custom-call | tf_op jit(solution)/shard_map/dispatch/pallas_call | solution.py:186
  3.7 2.6 %collective-permute-start.1 = (bf16[16,1280]{1,0:T(8,128)(2,1)}, bf16[16,1280]{1,0:T(8,128)(2,1)S(1)}, u32[]{:S(2)}, u32[]{:S(2)}) collective-permute-start(bf16[16,1280]{1,0:T(8,128)(2,1)} %get-tuple-element.28), channel_id=1, source_target_pairs={{0,2},{1,3},{2,0},{3,1},{4,6},{5,7},{6,4},{7,5},{8,10},{9,11},{10,... | collective-permute-start | bytes 122888 | tf_op jit(solution)/shard_map/ppermute | solution.py:217
  6.2 2.3 %collective-permute-done.1.refs_2_ = bf16[16,1280]{1,0:T(8,128)(2,1)S(1)} collective-permute-done((bf16[16,1280]{1,0:T(8,128)(2,1)}, bf16[16,1280]{1,0:T(8,128)(2,1)S(1)}, u32[]{:S(2)}, u32[]{:S(2)}) %collective-permute-start.1) | collective-permute-done | bytes 40992 | tf_op jit(solution)/shard_map/ppermute | solution.py:217
  8.6 1.4 %collective-permute-done.2.refs_3_ = bf16[16,1280]{1,0:T(8,128)(2,1)S(1)} collective-permute-done((bf16[16,1280]{1,0:T(8,128)(2,1)}, bf16[16,1280]{1,0:T(8,128)(2,1)S(1)}, u32[]{:S(2)}, u32[]{:S(2)}) %collective-permute-start.2) | collective-permute-done | bytes 40992 | tf_op jit(solution)/shard_map/ppermute | solution.py:217
  10.7 3.7 %collective-permute-start.10 = (bf16[64,1280]{1,0:T(8,128)(2,1)S(1)}, bf16[64,1280]{1,0:T(8,128)(2,1)S(1)}, u32[]{:S(2)}, u32[]{:S(2)}) collective-permute-start(bf16[64,1280]{1,0:T(8,128)(2,1)S(1)} %shard_map.114.refs_0_), channel_id=1, source_target_pairs={{0,24},{8,16},{16,8},{24,0},{1,25},{9,17},{17,9},{25,1},{2,26},{10... | collective-permute-start | bytes 491528 | tf_op jit(solution)/shard_map/ppermute | solution.py:217
  14.4 1.5 %collective-permute-start.3 = (bf16[16,1280]{1,0:T(8,128)(2,1)}, bf16[16,1280]{1,0:T(8,128)(2,1)S(1)}, u32[]{:S(2)}, u32[]{:S(2)}) collective-permute-start(bf16[16,1280]{1,0:T(8,128)(2,1)} %get-tuple-element.30), channel_id=1, source_target_pairs={{0,4},{1,5},{2,6},{3,7},{4,0},{5,1},{6,2},{7,3},{8,12},{9,13},{10,... | collective-permute-start | bytes 122888 | tf_op jit(solution)/shard_map/ppermute | solution.py:217
  15.9 1.6 %collective-permute-start.5 = (bf16[16,1280]{1,0:T(8,128)(2,1)}, bf16[16,1280]{1,0:T(8,128)(2,1)S(1)}, u32[]{:S(2)}, u32[]{:S(2)}) collective-permute-start(bf16[16,1280]{1,0:T(8,128)(2,1)} %get-tuple-element.32), channel_id=1, source_target_pairs={{0,6},{1,7},{2,4},{3,5},{4,2},{5,3},{6,0},{7,1},{8,14},{9,15},{10,... | collective-permute-start | bytes 122888 | tf_op jit(solution)/shard_map/ppermute | solution.py:217
  19.8 1.4 %collective-permute-done.5.refs_2_ = bf16[16,1280]{1,0:T(8,128)(2,1)S(1)} collective-permute-done((bf16[16,1280]{1,0:T(8,128)(2,1)}, bf16[16,1280]{1,0:T(8,128)(2,1)S(1)}, u32[]{:S(2)}, u32[]{:S(2)}) %collective-permute-start.5) | collective-permute-done | bytes 40992 | tf_op jit(solution)/shard_map/ppermute | solution.py:217
  22.6 2.0 %collective-permute-start.8 = (bf16[64,1280]{1,0:T(8,128)(2,1)S(1)}, bf16[64,1280]{1,0:T(8,128)(2,1)S(1)}, u32[]{:S(2)}, u32[]{:S(2)}) collective-permute-start(bf16[64,1280]{1,0:T(8,128)(2,1)S(1)} %shard_map.115.refs_1_), channel_id=1, source_target_pairs={{0,8},{8,0},{16,24},{24,16},{1,9},{9,1},{17,25},{25,17},{2,10},{10... | collective-permute-start | bytes 491528 | tf_op jit(solution)/shard_map/ppermute | solution.py:217
  24.6 6.5 %collective-permute-done.11.refs_1_ = bf16[64,1280]{1,0:T(8,128)(2,1)S(1)} collective-permute-done((bf16[64,1280]{1,0:T(8,128)(2,1)S(1)}, bf16[64,1280]{1,0:T(8,128)(2,1)S(1)}, u32[]{:S(2)}, u32[]{:S(2)}) %collective-permute-start.11) | collective-permute-done | bytes 163872 | tf_op jit(solution)/shard_map/ppermute | solution.py:217
  31.9 1.9 %copy-done = bf16[1,1280,1280]{2,1,0:T(8,128)(2,1)S(1)} copy-done((bf16[1,1280,1280]{2,1,0:T(8,128)(2,1)S(1)}, bf16[1,1280,1280]{2,1,0:T(8,128)(2,1)}, u32[]{:S(2)}) %copy-start) | copy-done | bytes 3276824
  33.8 1.9 %copy-done.2 = bf16[1,1280,1280]{2,1,0:T(8,128)(2,1)S(1)} copy-done((bf16[1,1280,1280]{2,1,0:T(8,128)(2,1)S(1)}, bf16[1,1280,1280]{2,1,0:T(8,128)(2,1)}, u32[]{:S(2)}) %copy-start.2) | copy-done | bytes 3276824
  39.4 1.5 %copy-done.1 = bf16[1,1280,1280]{2,1,0:T(8,128)(2,1)S(1)} copy-done((bf16[1,1280,1280]{2,1,0:T(8,128)(2,1)S(1)}, bf16[1,1280,1280]{2,1,0:T(8,128)(2,1)}, u32[]{:S(2)}) %copy-start.1) | copy-done | bytes 3276824
  41.8 1.8 %shard_map.119 = bf16[64,1408]{1,0:T(8,128)(2,1)S(1)} custom-call(bf16[64,1280]{1,0:T(8,128)(2,1)S(1)} %collective-permute-done.12.refs_0_, bf16[1280,1280]{1,0:T(8,128)(2,1)S(1)} %bitcast.7, bf16[1,1280]{1,0:T(2,128)(2,1)S(1)} %copy-done.5, bf16[1280,1280]{1,0:T(8,128)(2,1)S(1)} %bitcast.13, f32[8,128]{1,0:T(8,128)S(1)} %get-tuple-element.34.refs_4_.refs_0_.refs_1_), custom_call_target="tpu_custom_call" | custom-call | flops 419430400 | bytes 6881280 | tf_op jit(solution)/shard_map/pallas_call | solution.py:200
  44.9 1.8 %shard_map.117 = bf16[128,1280]{1,0:T(8,128)(2,1)S(1)} custom-call(bf16[64,1280]{1,0:T(8,128)(2,1)S(1)} %collective-permute-done.7.refs_0_, bf16[64,1280]{1,0:T(8,128)(2,1)S(1)} %collective-permute-done.8.refs_1_, bf16[1280,1280]{1,0:T(8,128)(2,1)S(1)} %bitcast.8, bf16[1,1280]{1,0:T(2,128)(2,1)S(1)} %copy-done.5, bf16[1280,1280]{1,0:T(8,128)(2,1)S(1)} %bitcast.14), custom_call_target="tpu_custom_call" | custom-call | flops 838860800 | bytes 7208960 | tf_op jit(solution)/shard_map/pallas_call | solution.py:200
  47.5 1.8 %shard_map.122 = bf16[64,1280]{1,0:T(8,128)(2,1)S(1)} custom-call(bf16[64,1280]{1,0:T(8,128)(2,1)S(1)} %collective-permute-done.18.refs_0_, bf16[1280,1280]{1,0:T(8,128)(2,1)S(1)} %bitcast.9, bf16[1,1280]{1,0:T(2,128)(2,1)S(1)} %copy-done.5, bf16[1280,1280]{1,0:T(8,128)(2,1)S(1)} %bitcast.15), custom_call_target="tpu_custom_call" | custom-call | flops 419430400 | bytes 6881280 | tf_op jit(solution)/shard_map/pallas_call | solution.py:200
  50.6 1.8 %shard_map.118.own = f32[128,1280]{1,0:T(8,128)S(1)} custom-call(bf16[64,1280]{1,0:T(8,128)(2,1)S(1)} %collective-permute-done.10.refs_0_, bf16[64,1280]{1,0:T(8,128)(2,1)S(1)} %collective-permute-done.11.refs_1_, bf16[1280,1280]{1,0:T(8,128)(2,1)S(1)} %bitcast.10, bf16[1,1280]{1,0:T(2,128)(2,1)S(1)} %copy-done.5, bf16[1280,1280]{1,0:T(8,128)(2,1)S(1)} %bitcast.16), custom_call_target="tpu_custom_call" | custom-call | flops 838860800 | bytes 7208960 | tf_op jit(solution)/shard_map/pallas_call | solution.py:200
  52.9 12.6 %collective-permute-done.19.other = bf16[64,1280]{1,0:T(8,128)(2,1)S(1)} collective-permute-done((bf16[64,1280]{1,0:T(8,128)(2,1)S(1)}, bf16[64,1280]{1,0:T(8,128)(2,1)S(1)}, u32[]{:S(2)}, u32[]{:S(2)}) %collective-permute-start.19) | collective-permute-done | bytes 163872 | tf_op jit(solution)/shard_map/ppermute | solution.py:217
  65.6 1.8 %shard_map.116.own = f32[128,1280]{1,0:T(8,128)S(1)} custom-call(bf16[64,1280]{1,0:T(8,128)(2,1)S(1)} %shard_map.114.refs_0_, bf16[64,1280]{1,0:T(8,128)(2,1)S(1)} %shard_map.115.refs_1_, bf16[1280,1280]{1,0:T(8,128)(2,1)S(1)} %bitcast.11, bf16[1,1280]{1,0:T(2,128)(2,1)S(1)} %copy-done.5, bf16[1280,1280]{1,0:T(8,128)(2,1)S(1)} %bitcast.17), custom_call_target="tpu_custom_call" | custom-call | flops 838860800 | bytes 7208960 | tf_op jit(solution)/shard_map/pallas_call | solution.py:200
  67.6 1.5 %collective-permute-start.16 = (bf16[16,1408]{1,0:T(8,128)(2,1)S(1)}, bf16[16,1408]{1,0:T(8,128)(2,1)S(1)}, u32[]{:S(2)}, u32[]{:S(2)}) collective-permute-start(bf16[16,1408]{1,0:T(8,128)(2,1)S(1)} %get-tuple-element.37), channel_id=1, source_target_pairs={{0,2},{1,3},{2,0},{3,1},{4,6},{5,7},{6,4},{7,5},{8,10},{9,11},{10,... | collective-permute-start | bytes 135176 | tf_op jit(solution)/shard_map/ppermute | solution.py:217
  69.4 3.3 %collective-permute-done.20.refs_0_ = bf16[64,1280]{1,0:T(8,128)(2,1)S(1)} collective-permute-done((bf16[64,1280]{1,0:T(8,128)(2,1)S(1)}, bf16[64,1280]{1,0:T(8,128)(2,1)S(1)}, u32[]{:S(2)}, u32[]{:S(2)}) %collective-permute-start.20) | collective-permute-done | bytes 163872 | tf_op jit(solution)/shard_map/ppermute | solution.py:217
  72.9 2.8 %collective-permute-start.23 = (bf16[16,1408]{1,0:T(8,128)(2,1)S(1)}, bf16[16,1408]{1,0:T(8,128)(2,1)S(1)}, u32[]{:S(2)}, u32[]{:S(2)}) collective-permute-start(bf16[16,1408]{1,0:T(8,128)(2,1)S(1)} %get-tuple-element.42), channel_id=1, source_target_pairs={{0,6},{1,7},{2,4},{3,5},{4,2},{5,3},{6,0},{7,1},{8,14},{9,15},{10,... | collective-permute-start | bytes 135176 | tf_op jit(solution)/shard_map/ppermute | solution.py:217
  75.8 1.5 %collective-permute-start.24 = (bf16[16,1408]{1,0:T(8,128)(2,1)S(1)}, bf16[16,1408]{1,0:T(8,128)(2,1)S(1)}, u32[]{:S(2)}, u32[]{:S(2)}) collective-permute-start(bf16[16,1408]{1,0:T(8,128)(2,1)S(1)} %get-tuple-element.43), channel_id=1, source_target_pairs={{0,7},{1,6},{2,5},{3,4},{4,3},{5,2},{6,1},{7,0},{8,15},{9,14},{10,... | collective-permute-start | bytes 135176 | tf_op jit(solution)/shard_map/ppermute | solution.py:217
  77.9 2.6 %collective-permute-done.24.refs_7_ = bf16[16,1408]{1,0:T(8,128)(2,1)S(1)} collective-permute-done((bf16[16,1408]{1,0:T(8,128)(2,1)S(1)}, bf16[16,1408]{1,0:T(8,128)(2,1)S(1)}, u32[]{:S(2)}, u32[]{:S(2)}) %collective-permute-start.24) | collective-permute-done | bytes 45088 | tf_op jit(solution)/shard_map/ppermute | solution.py:217
  (64 shorter events, 17.1 us)
Async XLA Ops:
  3.7 4.9 %collective-permute-start.1 = (bf16[16,1280]{1,0:T(8,128)(2,1)}, bf16[16,1280]{1,0:T(8,128)(2,1)S(1)}, u32[]{:S(2)}, u32[]{:S(2)}) collective-permute-start(bf16[16,1280]{1,0:T(8,128)(2,1)} %get-tuple-element.28), channel_id=1, source_target_pairs={{0,2},{1,3},{2,0},{3,1},{4,6},{5,7},{6,4},{7,5},{8,10},{9,11},{10,... | collective-permute-start | bytes 122888 | tf_op jit(solution)/shard_map/ppermute | solution.py:217
  6.2 3.7 %collective-permute-start.2 = (bf16[16,1280]{1,0:T(8,128)(2,1)}, bf16[16,1280]{1,0:T(8,128)(2,1)S(1)}, u32[]{:S(2)}, u32[]{:S(2)}) collective-permute-start(bf16[16,1280]{1,0:T(8,128)(2,1)} %get-tuple-element.29), channel_id=1, source_target_pairs={{0,3},{1,2},{2,1},{3,0},{4,7},{5,6},{6,5},{7,4},{8,11},{9,10},{10,... | collective-permute-start | bytes 122888 | tf_op jit(solution)/shard_map/ppermute | solution.py:217
  10.7 11.8 %collective-permute-start.10 = (bf16[64,1280]{1,0:T(8,128)(2,1)S(1)}, bf16[64,1280]{1,0:T(8,128)(2,1)S(1)}, u32[]{:S(2)}, u32[]{:S(2)}) collective-permute-start(bf16[64,1280]{1,0:T(8,128)(2,1)S(1)} %shard_map.114.refs_0_), channel_id=1, source_target_pairs={{0,24},{8,16},{16,8},{24,0},{1,25},{9,17},{17,9},{25,1},{2,26},{10... | collective-permute-start | bytes 491528 | tf_op jit(solution)/shard_map/ppermute | solution.py:217
  14.4 4.4 %collective-permute-start.3 = (bf16[16,1280]{1,0:T(8,128)(2,1)}, bf16[16,1280]{1,0:T(8,128)(2,1)S(1)}, u32[]{:S(2)}, u32[]{:S(2)}) collective-permute-start(bf16[16,1280]{1,0:T(8,128)(2,1)} %get-tuple-element.30), channel_id=1, source_target_pairs={{0,4},{1,5},{2,6},{3,7},{4,0},{5,1},{6,2},{7,3},{8,12},{9,13},{10,... | collective-permute-start | bytes 122888 | tf_op jit(solution)/shard_map/ppermute | solution.py:217
  15.9 3.9 %collective-permute-start.4 = (bf16[16,1280]{1,0:T(8,128)(2,1)}, bf16[16,1280]{1,0:T(8,128)(2,1)S(1)}, u32[]{:S(2)}, u32[]{:S(2)}) collective-permute-start(bf16[16,1280]{1,0:T(8,128)(2,1)} %get-tuple-element.31), channel_id=1, source_target_pairs={{0,5},{1,4},{2,7},{3,6},{4,1},{5,0},{6,3},{7,2},{8,13},{9,12},{10,... | collective-permute-start | bytes 122888 | tf_op jit(solution)/shard_map/ppermute | solution.py:217
  15.9 5.2 %collective-permute-start.5 = (bf16[16,1280]{1,0:T(8,128)(2,1)}, bf16[16,1280]{1,0:T(8,128)(2,1)S(1)}, u32[]{:S(2)}, u32[]{:S(2)}) collective-permute-start(bf16[16,1280]{1,0:T(8,128)(2,1)} %get-tuple-element.32), channel_id=1, source_target_pairs={{0,6},{1,7},{2,4},{3,5},{4,2},{5,3},{6,0},{7,1},{8,14},{9,15},{10,... | collective-permute-start | bytes 122888 | tf_op jit(solution)/shard_map/ppermute | solution.py:217
  17.6 4.5 %collective-permute-start.6 = (bf16[16,1280]{1,0:T(8,128)(2,1)}, bf16[16,1280]{1,0:T(8,128)(2,1)S(1)}, u32[]{:S(2)}, u32[]{:S(2)}) collective-permute-start(bf16[16,1280]{1,0:T(8,128)(2,1)} %get-tuple-element.33), channel_id=1, source_target_pairs={{0,7},{1,6},{2,5},{3,4},{4,3},{5,2},{6,1},{7,0},{8,15},{9,14},{10,... | collective-permute-start | bytes 122888 | tf_op jit(solution)/shard_map/ppermute | solution.py:217
  22.1 9.0 %collective-permute-start.11 = (bf16[64,1280]{1,0:T(8,128)(2,1)S(1)}, bf16[64,1280]{1,0:T(8,128)(2,1)S(1)}, u32[]{:S(2)}, u32[]{:S(2)}) collective-permute-start(bf16[64,1280]{1,0:T(8,128)(2,1)S(1)} %shard_map.115.refs_1_), channel_id=1, source_target_pairs={{0,24},{8,16},{16,8},{24,0},{1,25},{9,17},{17,9},{25,1},{2,26},{10... | collective-permute-start | bytes 491528 | tf_op jit(solution)/shard_map/ppermute | solution.py:217
  22.5 16.8 %collective-permute-start.12 = (bf16[64,1280]{1,0:T(8,128)(2,1)S(1)}, bf16[64,1280]{1,0:T(8,128)(2,1)S(1)}, u32[]{:S(2)}, u32[]{:S(2)}) collective-permute-start(bf16[64,1280]{1,0:T(8,128)(2,1)S(1)} %collective-permute-done.10.refs_0_), channel_id=1, source_target_pairs={{0,8},{8,0},{16,24},{24,16},{1,9},{9,1},{17,25},{25,17},{2,10},{10... | collective-permute-start | bytes 491528 | tf_op jit(solution)/shard_map/ppermute | solution.py:217
  22.6 22.4 %collective-permute-start.8 = (bf16[64,1280]{1,0:T(8,128)(2,1)S(1)}, bf16[64,1280]{1,0:T(8,128)(2,1)S(1)}, u32[]{:S(2)}, u32[]{:S(2)}) collective-permute-start(bf16[64,1280]{1,0:T(8,128)(2,1)S(1)} %shard_map.115.refs_1_), channel_id=1, source_target_pairs={{0,8},{8,0},{16,24},{24,16},{1,9},{9,1},{17,25},{25,17},{2,10},{10... | collective-permute-start | bytes 491528 | tf_op jit(solution)/shard_map/ppermute | solution.py:217
  24.6 20.3 %collective-permute-start.7 = (bf16[64,1280]{1,0:T(8,128)(2,1)S(1)}, bf16[64,1280]{1,0:T(8,128)(2,1)S(1)}, u32[]{:S(2)}, u32[]{:S(2)}) collective-permute-start(bf16[64,1280]{1,0:T(8,128)(2,1)S(1)} %shard_map.114.refs_0_), channel_id=1, source_target_pairs={{0,8},{8,0},{16,24},{24,16},{1,9},{9,1},{17,25},{25,17},{2,10},{10... | collective-permute-start | bytes 491528 | tf_op jit(solution)/shard_map/ppermute | solution.py:217
  31.1 16.4 %collective-permute-start.18 = (bf16[64,1280]{1,0:T(8,128)(2,1)S(1)}, bf16[64,1280]{1,0:T(8,128)(2,1)S(1)}, u32[]{:S(2)}, u32[]{:S(2)}) collective-permute-start(bf16[64,1280]{1,0:T(8,128)(2,1)S(1)} %collective-permute-done.11.refs_1_), channel_id=1, source_target_pairs={{0,8},{8,0},{16,24},{24,16},{1,9},{9,1},{17,25},{25,17},{2,10},{10... | collective-permute-start | bytes 491528 | tf_op jit(solution)/shard_map/ppermute | solution.py:217
  43.6 8.8 %collective-permute-start.13 = (bf16[64,1408]{1,0:T(8,128)(2,1)S(1)}, bf16[64,1408]{1,0:T(8,128)(2,1)S(1)}, u32[]{:S(2)}, u32[]{:S(2)}) collective-permute-start(bf16[64,1408]{1,0:T(8,128)(2,1)S(1)} %shard_map.119), channel_id=1, source_target_pairs={{0,8},{8,0},{16,24},{24,16},{1,9},{9,1},{17,25},{25,17},{2,10},{10... | collective-permute-start | bytes 540680 | tf_op jit(solution)/shard_map/ppermute | solution.py:217
  46.7 20.7 %collective-permute-start.9 = (bf16[128,1280]{1,0:T(8,128)(2,1)S(1)}, bf16[128,1280]{1,0:T(8,128)(2,1)S(1)}, u32[]{:S(2)}, u32[]{:S(2)}) collective-permute-start(bf16[128,1280]{1,0:T(8,128)(2,1)S(1)} %shard_map.117), channel_id=1, source_target_pairs={{0,8},{8,0},{16,24},{24,16},{1,9},{9,1},{17,25},{25,17},{2,10},{10... | collective-permute-start | bytes 983048 | tf_op jit(solution)/shard_map/ppermute | solution.py:217
  49.3 16.1 %collective-permute-start.19 = (bf16[64,1280]{1,0:T(8,128)(2,1)S(1)}, bf16[64,1280]{1,0:T(8,128)(2,1)S(1)}, u32[]{:S(2)}, u32[]{:S(2)}) collective-permute-start(bf16[64,1280]{1,0:T(8,128)(2,1)S(1)} %shard_map.122), channel_id=1, source_target_pairs={{0,8},{8,0},{16,24},{24,16},{1,9},{9,1},{17,25},{25,17},{2,10},{10... | collective-permute-start | bytes 491528 | tf_op jit(solution)/shard_map/ppermute | solution.py:217
  52.5 14.9 %collective-permute-start.14 = (bf16[64,1408]{1,0:T(8,128)(2,1)S(1)}, bf16[64,1408]{1,0:T(8,128)(2,1)S(1)}, u32[]{:S(2)}, u32[]{:S(2)}) collective-permute-start(bf16[64,1408]{1,0:T(8,128)(2,1)S(1)} %shard_map.120), channel_id=1, source_target_pairs={{0,24},{8,16},{16,8},{24,0},{1,25},{9,17},{17,9},{25,1},{2,26},{10... | collective-permute-start | bytes 540680 | tf_op jit(solution)/shard_map/ppermute | solution.py:217
  65.5 7.2 %collective-permute-start.20 = (bf16[64,1280]{1,0:T(8,128)(2,1)S(1)}, bf16[64,1280]{1,0:T(8,128)(2,1)S(1)}, u32[]{:S(2)}, u32[]{:S(2)}) collective-permute-start(bf16[64,1280]{1,0:T(8,128)(2,1)S(1)} %shard_map.123), channel_id=1, source_target_pairs={{0,24},{8,16},{16,8},{24,0},{1,25},{9,17},{17,9},{25,1},{2,26},{10... | collective-permute-start | bytes 491528 | tf_op jit(solution)/shard_map/ppermute | solution.py:217
  67.5 5.4 %collective-permute-start.15 = (bf16[16,1408]{1,0:T(8,128)(2,1)S(1)}, bf16[16,1408]{1,0:T(8,128)(2,1)S(1)}, u32[]{:S(2)}, u32[]{:S(2)}) collective-permute-start(bf16[16,1408]{1,0:T(8,128)(2,1)S(1)} %get-tuple-element.36), channel_id=1, source_target_pairs={{0,1},{1,0},{2,3},{3,2},{4,5},{5,4},{6,7},{7,6},{8,9},{9,8},{10,11... | collective-permute-start | bytes 135176 | tf_op jit(solution)/shard_map/ppermute | solution.py:217
  67.6 8.2 %collective-permute-start.16 = (bf16[16,1408]{1,0:T(8,128)(2,1)S(1)}, bf16[16,1408]{1,0:T(8,128)(2,1)S(1)}, u32[]{:S(2)}, u32[]{:S(2)}) collective-permute-start(bf16[16,1408]{1,0:T(8,128)(2,1)S(1)} %get-tuple-element.37), channel_id=1, source_target_pairs={{0,2},{1,3},{2,0},{3,1},{4,6},{5,7},{6,4},{7,5},{8,10},{9,11},{10,... | collective-permute-start | bytes 135176 | tf_op jit(solution)/shard_map/ppermute | solution.py:217
  69.1 8.2 %collective-permute-start.17 = (bf16[16,1408]{1,0:T(8,128)(2,1)S(1)}, bf16[16,1408]{1,0:T(8,128)(2,1)S(1)}, u32[]{:S(2)}, u32[]{:S(2)}) collective-permute-start(bf16[16,1408]{1,0:T(8,128)(2,1)S(1)} %get-tuple-element.38), channel_id=1, source_target_pairs={{0,3},{1,2},{2,1},{3,0},{4,7},{5,6},{6,5},{7,4},{8,11},{9,10},{10,... | collective-permute-start | bytes 135176 | tf_op jit(solution)/shard_map/ppermute | solution.py:217
  72.8 4.5 %collective-permute-start.21 = (bf16[16,1408]{1,0:T(8,128)(2,1)S(1)}, bf16[16,1408]{1,0:T(8,128)(2,1)S(1)}, u32[]{:S(2)}, u32[]{:S(2)}) collective-permute-start(bf16[16,1408]{1,0:T(8,128)(2,1)S(1)} %get-tuple-element.40), channel_id=1, source_target_pairs={{0,4},{1,5},{2,6},{3,7},{4,0},{5,1},{6,2},{7,3},{8,12},{9,13},{10,... | collective-permute-start | bytes 135176 | tf_op jit(solution)/shard_map/ppermute | solution.py:217
  72.8 4.4 %collective-permute-start.22 = (bf16[16,1408]{1,0:T(8,128)(2,1)S(1)}, bf16[16,1408]{1,0:T(8,128)(2,1)S(1)}, u32[]{:S(2)}, u32[]{:S(2)}) collective-permute-start(bf16[16,1408]{1,0:T(8,128)(2,1)S(1)} %get-tuple-element.41), channel_id=1, source_target_pairs={{0,5},{1,4},{2,7},{3,6},{4,1},{5,0},{6,3},{7,2},{8,13},{9,12},{10,... | collective-permute-start | bytes 135176 | tf_op jit(solution)/shard_map/ppermute | solution.py:217
  72.9 5.0 %collective-permute-start.23 = (bf16[16,1408]{1,0:T(8,128)(2,1)S(1)}, bf16[16,1408]{1,0:T(8,128)(2,1)S(1)}, u32[]{:S(2)}, u32[]{:S(2)}) collective-permute-start(bf16[16,1408]{1,0:T(8,128)(2,1)S(1)} %get-tuple-element.42), channel_id=1, source_target_pairs={{0,6},{1,7},{2,4},{3,5},{4,2},{5,3},{6,0},{7,1},{8,14},{9,15},{10,... | collective-permute-start | bytes 135176 | tf_op jit(solution)/shard_map/ppermute | solution.py:217
  75.8 4.8 %collective-permute-start.24 = (bf16[16,1408]{1,0:T(8,128)(2,1)S(1)}, bf16[16,1408]{1,0:T(8,128)(2,1)S(1)}, u32[]{:S(2)}, u32[]{:S(2)}) collective-permute-start(bf16[16,1408]{1,0:T(8,128)(2,1)S(1)} %get-tuple-element.43), channel_id=1, source_target_pairs={{0,7},{1,6},{2,5},{3,4},{4,3},{5,2},{6,1},{7,0},{8,15},{9,14},{10,... | collective-permute-start | bytes 135176 | tf_op jit(solution)/shard_map/ppermute | solution.py:217
  (13 other events, 35.6 us)

commit v6 on v5

--- a/solution.py
+++ b/solution.py
@@ -34,26 +34,28 @@
     return jnp.sum(block.astype(jnp.float32), axis=0, keepdims=True)
 
 
-def dispatch_kernel(tokens, gain, choice, slot, normed_out, target_out, *slabs):
+def dispatch_kernel(tokens, gain, choice, slot, normed_out, target_out, buffer):
     values = tokens[...].astype(jnp.float32)
     center = values - jnp.mean(values, axis=-1, keepdims=True)
     spread = jnp.mean(center * center, axis=-1, keepdims=True)
     scaled = center * lax.rsqrt(spread + 1e-06) * gain[...].reshape(1, values.shape[1])
     normed = scaled.astype(jnp.bfloat16)
     normed_out[...] = normed
-    distance = choice[...] ^ lax.axis_index("expert")
-    target = jnp.where(slot[...] >= 0, distance * CAP + slot[...], -1)
-    target_out[...] = target
-    table = one_hot(len(slabs) * CAP, target)
-    packed = jnp.dot(table, normed, preferred_element_type=jnp.float32).astype(jnp.bfloat16)
-    for index, slab in enumerate(slabs):
-        slab[...] = packed[index * CAP : (index + 1) * CAP]
-
-
-def pack_kernel(*refs):
-    slabs, out = refs[:-1], refs[-1]
-    for index, slab in enumerate(slabs):
-        out[index * CAP : (index + 1) * CAP] = slab[...]
+    kept = slot[...] >= 0
+    relative = choice[...] ^ lax.axis_index("expert")
+    target_out[...] = jnp.where(kept, relative * CAP + slot[...], -1)
+    table = one_hot(buffer.shape[0], jnp.where(kept, choice[...] * CAP + slot[...], -1))
+    buffer[...] = jnp.dot(table, normed, preferred_element_type=jnp.float32).astype(jnp.bfloat16)
+
+
+def pack_kernel(received, home, *parts):
+    me = lax.axis_index("expert")
+    each = parts[0].shape[0] // CAP
+    for k in range(home.shape[0] // CAP):
+        slab = received[pl.ds(pl.multiple_of((me ^ k) * CAP, CAP), CAP)]
+        home[k * CAP : (k + 1) * CAP] = slab
+        at = (k % each) * CAP
+        parts[k // each][at : at + CAP] = slab
 
 
 def router_kernel(normed, router, choice, modality, first, second, gate_out, stats_out):
@@ -176,22 +178,22 @@
     experts = router.shape[1]
     layers, senders = lax.axis_size("dp"), lax.axis_size("expert")
     assert w_in.shape[0] == 1 and experts == senders and layers % 4 == 0
-    assert 2 * experts + 4 <= LANES
+    assert 2 * experts + 4 <= LANES and experts & (experts - 1) == 0
     hidden = w_in.shape[1]
     rows = experts * CAP
     tall = rows // PARTS
     full = width + LANES
     far_steps = [m ^ ((m >> 1) & 1) for m in range(2, layers, 2)]
     choice = expert_choice.reshape(1, count)
-    normed, target, *slabs = pl.pallas_call(
+    normed, target, buffer = pl.pallas_call(
         dispatch_kernel,
         out_shape=[
             jax.ShapeDtypeStruct((count, width), jnp.bfloat16),
             jax.ShapeDtypeStruct((1, count), jnp.int32),
-        ]
-        + [jax.ShapeDtypeStruct((CAP, width), jnp.bfloat16)] * experts,
+            jax.ShapeDtypeStruct((rows, width), jnp.bfloat16),
+        ],
         in_specs=[VMEM] * 4,
-        out_specs=[VMEM] * (2 + experts),
+        out_specs=[VMEM] * 3,
         name="dispatch",
     )(tokens, ln_gain, choice, slot.reshape(1, count))
 
@@ -204,6 +206,7 @@
             out_specs=[VMEM] * len(shapes) if many else VMEM,
             cost_estimate=cost,
             compiler_params=PARAMS,
+            name="kernel",
         )(*operands)
 
     def bf16(*shape):
@@ -217,14 +220,16 @@
         return lax.ppermute(block, axis, [(i, i ^ step) for i in range(size)])
 
     each = experts // PARTS
-    homes, visitors, beside = [], {}, []
-    slabs = [slabs[0]] + [hop(slabs[k], "expert", k) for k in range(1, experts)]
-    for part in range(PARTS):
-        home = kernel(pack_kernel, bf16(tall, width), *slabs[part * each : (part + 1) * each])
-        homes.append(home)
-        for step in far_steps:
-            visitors[step, part] = hop(home, "dp", step)
-        beside.append(hop(home, "dp", 1))
+    received = lax.all_to_all(
+        buffer.reshape(experts, CAP, width), "expert", split_axis=0, concat_axis=0, tiled=True
+    ).reshape(rows, width)
+    home, *homes = kernel(pack_kernel, [bf16(rows, width)] + [bf16(tall, width)] * PARTS, received)
+    beside = hop(home, "dp", 1)
+    visitors = {
+        (step, part): hop(homes[part], "dp", step)
+        for part in range(PARTS)
+        for step in far_steps
+    }
     first = pltpu.with_memory_space_constraint(w_in.reshape(hidden, width), pltpu.VMEM)
     second = pltpu.with_memory_space_constraint(w_out.reshape(hidden, width), pltpu.VMEM)
     gate, stats = kernel(
@@ -261,7 +266,7 @@
     for at in order:
         theirs = run_expert([forwarded[at]], jnp.bfloat16, at[1] == 0)
         answers[at] = hop(theirs, "dp", 1)
-    theirs = run_expert(beside, jnp.bfloat16)
+    theirs = run_expert([beside], jnp.bfloat16)
     answer = hop(theirs, "dp", 1)
     owns = {}
     for step in far_steps:
@@ -278,7 +283,7 @@
             *((stats, shared) if carry else ()),
         )
         returned[step, part] = hop(summed, "dp", step)
-    own = run_expert(homes, jnp.float32)
+    own = run_expert([home], jnp.float32)
     back, extra = [], None
     for part in range(PARTS):
         far = [returned[step, part] for step in far_steps]

time: 82.2 us -> 84 us (1.022)
  waiting for transfers between devices: 32.7 us -> 19.4 us
  blocking collectives: 0 us -> 12.8 us
  starting transfers between devices: 24.7 us -> 27.7 us
    ppermute x25 -> x17, waiting for transfers between devices: 32.7 us -> 19.4 us  [hop(): return lax.ppermute(block, axis, [(i, i ^ step) for i in range(size)])]
    all_to_all x0 -> x1, blocking collectives: none -> 12.8 us  [on_device(): lax.all_to_all(buffer.reshape(experts, CAP, width), 'expert', split_axis=...]
    ppermute x25 -> x17, starting transfers between devices: 24.7 us -> 27.7 us  [hop(): return lax.ppermute(block, axis, [(i, i ^ step) for i in range(size)])]
    unnamed x24 -> x22, local copies, waits for them, and re-layouts: 10.3 us -> 9.51 us
    pallas_call x13 -> x12, Pallas kernels: 10.8 us -> 10.8 us  [kernel(): pl.pallas_call(body, out_shape=shapes, in_specs=[VMEM] * len(operands), o...]
  transfers between devices with their start and end apart: 25 -> 17, of which waited for: 10 -> 7; matrix products, arithmetic and copies ran while one was open for 0% -> 0% of each run, Pallas kernels for 12% -> 11%
where the time goes in v6:
time: 84 us; the launch traced here: 83.5 us
  starting transfers between devices  27.7 us (33%)
  waiting for transfers between devices  19.4 us (23%)
  Pallas kernels  13.3 us (16%)
  blocking collectives  12.8 us (15%)
  local copies, waits for them, and re-layouts  9.51 us (11%)
    ppermute x17, starting transfers between devices, hop(): return lax.ppermute(block, axis, [(i, i ^ step) for i in range(size)])  27.7 us
    ppermute x17, waiting for transfers between devices, hop(): return lax.ppermute(block, axis, [(i, i ^ step) for i in range(size)])  19.4 us
    all_to_all x1, blocking collectives, on_device(): lax.all_to_all(buffer.reshape(experts, CAP, width), 'expert', split_axis=...  12.8 us
    pallas_call x12, Pallas kernels, kernel(): pl.pallas_call(body, out_shape=shapes, in_specs=[VMEM] * len(operands), o...  10.8 us
    unnamed x22, local copies, waits for them, and re-layouts  9.51 us
    pallas_call x1, Pallas kernels, on_device(): pl.pallas_call(dispatch_kernel, out_shape=[jax.ShapeDtypeStruct((count, w...  2.53 us
  transfers between devices with their start and end apart: 17, of which 7 were waited for; matrix products, arithmetic and copies ran while one was open for 0% of the time, Pallas kernels for 11%

profile of v6, /device:TPU:0, one launch (start us, length us, event | category | flops | bytes accessed | tf_op | source)
XLA Modules:
  0.0 83.5 jit_solution(13455545966576539887)
XLA Ops:
  0.6 2.5 %dispatch.1 = (bf16[256,1280]{1,0:T(8,128)(2,1)}, s32[1,256]{1,0:T(1,128)}, bf16[128,1280]{1,0:T(8,128)(2,1)}) custom-call(bf16[256,1280]{1,0:T(8,128)(2,1)} %tokens.1, f32[1280]{0:T(1024)} %gain.1, s32[1,256]{1,0:T(1,128)} %bitcast.22, s32[1,256]{1,0:T(1,128)} %bitcast.26), custom_call_target="tpu_custom_call" | custom-call | tf_op jit(solution)/shard_map/dispatch/pallas_call | solution.py:188
  3.2 12.8 %all_to_all.5 = bf16[8,16,1280]{2,1,0:T(8,128)(2,1)S(1)} all-to-all(bf16[8,16,1280]{2,1,0:T(8,128)(2,1)} %bitcast.25), channel_id=1, replica_groups=mesh['dp'=4,'expert'=8] {'expert'}, dimensions={0} | all-to-all | bytes 655360 | tf_op jit(solution)/shard_map/all_to_all | solution.py:223
  16.0 3.7 %collective-permute-start.2 = (bf16[64,1280]{1,0:T(8,128)(2,1)S(1)}, bf16[64,1280]{1,0:T(8,128)(2,1)S(1)}, u32[]{:S(2)}, u32[]{:S(2)}) collective-permute-start(bf16[64,1280]{1,0:T(8,128)(2,1)S(1)} %get-tuple-element.24), channel_id=1, source_target_pairs={{0,24},{8,16},{16,8},{24,0},{1,25},{9,17},{17,9},{25,1},{2,26},{10... | collective-permute-start | bytes 491528 | tf_op jit(solution)/shard_map/ppermute | solution.py:220
  20.6 4.4 %collective-permute-done.2.refs_0_ = bf16[64,1280]{1,0:T(8,128)(2,1)S(1)} collective-permute-done((bf16[64,1280]{1,0:T(8,128)(2,1)S(1)}, bf16[64,1280]{1,0:T(8,128)(2,1)S(1)}, u32[]{:S(2)}, u32[]{:S(2)}) %collective-permute-start.2) | collective-permute-done | bytes 163872 | tf_op jit(solution)/shard_map/ppermute | solution.py:220
  24.9 3.0 %collective-permute-start.4 = (bf16[64,1280]{1,0:T(8,128)(2,1)S(1)}, bf16[64,1280]{1,0:T(8,128)(2,1)S(1)}, u32[]{:S(2)}, u32[]{:S(2)}) collective-permute-start(bf16[64,1280]{1,0:T(8,128)(2,1)S(1)} %collective-permute-done.2.refs_0_), channel_id=1, source_target_pairs={{0,8},{8,0},{16,24},{24,16},{1,9},{9,1},{17,25},{25,17},{2,10},{10... | collective-permute-start | bytes 491528 | tf_op jit(solution)/shard_map/ppermute | solution.py:220
  28.0 7.5 %collective-permute-done.3.refs_1_ = bf16[64,1280]{1,0:T(8,128)(2,1)S(1)} collective-permute-done((bf16[64,1280]{1,0:T(8,128)(2,1)S(1)}, bf16[64,1280]{1,0:T(8,128)(2,1)S(1)}, u32[]{:S(2)}, u32[]{:S(2)}) %collective-permute-start.3) | collective-permute-done | bytes 163872 | tf_op jit(solution)/shard_map/ppermute | solution.py:220
  35.5 1.9 %copy-done = bf16[1,1280,1280]{2,1,0:T(8,128)(2,1)S(1)} copy-done((bf16[1,1280,1280]{2,1,0:T(8,128)(2,1)S(1)}, bf16[1,1280,1280]{2,1,0:T(8,128)(2,1)}, u32[]{:S(2)}) %copy-start) | copy-done | bytes 3276824
  37.4 1.9 %copy-done.2 = bf16[1,1280,1280]{2,1,0:T(8,128)(2,1)S(1)} copy-done((bf16[1,1280,1280]{2,1,0:T(8,128)(2,1)S(1)}, bf16[1,1280,1280]{2,1,0:T(8,128)(2,1)}, u32[]{:S(2)}) %copy-start.2) | copy-done | bytes 3276824
  43.0 1.5 %copy-done.1 = bf16[1,1280,1280]{2,1,0:T(8,128)(2,1)S(1)} copy-done((bf16[1,1280,1280]{2,1,0:T(8,128)(2,1)S(1)}, bf16[1,1280,1280]{2,1,0:T(8,128)(2,1)}, u32[]{:S(2)}) %copy-start.1) | copy-done | bytes 3276824
  45.4 1.8 %kernel.17 = bf16[64,1408]{1,0:T(8,128)(2,1)S(1)} custom-call(bf16[64,1280]{1,0:T(8,128)(2,1)S(1)} %collective-permute-done.4.refs_0_, bf16[1280,1280]{1,0:T(8,128)(2,1)S(1)} %bitcast.9, bf16[1,1280]{1,0:T(2,128)(2,1)S(1)} %copy-done.5, bf16[1280,1280]{1,0:T(8,128)(2,1)S(1)} %bitcast.15, f32[8,128]{1,0:T(8,128)S(1)} %get-tuple-element.26.refs_4_.refs_0_.refs_1_), custom_call_target="tpu_custom_call" | custom-call | flops 419430400 | bytes 6881280 | tf_op jit(solution)/shard_map/kernel/pallas_call | solution.py:202
  47.2 2.1 %collective-permute-start.5 = (bf16[64,1408]{1,0:T(8,128)(2,1)S(1)}, bf16[64,1408]{1,0:T(8,128)(2,1)S(1)}, u32[]{:S(2)}, u32[]{:S(2)}) collective-permute-start(bf16[64,1408]{1,0:T(8,128)(2,1)S(1)} %kernel.17), channel_id=1, source_target_pairs={{0,8},{8,0},{16,24},{24,16},{1,9},{9,1},{17,25},{25,17},{2,10},{10... | collective-permute-start | bytes 540680 | tf_op jit(solution)/shard_map/ppermute | solution.py:220
  49.3 1.8 %kernel.15 = bf16[128,1280]{1,0:T(8,128)(2,1)S(1)} custom-call(bf16[128,1280]{1,0:T(8,128)(2,1)S(1)} %collective-permute-done.refs_0_, bf16[1280,1280]{1,0:T(8,128)(2,1)S(1)} %bitcast.10, bf16[1,1280]{1,0:T(2,128)(2,1)S(1)} %copy-done.5, bf16[1280,1280]{1,0:T(8,128)(2,1)S(1)} %bitcast.16), custom_call_target="tpu_custom_call" | custom-call | flops 838860800 | bytes 7208960 | tf_op jit(solution)/shard_map/kernel/pallas_call | solution.py:202
  51.1 1.8 %kernel.20 = bf16[64,1280]{1,0:T(8,128)(2,1)S(1)} custom-call(bf16[64,1280]{1,0:T(8,128)(2,1)S(1)} %collective-permute-done.10.refs_0_, bf16[1280,1280]{1,0:T(8,128)(2,1)S(1)} %bitcast.11, bf16[1,1280]{1,0:T(2,128)(2,1)S(1)} %copy-done.5, bf16[1280,1280]{1,0:T(8,128)(2,1)S(1)} %bitcast.17), custom_call_target="tpu_custom_call" | custom-call | flops 419430400 | bytes 6881280 | tf_op jit(solution)/shard_map/kernel/pallas_call | solution.py:202
  52.9 2.1 %collective-permute-start.11 = (bf16[64,1280]{1,0:T(8,128)(2,1)S(1)}, bf16[64,1280]{1,0:T(8,128)(2,1)S(1)}, u32[]{:S(2)}, u32[]{:S(2)}) collective-permute-start(bf16[64,1280]{1,0:T(8,128)(2,1)S(1)} %kernel.20), channel_id=1, source_target_pairs={{0,8},{8,0},{16,24},{24,16},{1,9},{9,1},{17,25},{25,17},{2,10},{10... | collective-permute-start | bytes 491528 | tf_op jit(solution)/shard_map/ppermute | solution.py:220
  55.0 1.8 %kernel.16.own = f32[128,1280]{1,0:T(8,128)S(1)} custom-call(bf16[64,1280]{1,0:T(8,128)(2,1)S(1)} %collective-permute-done.2.refs_0_, bf16[64,1280]{1,0:T(8,128)(2,1)S(1)} %collective-permute-done.3.refs_1_, bf16[1280,1280]{1,0:T(8,128)(2,1)S(1)} %bitcast.12, bf16[1,1280]{1,0:T(2,128)(2,1)S(1)} %copy-done.5, bf16[1280,1280]{1,0:T(8,128)(2,1)S(1)} %bitcast.18), custom_call_target="tpu_custom_call" | custom-call | flops 838860800 | bytes 7208960 | tf_op jit(solution)/shard_map/kernel/pallas_call | solution.py:202
  56.8 3.7 %collective-permute-start.6 = (bf16[64,1408]{1,0:T(8,128)(2,1)S(1)}, bf16[64,1408]{1,0:T(8,128)(2,1)S(1)}, u32[]{:S(2)}, u32[]{:S(2)}) collective-permute-start(bf16[64,1408]{1,0:T(8,128)(2,1)S(1)} %kernel.18), channel_id=1, source_target_pairs={{0,24},{8,16},{16,8},{24,0},{1,25},{9,17},{17,9},{25,1},{2,26},{10... | collective-permute-start | bytes 540680 | tf_op jit(solution)/shard_map/ppermute | solution.py:220
  60.5 4.2 %collective-permute-done.11.other = bf16[64,1280]{1,0:T(8,128)(2,1)S(1)} collective-permute-done((bf16[64,1280]{1,0:T(8,128)(2,1)S(1)}, bf16[64,1280]{1,0:T(8,128)(2,1)S(1)}, u32[]{:S(2)}, u32[]{:S(2)}) %collective-permute-start.11) | collective-permute-done | bytes 163872 | tf_op jit(solution)/shard_map/ppermute | solution.py:220
  64.7 6.1 %collective-permute-start.12 = (bf16[64,1280]{1,0:T(8,128)(2,1)S(1)}, bf16[64,1280]{1,0:T(8,128)(2,1)S(1)}, u32[]{:S(2)}, u32[]{:S(2)}) collective-permute-start(bf16[64,1280]{1,0:T(8,128)(2,1)S(1)} %kernel.21), channel_id=1, source_target_pairs={{0,24},{8,16},{16,8},{24,0},{1,25},{9,17},{17,9},{25,1},{2,26},{10... | collective-permute-start | bytes 491528 | tf_op jit(solution)/shard_map/ppermute | solution.py:220
  70.9 1.8 %kernel.14.own = f32[128,1280]{1,0:T(8,128)S(1)} custom-call(bf16[128,1280]{1,0:T(8,128)(2,1)S(1)} %get-tuple-element.23.refs_0_, bf16[1280,1280]{1,0:T(8,128)(2,1)S(1)} %bitcast.13, bf16[1,1280]{1,0:T(2,128)(2,1)S(1)} %copy-done.5, bf16[1280,1280]{1,0:T(8,128)(2,1)S(1)} %bitcast.19), custom_call_target="tpu_custom_call" | custom-call | flops 838860800 | bytes 7208960 | tf_op jit(solution)/shard_map/kernel/pallas_call | solution.py:202
  73.5 1.2 %collective-permute-start.9 = (bf16[16,1408]{1,0:T(8,128)(2,1)S(1)}, bf16[16,1408]{1,0:T(8,128)(2,1)S(1)}, u32[]{:S(2)}, u32[]{:S(2)}) collective-permute-start(bf16[16,1408]{1,0:T(8,128)(2,1)S(1)} %get-tuple-element.30), channel_id=1, source_target_pairs={{0,3},{1,2},{2,1},{3,0},{4,7},{5,6},{6,5},{7,4},{8,11},{9,10},{10,... | collective-permute-start | bytes 135176 | tf_op jit(solution)/shard_map/ppermute | solution.py:220
  75.4 1.1 %collective-permute-start.14 = (bf16[16,1408]{1,0:T(8,128)(2,1)S(1)}, bf16[16,1408]{1,0:T(8,128)(2,1)S(1)}, u32[]{:S(2)}, u32[]{:S(2)}) collective-permute-start(bf16[16,1408]{1,0:T(8,128)(2,1)S(1)} %get-tuple-element.33), channel_id=1, source_target_pairs={{0,5},{1,4},{2,7},{3,6},{4,1},{5,0},{6,3},{7,2},{8,13},{9,12},{10,... | collective-permute-start | bytes 135176 | tf_op jit(solution)/shard_map/ppermute | solution.py:220
  77.4 1.8 %collective-permute-start.16 = (bf16[16,1408]{1,0:T(8,128)(2,1)S(1)}, bf16[16,1408]{1,0:T(8,128)(2,1)S(1)}, u32[]{:S(2)}, u32[]{:S(2)}) collective-permute-start(bf16[16,1408]{1,0:T(8,128)(2,1)S(1)} %get-tuple-element.35), channel_id=1, source_target_pairs={{0,7},{1,6},{2,5},{3,4},{4,3},{5,2},{6,1},{7,0},{8,15},{9,14},{10,... | collective-permute-start | bytes 135176 | tf_op jit(solution)/shard_map/ppermute | solution.py:220
  79.4 2.3 %collective-permute-done.15.refs_6_ = bf16[16,1408]{1,0:T(8,128)(2,1)S(1)} collective-permute-done((bf16[16,1408]{1,0:T(8,128)(2,1)S(1)}, bf16[16,1408]{1,0:T(8,128)(2,1)S(1)}, u32[]{:S(2)}, u32[]{:S(2)}) %collective-permute-start.15) | collective-permute-done | bytes 45088 | tf_op jit(solution)/shard_map/ppermute | solution.py:220
  82.3 1.2 %kernel.23 = (bf16[256,1280]{1,0:T(8,128)(2,1)}, f32[2,2]{1,0:T(2,128)}) custom-call(s32[1,256]{1,0:T(1,128)S(1)} %copy-done.9, f32[8,256]{1,0:T(8,128)S(1)} %get-tuple-element.21.gate, bf16[16,1408]{1,0:T(8,128)(2,1)S(1)} %get-tuple-element.27.refs_0_, bf16[16,1408]{1,0:T(8,128)(2,1)S(1)} %collective-permute-done.7.refs_1_, ...), custom_call_target="tpu_custom_call" | custom-call | tf_op jit(solution)/shard_map/kernel/pallas_call | solution.py:202
  (46 shorter events, 8.9 us)
Async XLA Ops:
  16.0 8.9 %collective-permute-start.2 = (bf16[64,1280]{1,0:T(8,128)(2,1)S(1)}, bf16[64,1280]{1,0:T(8,128)(2,1)S(1)}, u32[]{:S(2)}, u32[]{:S(2)}) collective-permute-start(bf16[64,1280]{1,0:T(8,128)(2,1)S(1)} %get-tuple-element.24), channel_id=1, source_target_pairs={{0,24},{8,16},{16,8},{24,0},{1,25},{9,17},{17,9},{25,1},{2,26},{10... | collective-permute-start | bytes 491528 | tf_op jit(solution)/shard_map/ppermute | solution.py:220
  19.7 29.6 %collective-permute-start = (bf16[128,1280]{1,0:T(8,128)(2,1)S(1)}, bf16[128,1280]{1,0:T(8,128)(2,1)S(1)}, u32[]{:S(2)}, u32[]{:S(2)}) collective-permute-start(bf16[128,1280]{1,0:T(8,128)(2,1)S(1)} %get-tuple-element.23.refs_0_), channel_id=1, source_target_pairs={{0,8},{8,0},{16,24},{24,16},{1,9},{9,1},{17,25},{25,17},{2,10},{10... | collective-permute-start | bytes 983048 | tf_op jit(solution)/shard_map/ppermute | solution.py:220
  19.7 15.8 %collective-permute-start.3 = (bf16[64,1280]{1,0:T(8,128)(2,1)S(1)}, bf16[64,1280]{1,0:T(8,128)(2,1)S(1)}, u32[]{:S(2)}, u32[]{:S(2)}) collective-permute-start(bf16[64,1280]{1,0:T(8,128)(2,1)S(1)} %get-tuple-element.25), channel_id=1, source_target_pairs={{0,24},{8,16},{16,8},{24,0},{1,25},{9,17},{17,9},{25,1},{2,26},{10... | collective-permute-start | bytes 491528 | tf_op jit(solution)/shard_map/ppermute | solution.py:220
  24.9 18.0 %collective-permute-start.4 = (bf16[64,1280]{1,0:T(8,128)(2,1)S(1)}, bf16[64,1280]{1,0:T(8,128)(2,1)S(1)}, u32[]{:S(2)}, u32[]{:S(2)}) collective-permute-start(bf16[64,1280]{1,0:T(8,128)(2,1)S(1)} %collective-permute-done.2.refs_0_), channel_id=1, source_target_pairs={{0,8},{8,0},{16,24},{24,16},{1,9},{9,1},{17,25},{25,17},{2,10},{10... | collective-permute-start | bytes 491528 | tf_op jit(solution)/shard_map/ppermute | solution.py:220
  35.5 15.7 %collective-permute-start.10 = (bf16[64,1280]{1,0:T(8,128)(2,1)S(1)}, bf16[64,1280]{1,0:T(8,128)(2,1)S(1)}, u32[]{:S(2)}, u32[]{:S(2)}) collective-permute-start(bf16[64,1280]{1,0:T(8,128)(2,1)S(1)} %collective-permute-done.3.refs_1_), channel_id=1, source_target_pairs={{0,8},{8,0},{16,24},{24,16},{1,9},{9,1},{17,25},{25,17},{2,10},{10... | collective-permute-start | bytes 491528 | tf_op jit(solution)/shard_map/ppermute | solution.py:220
  35.5 1.9 %copy-start = (bf16[1,1280,1280]{2,1,0:T(8,128)(2,1)S(1)}, bf16[1,1280,1280]{2,1,0:T(8,128)(2,1)}, u32[]{:S(2)}) copy-start(bf16[1,1280,1280]{2,1,0:T(8,128)(2,1)} %param.13) | copy-start | bytes 9830404
  37.4 1.9 %copy-start.2 = (bf16[1,1280,1280]{2,1,0:T(8,128)(2,1)S(1)}, bf16[1,1280,1280]{2,1,0:T(8,128)(2,1)}, u32[]{:S(2)}) copy-start(bf16[1,1280,1280]{2,1,0:T(8,128)(2,1)} %param.15) | copy-start | bytes 9830404
  42.5 1.9 %copy-start.1 = (bf16[1,1280,1280]{2,1,0:T(8,128)(2,1)S(1)}, bf16[1,1280,1280]{2,1,0:T(8,128)(2,1)}, u32[]{:S(2)}) copy-start(bf16[1,1280,1280]{2,1,0:T(8,128)(2,1)} %param.13) | copy-start | bytes 9830404
  42.5 2.9 %copy-start.3 = (bf16[1,1280,1280]{2,1,0:T(8,128)(2,1)S(1)}, bf16[1,1280,1280]{2,1,0:T(8,128)(2,1)}, u32[]{:S(2)}) copy-start(bf16[1,1280,1280]{2,1,0:T(8,128)(2,1)} %param.15) | copy-start | bytes 9830404
  42.5 2.9 %copy-start.5 = (bf16[1,1280]{1,0:T(2,128)(2,1)S(1)}, bf16[1,1280]{1,0:T(2,128)(2,1)}, u32[]{:S(2)}) copy-start(bf16[1,1280]{1,0:T(2,128)(2,1)} %refs_2_.7) | copy-start | bytes 7684
  47.2 9.5 %collective-permute-start.5 = (bf16[64,1408]{1,0:T(8,128)(2,1)S(1)}, bf16[64,1408]{1,0:T(8,128)(2,1)S(1)}, u32[]{:S(2)}, u32[]{:S(2)}) collective-permute-start(bf16[64,1408]{1,0:T(8,128)(2,1)S(1)} %kernel.17), channel_id=1, source_target_pairs={{0,8},{8,0},{16,24},{24,16},{1,9},{9,1},{17,25},{25,17},{2,10},{10... | collective-permute-start | bytes 540680 | tf_op jit(solution)/shard_map/ppermute | solution.py:220
  51.1 21.6 %collective-permute-start.1 = (bf16[128,1280]{1,0:T(8,128)(2,1)S(1)}, bf16[128,1280]{1,0:T(8,128)(2,1)S(1)}, u32[]{:S(2)}, u32[]{:S(2)}) collective-permute-start(bf16[128,1280]{1,0:T(8,128)(2,1)S(1)} %kernel.15), channel_id=1, source_target_pairs={{0,8},{8,0},{16,24},{24,16},{1,9},{9,1},{17,25},{25,17},{2,10},{10... | collective-permute-start | bytes 983048 | tf_op jit(solution)/shard_map/ppermute | solution.py:220
  52.9 11.8 %collective-permute-start.11 = (bf16[64,1280]{1,0:T(8,128)(2,1)S(1)}, bf16[64,1280]{1,0:T(8,128)(2,1)S(1)}, u32[]{:S(2)}, u32[]{:S(2)}) collective-permute-start(bf16[64,1280]{1,0:T(8,128)(2,1)S(1)} %kernel.20), channel_id=1, source_target_pairs={{0,8},{8,0},{16,24},{24,16},{1,9},{9,1},{17,25},{25,17},{2,10},{10... | collective-permute-start | bytes 491528 | tf_op jit(solution)/shard_map/ppermute | solution.py:220
  56.8 15.8 %collective-permute-start.6 = (bf16[64,1408]{1,0:T(8,128)(2,1)S(1)}, bf16[64,1408]{1,0:T(8,128)(2,1)S(1)}, u32[]{:S(2)}, u32[]{:S(2)}) collective-permute-start(bf16[64,1408]{1,0:T(8,128)(2,1)S(1)} %kernel.18), channel_id=1, source_target_pairs={{0,24},{8,16},{16,8},{24,0},{1,25},{9,17},{17,9},{25,1},{2,26},{10... | collective-permute-start | bytes 540680 | tf_op jit(solution)/shard_map/ppermute | solution.py:220
  64.7 8.0 %copy-start.7 = (bf16[1,1280]{1,0:T(2,128)(2,1)S(1)}, bf16[1,1280]{1,0:T(2,128)(2,1)}, u32[]{:S(2)}) copy-start(bf16[1,1280]{1,0:T(2,128)(2,1)} %bias.3) | copy-start | bytes 7684
  64.7 17.6 %copy-start.9 = (s32[1,256]{1,0:T(1,128)S(1)}, s32[1,256]{1,0:T(1,128)}, u32[]{:S(2)}) copy-start(s32[1,256]{1,0:T(1,128)} %get-tuple-element.19.target) | copy-start | bytes 3076
  64.7 10.0 %collective-permute-start.12 = (bf16[64,1280]{1,0:T(8,128)(2,1)S(1)}, bf16[64,1280]{1,0:T(8,128)(2,1)S(1)}, u32[]{:S(2)}, u32[]{:S(2)}) collective-permute-start(bf16[64,1280]{1,0:T(8,128)(2,1)S(1)} %kernel.21), channel_id=1, source_target_pairs={{0,24},{8,16},{16,8},{24,0},{1,25},{9,17},{17,9},{25,1},{2,26},{10... | collective-permute-start | bytes 491528 | tf_op jit(solution)/shard_map/ppermute | solution.py:220
  72.8 3.8 %collective-permute-start.7 = (bf16[16,1408]{1,0:T(8,128)(2,1)S(1)}, bf16[16,1408]{1,0:T(8,128)(2,1)S(1)}, u32[]{:S(2)}, u32[]{:S(2)}) collective-permute-start(bf16[16,1408]{1,0:T(8,128)(2,1)S(1)} %get-tuple-element.28), channel_id=1, source_target_pairs={{0,1},{1,0},{2,3},{3,2},{4,5},{5,4},{6,7},{7,6},{8,9},{9,8},{10,11... | collective-permute-start | bytes 135176 | tf_op jit(solution)/shard_map/ppermute | solution.py:220
  72.9 4.6 %collective-permute-start.8 = (bf16[16,1408]{1,0:T(8,128)(2,1)S(1)}, bf16[16,1408]{1,0:T(8,128)(2,1)S(1)}, u32[]{:S(2)}, u32[]{:S(2)}) collective-permute-start(bf16[16,1408]{1,0:T(8,128)(2,1)S(1)} %get-tuple-element.29), channel_id=1, source_target_pairs={{0,2},{1,3},{2,0},{3,1},{4,6},{5,7},{6,4},{7,5},{8,10},{9,11},{10,... | collective-permute-start | bytes 135176 | tf_op jit(solution)/shard_map/ppermute | solution.py:220
  73.5 5.8 %collective-permute-start.9 = (bf16[16,1408]{1,0:T(8,128)(2,1)S(1)}, bf16[16,1408]{1,0:T(8,128)(2,1)S(1)}, u32[]{:S(2)}, u32[]{:S(2)}) collective-permute-start(bf16[16,1408]{1,0:T(8,128)(2,1)S(1)} %get-tuple-element.30), channel_id=1, source_target_pairs={{0,3},{1,2},{2,1},{3,0},{4,7},{5,6},{6,5},{7,4},{8,11},{9,10},{10,... | collective-permute-start | bytes 135176 | tf_op jit(solution)/shard_map/ppermute | solution.py:220
  74.8 4.6 %collective-permute-start.13 = (bf16[16,1408]{1,0:T(8,128)(2,1)S(1)}, bf16[16,1408]{1,0:T(8,128)(2,1)S(1)}, u32[]{:S(2)}, u32[]{:S(2)}) collective-permute-start(bf16[16,1408]{1,0:T(8,128)(2,1)S(1)} %get-tuple-element.32), channel_id=1, source_target_pairs={{0,4},{1,5},{2,6},{3,7},{4,0},{5,1},{6,2},{7,3},{8,12},{9,13},{10,... | collective-permute-start | bytes 135176 | tf_op jit(solution)/shard_map/ppermute | solution.py:220
  75.4 4.0 %collective-permute-start.14 = (bf16[16,1408]{1,0:T(8,128)(2,1)S(1)}, bf16[16,1408]{1,0:T(8,128)(2,1)S(1)}, u32[]{:S(2)}, u32[]{:S(2)}) collective-permute-start(bf16[16,1408]{1,0:T(8,128)(2,1)S(1)} %get-tuple-element.33), channel_id=1, source_target_pairs={{0,5},{1,4},{2,7},{3,6},{4,1},{5,0},{6,3},{7,2},{8,13},{9,12},{10,... | collective-permute-start | bytes 135176 | tf_op jit(solution)/shard_map/ppermute | solution.py:220
  76.6 5.1 %collective-permute-start.15 = (bf16[16,1408]{1,0:T(8,128)(2,1)S(1)}, bf16[16,1408]{1,0:T(8,128)(2,1)S(1)}, u32[]{:S(2)}, u32[]{:S(2)}) collective-permute-start(bf16[16,1408]{1,0:T(8,128)(2,1)S(1)} %get-tuple-element.34), channel_id=1, source_target_pairs={{0,6},{1,7},{2,4},{3,5},{4,2},{5,3},{6,0},{7,1},{8,14},{9,15},{10,... | collective-permute-start | bytes 135176 | tf_op jit(solution)/shard_map/ppermute | solution.py:220
  77.4 4.8 %collective-permute-start.16 = (bf16[16,1408]{1,0:T(8,128)(2,1)S(1)}, bf16[16,1408]{1,0:T(8,128)(2,1)S(1)}, u32[]{:S(2)}, u32[]{:S(2)}) collective-permute-start(bf16[16,1408]{1,0:T(8,128)(2,1)S(1)} %get-tuple-element.35), channel_id=1, source_target_pairs={{0,7},{1,6},{2,5},{3,4},{4,3},{5,2},{6,1},{7,0},{8,15},{9,14},{10,... | collective-permute-start | bytes 135176 | tf_op jit(solution)/shard_map/ppermute | solution.py:220
  (4 other events, 3.2 us)

commit v7 on v6

--- a/solution.py
+++ b/solution.py
@@ -48,17 +48,29 @@
     buffer[...] = jnp.dot(table, normed, preferred_element_type=jnp.float32).astype(jnp.bfloat16)
 
 
-def pack_kernel(received, home, *parts):
+def pack_kernel(received, *parts):
     me = lax.axis_index("expert")
     each = parts[0].shape[0] // CAP
-    for k in range(home.shape[0] // CAP):
+    for k in range(received.shape[0] // CAP):
         slab = received[pl.ds(pl.multiple_of((me ^ k) * CAP, CAP), CAP)]
-        home[k * CAP : (k + 1) * CAP] = slab
         at = (k % each) * CAP
         parts[k // each][at : at + CAP] = slab
 
 
-def router_kernel(normed, router, choice, modality, first, second, gate_out, stats_out):
+def hold_kernel(w_in, w_out, first, second, sems):
+    copies = []
+    for source, target in ((w_in, first), (w_out, second)):
+        size = target.shape[0] // 2
+        for at in (0, size):
+            rows = pl.ds(at, size)
+            copies.append(pltpu.make_async_copy(source.at[rows], target.at[rows], sems.at[len(copies)]))
+    for copy in copies:
+        copy.start()
+    for copy in copies:
+        copy.wait()
+
+
+def router_kernel(normed, router, choice, modality, gate_out, stats_out):
     logits = lax.dot_general(
         router[...], normed[...], (((1,), (1,)), ((), ())), preferred_element_type=jnp.float32
     )
@@ -197,7 +209,7 @@
         name="dispatch",
     )(tokens, ln_gain, choice, slot.reshape(1, count))
 
-    def kernel(body, shapes, *operands, cost=None):
+    def kernel(body, shapes, *operands, cost=None, params=PARAMS):
         many = isinstance(shapes, list)
         return pl.pallas_call(
             body,
@@ -205,7 +217,7 @@
             in_specs=[VMEM] * len(operands),
             out_specs=[VMEM] * len(shapes) if many else VMEM,
             cost_estimate=cost,
-            compiler_params=PARAMS,
+            compiler_params=params,
             name="kernel",
         )(*operands)
 
@@ -223,15 +235,13 @@
     received = lax.all_to_all(
         buffer.reshape(experts, CAP, width), "expert", split_axis=0, concat_axis=0, tiled=True
     ).reshape(rows, width)
-    home, *homes = kernel(pack_kernel, [bf16(rows, width)] + [bf16(tall, width)] * PARTS, received)
-    beside = hop(home, "dp", 1)
+    homes = kernel(pack_kernel, [bf16(tall, width)] * PARTS, received)
+    beside = [hop(homes[part], "dp", 1) for part in range(PARTS)]
     visitors = {
         (step, part): hop(homes[part], "dp", step)
         for part in range(PARTS)
         for step in far_steps
     }
-    first = pltpu.with_memory_space_constraint(w_in.reshape(hidden, width), pltpu.VMEM)
-    second = pltpu.with_memory_space_constraint(w_out.reshape(hidden, width), pltpu.VMEM)
     gate, stats = kernel(
         router_kernel,
         [f32(8, count), f32(8, LANES)],
@@ -239,9 +249,20 @@
         router.T,
         choice,
         modality.reshape(1, count),
-        first,
-        second,
-    )
+        params=None,
+    )
+    hold = pl.pallas_call(
+        hold_kernel,
+        out_shape=[pltpu.VMEM((hidden, width), jnp.bfloat16)] * 2,
+        in_specs=[pl.BlockSpec(memory_space=pl.ANY)] * 2,
+        out_specs=[VMEM] * 2,
+        scratch_shapes=[pltpu.SemaphoreType.DMA((4,))],
+        compiler_params=pltpu.CompilerParams(vmem_limit_bytes=56 << 20),
+        name="kernel",
+    )
+    first, second = hold(w_in.reshape(hidden, width), w_out.reshape(hidden, width))
+    first = pltpu.with_memory_space_constraint(first, pltpu.VMEM)
+    second = pltpu.with_memory_space_constraint(second, pltpu.VMEM)
 
     def run_expert(parts, dtype, carry=False):
         size = sum(part.shape[0] for part in parts)
@@ -266,7 +287,7 @@
     for at in order:
         theirs = run_expert([forwarded[at]], jnp.bfloat16, at[1] == 0)
         answers[at] = hop(theirs, "dp", 1)
-    theirs = run_expert([beside], jnp.bfloat16)
+    theirs = run_expert(beside, jnp.bfloat16)
     answer = hop(theirs, "dp", 1)
     owns = {}
     for step in far_steps:
@@ -283,7 +304,7 @@
             *((stats, shared) if carry else ()),
         )
         returned[step, part] = hop(summed, "dp", step)
-    own = run_expert([home], jnp.float32)
+    own = run_expert(homes, jnp.float32)
     back, extra = [], None
     for part in range(PARTS):
         far = [returned[step, part] for step in far_steps]

time: 84 us -> 82.2 us (0.979)
  Pallas kernels: 13.3 us -> 22.8 us
  waiting for transfers between devices: 19.4 us -> 12.2 us
  local copies, waits for them, and re-layouts: 9.51 us -> 4.29 us
  starting transfers between devices: 27.7 us -> 28.9 us
    ppermute x17 -> x18, waiting for transfers between devices: 19.4 us -> 12.2 us  [hop(): return lax.ppermute(block, axis, [(i, i ^ step) for i in range(size)])]
    pallas_call x12, Pallas kernels: 10.8 us -> 17.3 us  [kernel(): pl.pallas_call(body, out_shape=shapes, in_specs=[VMEM] * len(operands), o...]
    unnamed x22 -> x18, local copies, waits for them, and re-layouts: 9.51 us -> 4.29 us
    pallas_call x0 -> x1, Pallas kernels: none -> 2.96 us  [on_device(): hold(w_in.reshape(hidden, width), w_out.reshape(hidden, width))]
    ppermute x17 -> x18, starting transfers between devices: 27.7 us -> 28.9 us  [hop(): return lax.ppermute(block, axis, [(i, i ^ step) for i in range(size)])]
  transfers between devices with their start and end apart: 17 -> 18, of which waited for: 7 -> 8; matrix products, arithmetic and copies ran while one was open for 0% -> 0% of each run, Pallas kernels for 11% -> 22%
where the time goes in v7:
time: 82.2 us; the launch traced here: 81.7 us
  starting transfers between devices  28.9 us (35%)
  Pallas kernels  22.8 us (28%)
  blocking collectives  12.8 us (16%)
  waiting for transfers between devices  12.2 us (15%)
  local copies, waits for them, and re-layouts  4.29 us (5%)
    ppermute x18, starting transfers between devices, hop(): return lax.ppermute(block, axis, [(i, i ^ step) for i in range(size)])  28.9 us
    pallas_call x12, Pallas kernels, kernel(): pl.pallas_call(body, out_shape=shapes, in_specs=[VMEM] * len(operands), o...  17.3 us
    all_to_all x1, blocking collectives, on_device(): lax.all_to_all(buffer.reshape(experts, CAP, width), 'expert', split_axis=...  12.8 us
    ppermute x18, waiting for transfers between devices, hop(): return lax.ppermute(block, axis, [(i, i ^ step) for i in range(size)])  12.2 us
    unnamed x18, local copies, waits for them, and re-layouts  4.29 us
    pallas_call x1, Pallas kernels, on_device(): hold(w_in.reshape(hidden, width), w_out.reshape(hidden, width))  2.96 us
    pallas_call x1, Pallas kernels, on_device(): pl.pallas_call(dispatch_kernel, out_shape=[jax.ShapeDtypeStruct((count, w...  2.53 us
  transfers between devices with their start and end apart: 18, of which 8 were waited for; matrix products, arithmetic and copies ran while one was open for 0% of the time, Pallas kernels for 22%

profile of v7, /device:TPU:0, one launch (start us, length us, event | category | flops | bytes accessed | tf_op | source)
XLA Modules:
  0.0 81.7 jit_solution(4022709393031044964)
XLA Ops:
  0.6 2.5 %dispatch.1 = (bf16[256,1280]{1,0:T(8,128)(2,1)}, s32[1,256]{1,0:T(1,128)}, bf16[128,1280]{1,0:T(8,128)(2,1)}) custom-call(bf16[256,1280]{1,0:T(8,128)(2,1)} %tokens.1, f32[1280]{0:T(1024)} %gain.1, s32[1,256]{1,0:T(1,128)} %bitcast.13, s32[1,256]{1,0:T(1,128)} %bitcast.15), custom_call_target="tpu_custom_call" | custom-call | tf_op jit(solution)/shard_map/dispatch/pallas_call | solution.py:200
  3.2 12.8 %all_to_all.5 = bf16[8,16,1280]{2,1,0:T(8,128)(2,1)S(1)} all-to-all(bf16[8,16,1280]{2,1,0:T(8,128)(2,1)} %bitcast.11), channel_id=1, replica_groups=mesh['dp'=4,'expert'=8] {'expert'}, dimensions={0} | all-to-all | bytes 655360 | tf_op jit(solution)/shard_map/all_to_all | solution.py:235
  16.7 3.6 %collective-permute-start.3 = (bf16[64,1280]{1,0:T(8,128)(2,1)}, bf16[64,1280]{1,0:T(8,128)(2,1)}, u32[]{:S(2)}, u32[]{:S(2)}) collective-permute-start(bf16[64,1280]{1,0:T(8,128)(2,1)} %get-tuple-element.24.refs_0_), channel_id=1, source_target_pairs={{0,24},{8,16},{16,8},{24,0},{1,25},{9,17},{17,9},{25,1},{2,26},{10... | collective-permute-start | bytes 491528 | tf_op jit(solution)/shard_map/ppermute | solution.py:232
  20.6 4.7 %collective-permute-done.3.refs_0_ = bf16[64,1280]{1,0:T(8,128)(2,1)} collective-permute-done((bf16[64,1280]{1,0:T(8,128)(2,1)}, bf16[64,1280]{1,0:T(8,128)(2,1)}, u32[]{:S(2)}, u32[]{:S(2)}) %collective-permute-start.3) | collective-permute-done | bytes 163872 | tf_op jit(solution)/shard_map/ppermute | solution.py:232
  25.2 7.2 %collective-permute-start.5 = (bf16[64,1280]{1,0:T(8,128)(2,1)}, bf16[64,1280]{1,0:T(8,128)(2,1)}, u32[]{:S(2)}, u32[]{:S(2)}) collective-permute-start(bf16[64,1280]{1,0:T(8,128)(2,1)} %collective-permute-done.3.refs_0_), channel_id=1, source_target_pairs={{0,8},{8,0},{16,24},{24,16},{1,9},{9,1},{17,25},{25,17},{2,10},{10... | collective-permute-start | bytes 491528 | tf_op jit(solution)/shard_map/ppermute | solution.py:232
  32.5 2.0 %collective-permute-start.1 = (bf16[64,1280]{1,0:T(8,128)(2,1)}, bf16[64,1280]{1,0:T(8,128)(2,1)}, u32[]{:S(2)}, u32[]{:S(2)}) collective-permute-start(bf16[64,1280]{1,0:T(8,128)(2,1)} %get-tuple-element.25.refs_1_), channel_id=1, source_target_pairs={{0,8},{8,0},{16,24},{24,16},{1,9},{9,1},{17,25},{25,17},{2,10},{10... | collective-permute-start | bytes 491528 | tf_op jit(solution)/shard_map/ppermute | solution.py:232
  35.0 3.0 %kernel.15 = (bf16[1280,1280]{1,0:T(8,128)(2,1)S(1)}, bf16[1280,1280]{1,0:T(8,128)(2,1)S(1)}) custom-call(bf16[1280,1280]{1,0:T(8,128)(2,1)} %bitcast.9, bf16[1280,1280]{1,0:T(8,128)(2,1)} %bitcast.10), custom_call_target="tpu_custom_call" | custom-call | tf_op jit(solution)/shard_map/kernel/pallas_call | solution.py:263
  38.0 1.7 %copy-done = bf16[1280,1280]{1,0:T(8,128)(2,1)} copy-done((bf16[1280,1280]{1,0:T(8,128)(2,1)}, bf16[1280,1280]{1,0:T(8,128)(2,1)S(1)}, u32[]{:S(2)}) %copy-start) | copy-done | bytes 3276824
  39.7 2.1 %kernel.13 = (f32[8,256]{1,0:T(8,128)}, f32[8,128]{1,0:T(8,128)}) custom-call(bf16[256,1280]{1,0:T(8,128)(2,1)} %get-tuple-element.21.normed, bf16[8,1280]{1,0:T(8,128)(2,1)} %bitcast.12, s32[1,256]{1,0:T(1,128)} %bitcast.14, s32[1,256]{1,0:T(1,128)} %bitcast.16), custom_call_target="tpu_custom_call" | custom-call | tf_op jit(solution)/shard_map/kernel/pallas_call | solution.py:214
  41.8 1.9 %copy-done.1 = bf16[1280,1280]{1,0:T(8,128)(2,1)S(1)} copy-done((bf16[1280,1280]{1,0:T(8,128)(2,1)S(1)}, bf16[1280,1280]{1,0:T(8,128)(2,1)}, u32[]{:S(2)}) %copy-start.1) | copy-done | bytes 3276824
  44.4 2.8 %kernel.19 = bf16[64,1408]{1,0:T(8,128)(2,1)S(1)} custom-call(bf16[64,1280]{1,0:T(8,128)(2,1)} %collective-permute-done.5.refs_0_, bf16[1280,1280]{1,0:T(8,128)(2,1)S(1)} %copy-done.1, bf16[1,1280]{1,0:T(2,128)(2,1)S(1)} %copy-done.3, bf16[1280,1280]{1,0:T(8,128)(2,1)S(1)} %get-tuple-element.27.refs_4_.refs_3_, f32[8,128]{1,0:T(8,128)S(1)} %copy-done.4), custom_call_target="tpu_custom_call" | custom-call | flops 419430400 | bytes 6881280 | tf_op jit(solution)/shard_map/kernel/pallas_call | solution.py:214
  47.3 1.5 %collective-permute-start.6 = (bf16[64,1408]{1,0:T(8,128)(2,1)S(1)}, bf16[64,1408]{1,0:T(8,128)(2,1)S(1)}, u32[]{:S(2)}, u32[]{:S(2)}) collective-permute-start(bf16[64,1408]{1,0:T(8,128)(2,1)S(1)} %kernel.19), channel_id=1, source_target_pairs={{0,8},{8,0},{16,24},{24,16},{1,9},{9,1},{17,25},{25,17},{2,10},{10... | collective-permute-start | bytes 540680 | tf_op jit(solution)/shard_map/ppermute | solution.py:232
  48.8 2.8 %kernel.17 = bf16[128,1280]{1,0:T(8,128)(2,1)S(1)} custom-call(bf16[64,1280]{1,0:T(8,128)(2,1)} %collective-permute-done.refs_0_, bf16[64,1280]{1,0:T(8,128)(2,1)} %collective-permute-done.1.refs_1_, bf16[1280,1280]{1,0:T(8,128)(2,1)S(1)} %copy-done.2, bf16[1,1280]{1,0:T(2,128)(2,1)S(1)} %copy-done.3, bf16[1280,1280]{1,0:T(8,128)(2,1)S(1)} %get-tuple-element.27.refs_4_.refs_3_), custom_call_target="tpu_custom_call" | custom-call | flops 838860800 | bytes 7208960 | tf_op jit(solution)/shard_map/kernel/pallas_call | solution.py:214
  52.2 1.8 %kernel.22 = bf16[64,1280]{1,0:T(8,128)(2,1)S(1)} custom-call(bf16[64,1280]{1,0:T(8,128)(2,1)S(1)} %collective-permute-done.11.refs_0_, bf16[1280,1280]{1,0:T(8,128)(2,1)S(1)} %copy-done.2, bf16[1,1280]{1,0:T(2,128)(2,1)S(1)} %copy-done.3, bf16[1280,1280]{1,0:T(8,128)(2,1)S(1)} %get-tuple-element.27.refs_4_.refs_3_), custom_call_target="tpu_custom_call" | custom-call | flops 419430400 | bytes 6881280 | tf_op jit(solution)/shard_map/kernel/pallas_call | solution.py:214
  53.9 1.5 %collective-permute-start.12 = (bf16[64,1280]{1,0:T(8,128)(2,1)S(1)}, bf16[64,1280]{1,0:T(8,128)(2,1)S(1)}, u32[]{:S(2)}, u32[]{:S(2)}) collective-permute-start(bf16[64,1280]{1,0:T(8,128)(2,1)S(1)} %kernel.22), channel_id=1, source_target_pairs={{0,8},{8,0},{16,24},{24,16},{1,9},{9,1},{17,25},{25,17},{2,10},{10... | collective-permute-start | bytes 491528 | tf_op jit(solution)/shard_map/ppermute | solution.py:232
  55.5 2.8 %kernel.18.own = f32[128,1280]{1,0:T(8,128)S(1)} custom-call(bf16[64,1280]{1,0:T(8,128)(2,1)} %collective-permute-done.3.refs_0_, bf16[64,1280]{1,0:T(8,128)(2,1)} %collective-permute-done.4.refs_1_, bf16[1280,1280]{1,0:T(8,128)(2,1)S(1)} %copy-done.2, bf16[1,1280]{1,0:T(2,128)(2,1)S(1)} %copy-done.3, bf16[1280,1280]{1,0:T(8,128)(2,1)S(1)} %get-tuple-element.27.refs_4_.refs_3_), custom_call_target="tpu_custom_call" | custom-call | flops 838860800 | bytes 7208960 | tf_op jit(solution)/shard_map/kernel/pallas_call | solution.py:214
  58.3 2.8 %collective-permute-start.7 = (bf16[64,1408]{1,0:T(8,128)(2,1)S(1)}, bf16[64,1408]{1,0:T(8,128)(2,1)S(1)}, u32[]{:S(2)}, u32[]{:S(2)}) collective-permute-start(bf16[64,1408]{1,0:T(8,128)(2,1)S(1)} %kernel.20), channel_id=1, source_target_pairs={{0,24},{8,16},{16,8},{24,0},{1,25},{9,17},{17,9},{25,1},{2,26},{10... | collective-permute-start | bytes 540680 | tf_op jit(solution)/shard_map/ppermute | solution.py:232
  61.1 2.7 %collective-permute-done.12.other = bf16[64,1280]{1,0:T(8,128)(2,1)S(1)} collective-permute-done((bf16[64,1280]{1,0:T(8,128)(2,1)S(1)}, bf16[64,1280]{1,0:T(8,128)(2,1)S(1)}, u32[]{:S(2)}, u32[]{:S(2)}) %collective-permute-start.12) | collective-permute-done | bytes 163872 | tf_op jit(solution)/shard_map/ppermute | solution.py:232
  63.9 2.8 %collective-permute-start.13 = (bf16[64,1280]{1,0:T(8,128)(2,1)S(1)}, bf16[64,1280]{1,0:T(8,128)(2,1)S(1)}, u32[]{:S(2)}, u32[]{:S(2)}) collective-permute-start(bf16[64,1280]{1,0:T(8,128)(2,1)S(1)} %kernel.23), channel_id=1, source_target_pairs={{0,24},{8,16},{16,8},{24,0},{1,25},{9,17},{17,9},{25,1},{2,26},{10... | collective-permute-start | bytes 491528 | tf_op jit(solution)/shard_map/ppermute | solution.py:232
  66.7 2.8 %kernel.16.own = f32[128,1280]{1,0:T(8,128)S(1)} custom-call(bf16[64,1280]{1,0:T(8,128)(2,1)} %get-tuple-element.24.refs_0_, bf16[64,1280]{1,0:T(8,128)(2,1)} %get-tuple-element.25.refs_1_, bf16[1280,1280]{1,0:T(8,128)(2,1)S(1)} %copy-done.2, bf16[1,1280]{1,0:T(2,128)(2,1)S(1)} %copy-done.3, bf16[1280,1280]{1,0:T(8,128)(2,1)S(1)} %get-tuple-element.27.refs_4_.refs_3_), custom_call_target="tpu_custom_call" | custom-call | flops 838860800 | bytes 7208960 | tf_op jit(solution)/shard_map/kernel/pallas_call | solution.py:214
  69.4 1.5 %collective-permute-done.7.refs_0_ = bf16[64,1408]{1,0:T(8,128)(2,1)S(1)} collective-permute-done((bf16[64,1408]{1,0:T(8,128)(2,1)S(1)}, bf16[64,1408]{1,0:T(8,128)(2,1)S(1)}, u32[]{:S(2)}, u32[]{:S(2)}) %collective-permute-start.7) | collective-permute-done | bytes 180256 | tf_op jit(solution)/shard_map/ppermute | solution.py:232
  71.6 1.3 %collective-permute-start.10 = (bf16[16,1408]{1,0:T(8,128)(2,1)S(1)}, bf16[16,1408]{1,0:T(8,128)(2,1)S(1)}, u32[]{:S(2)}, u32[]{:S(2)}) collective-permute-start(bf16[16,1408]{1,0:T(8,128)(2,1)S(1)} %get-tuple-element.32), channel_id=1, source_target_pairs={{0,3},{1,2},{2,1},{3,0},{4,7},{5,6},{6,5},{7,4},{8,11},{9,10},{10,... | collective-permute-start | bytes 135176 | tf_op jit(solution)/shard_map/ppermute | solution.py:232
  75.6 1.9 %collective-permute-start.17 = (bf16[16,1408]{1,0:T(8,128)(2,1)S(1)}, bf16[16,1408]{1,0:T(8,128)(2,1)S(1)}, u32[]{:S(2)}, u32[]{:S(2)}) collective-permute-start(bf16[16,1408]{1,0:T(8,128)(2,1)S(1)} %get-tuple-element.37), channel_id=1, source_target_pairs={{0,7},{1,6},{2,5},{3,4},{4,3},{5,2},{6,1},{7,0},{8,15},{9,14},{10,... | collective-permute-start | bytes 135176 | tf_op jit(solution)/shard_map/ppermute | solution.py:232
  77.7 2.3 %collective-permute-done.16.refs_6_ = bf16[16,1408]{1,0:T(8,128)(2,1)S(1)} collective-permute-done((bf16[16,1408]{1,0:T(8,128)(2,1)S(1)}, bf16[16,1408]{1,0:T(8,128)(2,1)S(1)}, u32[]{:S(2)}, u32[]{:S(2)}) %collective-permute-start.16) | collective-permute-done | bytes 45088 | tf_op jit(solution)/shard_map/ppermute | solution.py:232
  (45 shorter events, 8.2 us)
Async XLA Ops:
  16.7 8.5 %collective-permute-start.3 = (bf16[64,1280]{1,0:T(8,128)(2,1)}, bf16[64,1280]{1,0:T(8,128)(2,1)}, u32[]{:S(2)}, u32[]{:S(2)}) collective-permute-start(bf16[64,1280]{1,0:T(8,128)(2,1)} %get-tuple-element.24.refs_0_), channel_id=1, source_target_pairs={{0,24},{8,16},{16,8},{24,0},{1,25},{9,17},{17,9},{25,1},{2,26},{10... | collective-permute-start | bytes 491528 | tf_op jit(solution)/shard_map/ppermute | solution.py:232
  20.3 14.2 %collective-permute-start.4 = (bf16[64,1280]{1,0:T(8,128)(2,1)}, bf16[64,1280]{1,0:T(8,128)(2,1)}, u32[]{:S(2)}, u32[]{:S(2)}) collective-permute-start(bf16[64,1280]{1,0:T(8,128)(2,1)} %get-tuple-element.25.refs_1_), channel_id=1, source_target_pairs={{0,24},{8,16},{16,8},{24,0},{1,25},{9,17},{17,9},{25,1},{2,26},{10... | collective-permute-start | bytes 491528 | tf_op jit(solution)/shard_map/ppermute | solution.py:232
  25.2 16.6 %collective-permute-start.5 = (bf16[64,1280]{1,0:T(8,128)(2,1)}, bf16[64,1280]{1,0:T(8,128)(2,1)}, u32[]{:S(2)}, u32[]{:S(2)}) collective-permute-start(bf16[64,1280]{1,0:T(8,128)(2,1)} %collective-permute-done.3.refs_0_), channel_id=1, source_target_pairs={{0,8},{8,0},{16,24},{24,16},{1,9},{9,1},{17,25},{25,17},{2,10},{10... | collective-permute-start | bytes 491528 | tf_op jit(solution)/shard_map/ppermute | solution.py:232
  32.5 16.3 %collective-permute-start = (bf16[64,1280]{1,0:T(8,128)(2,1)}, bf16[64,1280]{1,0:T(8,128)(2,1)}, u32[]{:S(2)}, u32[]{:S(2)}) collective-permute-start(bf16[64,1280]{1,0:T(8,128)(2,1)} %get-tuple-element.24.refs_0_), channel_id=1, source_target_pairs={{0,8},{8,0},{16,24},{24,16},{1,9},{9,1},{17,25},{25,17},{2,10},{10... | collective-permute-start | bytes 491528 | tf_op jit(solution)/shard_map/ppermute | solution.py:232
  32.5 16.3 %collective-permute-start.1 = (bf16[64,1280]{1,0:T(8,128)(2,1)}, bf16[64,1280]{1,0:T(8,128)(2,1)}, u32[]{:S(2)}, u32[]{:S(2)}) collective-permute-start(bf16[64,1280]{1,0:T(8,128)(2,1)} %get-tuple-element.25.refs_1_), channel_id=1, source_target_pairs={{0,8},{8,0},{16,24},{24,16},{1,9},{9,1},{17,25},{25,17},{2,10},{10... | collective-permute-start | bytes 491528 | tf_op jit(solution)/shard_map/ppermute | solution.py:232
  34.5 17.7 %collective-permute-start.11 = (bf16[64,1280]{1,0:T(8,128)(2,1)}, bf16[64,1280]{1,0:T(8,128)(2,1)S(1)}, u32[]{:S(2)}, u32[]{:S(2)}) collective-permute-start(bf16[64,1280]{1,0:T(8,128)(2,1)} %collective-permute-done.4.refs_1_), channel_id=1, source_target_pairs={{0,8},{8,0},{16,24},{24,16},{1,9},{9,1},{17,25},{25,17},{2,10},{10... | collective-permute-start | bytes 491528 | tf_op jit(solution)/shard_map/ppermute | solution.py:232
  35.0 6.8 %copy-start.3 = (bf16[1,1280]{1,0:T(2,128)(2,1)S(1)}, bf16[1,1280]{1,0:T(2,128)(2,1)}, u32[]{:S(2)}) copy-start(bf16[1,1280]{1,0:T(2,128)(2,1)} %refs_2_.3) | copy-start | bytes 7684
  44.4 4.4 %copy-start.2 = (bf16[1280,1280]{1,0:T(8,128)(2,1)S(1)}, bf16[1280,1280]{1,0:T(8,128)(2,1)}, u32[]{:S(2)}) copy-start(bf16[1280,1280]{1,0:T(8,128)(2,1)} %copy-done) | copy-start | bytes 9830404
  47.3 11.0 %collective-permute-start.6 = (bf16[64,1408]{1,0:T(8,128)(2,1)S(1)}, bf16[64,1408]{1,0:T(8,128)(2,1)S(1)}, u32[]{:S(2)}, u32[]{:S(2)}) collective-permute-start(bf16[64,1408]{1,0:T(8,128)(2,1)S(1)} %kernel.19), channel_id=1, source_target_pairs={{0,8},{8,0},{16,24},{24,16},{1,9},{9,1},{17,25},{25,17},{2,10},{10... | collective-permute-start | bytes 540680 | tf_op jit(solution)/shard_map/ppermute | solution.py:232
  51.6 17.9 %collective-permute-start.2 = (bf16[128,1280]{1,0:T(8,128)(2,1)S(1)}, bf16[128,1280]{1,0:T(8,128)(2,1)S(1)}, u32[]{:S(2)}, u32[]{:S(2)}) collective-permute-start(bf16[128,1280]{1,0:T(8,128)(2,1)S(1)} %kernel.17), channel_id=1, source_target_pairs={{0,8},{8,0},{16,24},{24,16},{1,9},{9,1},{17,25},{25,17},{2,10},{10... | collective-permute-start | bytes 983048 | tf_op jit(solution)/shard_map/ppermute | solution.py:232
  53.9 9.8 %collective-permute-start.12 = (bf16[64,1280]{1,0:T(8,128)(2,1)S(1)}, bf16[64,1280]{1,0:T(8,128)(2,1)S(1)}, u32[]{:S(2)}, u32[]{:S(2)}) collective-permute-start(bf16[64,1280]{1,0:T(8,128)(2,1)S(1)} %kernel.22), channel_id=1, source_target_pairs={{0,8},{8,0},{16,24},{24,16},{1,9},{9,1},{17,25},{25,17},{2,10},{10... | collective-permute-start | bytes 491528 | tf_op jit(solution)/shard_map/ppermute | solution.py:232
  58.3 12.6 %collective-permute-start.7 = (bf16[64,1408]{1,0:T(8,128)(2,1)S(1)}, bf16[64,1408]{1,0:T(8,128)(2,1)S(1)}, u32[]{:S(2)}, u32[]{:S(2)}) collective-permute-start(bf16[64,1408]{1,0:T(8,128)(2,1)S(1)} %kernel.20), channel_id=1, source_target_pairs={{0,24},{8,16},{16,8},{24,0},{1,25},{9,17},{17,9},{25,1},{2,26},{10... | collective-permute-start | bytes 540680 | tf_op jit(solution)/shard_map/ppermute | solution.py:232
  63.8 7.1 %copy-start.5 = (f32[8,128]{1,0:T(8,128)S(1)}, f32[8,128]{1,0:T(8,128)}, u32[]{:S(2)}) copy-start(f32[8,128]{1,0:T(8,128)} %get-tuple-element.28.refs_4_.refs_0_.refs_1_) | copy-start | bytes 12292
  63.8 7.1 %copy-start.6 = (bf16[1,1280]{1,0:T(2,128)(2,1)S(1)}, bf16[1,1280]{1,0:T(2,128)(2,1)}, u32[]{:S(2)}) copy-start(bf16[1,1280]{1,0:T(2,128)(2,1)} %bias.3) | copy-start | bytes 7684
  63.8 16.6 %copy-start.7 = (f32[8,256]{1,0:T(8,128)S(1)}, f32[8,256]{1,0:T(8,128)}, u32[]{:S(2)}) copy-start(f32[8,256]{1,0:T(8,128)} %get-tuple-element.22.gate) | copy-start | bytes 24580
  63.9 16.6 %copy-start.8 = (s32[1,256]{1,0:T(1,128)S(1)}, s32[1,256]{1,0:T(1,128)}, u32[]{:S(2)}) copy-start(s32[1,256]{1,0:T(1,128)} %get-tuple-element.20.target) | copy-start | bytes 3076
  63.9 9.1 %collective-permute-start.13 = (bf16[64,1280]{1,0:T(8,128)(2,1)S(1)}, bf16[64,1280]{1,0:T(8,128)(2,1)S(1)}, u32[]{:S(2)}, u32[]{:S(2)}) collective-permute-start(bf16[64,1280]{1,0:T(8,128)(2,1)S(1)} %kernel.23), channel_id=1, source_target_pairs={{0,24},{8,16},{16,8},{24,0},{1,25},{9,17},{17,9},{25,1},{2,26},{10... | collective-permute-start | bytes 491528 | tf_op jit(solution)/shard_map/ppermute | solution.py:232
  71.0 3.8 %collective-permute-start.8 = (bf16[16,1408]{1,0:T(8,128)(2,1)S(1)}, bf16[16,1408]{1,0:T(8,128)(2,1)S(1)}, u32[]{:S(2)}, u32[]{:S(2)}) collective-permute-start(bf16[16,1408]{1,0:T(8,128)(2,1)S(1)} %get-tuple-element.30), channel_id=1, source_target_pairs={{0,1},{1,0},{2,3},{3,2},{4,5},{5,4},{6,7},{7,6},{8,9},{9,8},{10,11... | collective-permute-start | bytes 135176 | tf_op jit(solution)/shard_map/ppermute | solution.py:232
  71.1 4.5 %collective-permute-start.9 = (bf16[16,1408]{1,0:T(8,128)(2,1)S(1)}, bf16[16,1408]{1,0:T(8,128)(2,1)S(1)}, u32[]{:S(2)}, u32[]{:S(2)}) collective-permute-start(bf16[16,1408]{1,0:T(8,128)(2,1)S(1)} %get-tuple-element.31), channel_id=1, source_target_pairs={{0,2},{1,3},{2,0},{3,1},{4,6},{5,7},{6,4},{7,5},{8,10},{9,11},{10,... | collective-permute-start | bytes 135176 | tf_op jit(solution)/shard_map/ppermute | solution.py:232
  71.6 5.9 %collective-permute-start.10 = (bf16[16,1408]{1,0:T(8,128)(2,1)S(1)}, bf16[16,1408]{1,0:T(8,128)(2,1)S(1)}, u32[]{:S(2)}, u32[]{:S(2)}) collective-permute-start(bf16[16,1408]{1,0:T(8,128)(2,1)S(1)} %get-tuple-element.32), channel_id=1, source_target_pairs={{0,3},{1,2},{2,1},{3,0},{4,7},{5,6},{6,5},{7,4},{8,11},{9,10},{10,... | collective-permute-start | bytes 135176 | tf_op jit(solution)/shard_map/ppermute | solution.py:232
  73.1 4.6 %collective-permute-start.14 = (bf16[16,1408]{1,0:T(8,128)(2,1)S(1)}, bf16[16,1408]{1,0:T(8,128)(2,1)S(1)}, u32[]{:S(2)}, u32[]{:S(2)}) collective-permute-start(bf16[16,1408]{1,0:T(8,128)(2,1)S(1)} %get-tuple-element.34), channel_id=1, source_target_pairs={{0,4},{1,5},{2,6},{3,7},{4,0},{5,1},{6,2},{7,3},{8,12},{9,13},{10,... | collective-permute-start | bytes 135176 | tf_op jit(solution)/shard_map/ppermute | solution.py:232
  73.7 4.0 %collective-permute-start.15 = (bf16[16,1408]{1,0:T(8,128)(2,1)S(1)}, bf16[16,1408]{1,0:T(8,128)(2,1)S(1)}, u32[]{:S(2)}, u32[]{:S(2)}) collective-permute-start(bf16[16,1408]{1,0:T(8,128)(2,1)S(1)} %get-tuple-element.35), channel_id=1, source_target_pairs={{0,5},{1,4},{2,7},{3,6},{4,1},{5,0},{6,3},{7,2},{8,13},{9,12},{10,... | collective-permute-start | bytes 135176 | tf_op jit(solution)/shard_map/ppermute | solution.py:232
  74.8 5.2 %collective-permute-start.16 = (bf16[16,1408]{1,0:T(8,128)(2,1)S(1)}, bf16[16,1408]{1,0:T(8,128)(2,1)S(1)}, u32[]{:S(2)}, u32[]{:S(2)}) collective-permute-start(bf16[16,1408]{1,0:T(8,128)(2,1)S(1)} %get-tuple-element.36), channel_id=1, source_target_pairs={{0,6},{1,7},{2,4},{3,5},{4,2},{5,3},{6,0},{7,1},{8,14},{9,15},{10,... | collective-permute-start | bytes 135176 | tf_op jit(solution)/shard_map/ppermute | solution.py:232
  75.6 4.9 %collective-permute-start.17 = (bf16[16,1408]{1,0:T(8,128)(2,1)S(1)}, bf16[16,1408]{1,0:T(8,128)(2,1)S(1)}, u32[]{:S(2)}, u32[]{:S(2)}) collective-permute-start(bf16[16,1408]{1,0:T(8,128)(2,1)S(1)} %get-tuple-element.37), channel_id=1, source_target_pairs={{0,7},{1,6},{2,5},{3,4},{4,3},{5,2},{6,1},{7,0},{8,15},{9,14},{10,... | collective-permute-start | bytes 135176 | tf_op jit(solution)/shard_map/ppermute | solution.py:232
  (3 other events, 4.3 us)

commit v8 on v7

--- a/solution.py
+++ b/solution.py
@@ -34,27 +34,41 @@
     return jnp.sum(block.astype(jnp.float32), axis=0, keepdims=True)
 
 
-def dispatch_kernel(tokens, gain, choice, slot, normed_out, target_out, buffer):
+def dispatch_kernel(tokens, gain, choice, slot, normed_out, target_out, odds, *evens):
     values = tokens[...].astype(jnp.float32)
     center = values - jnp.mean(values, axis=-1, keepdims=True)
     spread = jnp.mean(center * center, axis=-1, keepdims=True)
     scaled = center * lax.rsqrt(spread + 1e-06) * gain[...].reshape(1, values.shape[1])
     normed = scaled.astype(jnp.bfloat16)
     normed_out[...] = normed
-    kept = slot[...] >= 0
     relative = choice[...] ^ lax.axis_index("expert")
-    target_out[...] = jnp.where(kept, relative * CAP + slot[...], -1)
-    table = one_hot(buffer.shape[0], jnp.where(kept, choice[...] * CAP + slot[...], -1))
-    buffer[...] = jnp.dot(table, normed, preferred_element_type=jnp.float32).astype(jnp.bfloat16)
-
-
-def pack_kernel(received, *parts):
-    me = lax.axis_index("expert")
-    each = parts[0].shape[0] // CAP
-    for k in range(received.shape[0] // CAP):
-        slab = received[pl.ds(pl.multiple_of((me ^ k) * CAP, CAP), CAP)]
-        at = (k % each) * CAP
-        parts[k // each][at : at + CAP] = slab
+    target = jnp.where(slot[...] >= 0, relative * CAP + slot[...], -1)
+    target_out[...] = target
+    rows = odds.shape[0] + len(evens) * CAP
+    table = one_hot(rows, target)
+    packed = jnp.dot(table, normed, preferred_element_type=jnp.float32).astype(jnp.bfloat16)
+    for index, even in enumerate(evens):
+        start = 2 * index * CAP
+        even[...] = packed[start : start + CAP]
+        odds[index * CAP : (index + 1) * CAP] = packed[start + CAP : start + 2 * CAP]
+
+
+def join_kernel(first, *refs):
+    count = len(refs) // 2
+    partner, evens, outs = refs[0], refs[1 : count + 1], refs[count + 1 :]
+    for index in range(count):
+        start = (first + index) * CAP
+        outs[index][:CAP] = evens[index][...]
+        outs[index][CAP:] = partner[start : start + CAP]
+
+
+def pack_kernel(opening, *refs):
+    blocks, out = list(refs[:-1]), refs[-1]
+    at = 0
+    for index, block in enumerate(blocks):
+        size = CAP if opening and index == 1 else block.shape[0]
+        out[at : at + size] = block[:size]
+        at += size
 
 
 def hold_kernel(w_in, w_out, first, second, sems):
@@ -143,25 +157,28 @@
     else:
         extra = refs[0][...]
         slabs = refs[1:]
-    for place, slab in enumerate(slabs):
-        slab[:, :width] = result[place * CAP : (place + 1) * CAP]
-        slab[:, width:] = extra
+    odds, evens = slabs[0], slabs[1:]
+    for place, even in enumerate(evens):
+        start = 2 * place * CAP
+        even[:, :width] = result[start : start + CAP]
+        even[:, width:] = extra
+        here = slice(place * CAP, (place + 1) * CAP)
+        odds[here, :width] = result[start + CAP : start + 2 * CAP]
+        odds[here, width:] = extra
 
 
 def combine_kernel(experts, target, gate, *refs):
     slabs, (out, aux) = refs[:-2], refs[-2:]
     width = out.shape[1]
-    returned = jnp.concatenate([slab[...] for slab in slabs], axis=0)
+    blocks = [slabs[0][...], slabs[1][:CAP]] + [slab[...] for slab in slabs[2:]]
+    returned = jnp.concatenate(blocks, axis=0)
     table = one_hot(returned.shape[0], target[...])
     fetched = lax.dot_general(
         table, returned[:, :width], (((0,), (0,)), ((), ())), preferred_element_type=jnp.float32
     )
     scale = jnp.transpose(gate[...])[:, 0:1]
     out[...] = (scale * fetched).astype(jnp.bfloat16)
-    sums = join_stats(slabs[0][:, width:])
-    have = {0: sums}
-    for index in range(1, experts):
-        have[index] = join_stats(slabs[index][:, width:])
+    have = {k: join_stats(returned[k * CAP : (k + 1) * CAP, width:]) for k in range(experts)}
     while len(have) > 1:
         have = {at // 2: have[at] + have[at + 1] for at in range(0, len(have), 2)}
     sums = have[0]
@@ -197,15 +214,17 @@
     full = width + LANES
     far_steps = [m ^ ((m >> 1) & 1) for m in range(2, layers, 2)]
     choice = expert_choice.reshape(1, count)
-    normed, target, buffer = pl.pallas_call(
+    pairs = experts // 2
+    normed, target, odds, *evens = pl.pallas_call(
         dispatch_kernel,
         out_shape=[
             jax.ShapeDtypeStruct((count, width), jnp.bfloat16),
             jax.ShapeDtypeStruct((1, count), jnp.int32),
-            jax.ShapeDtypeStruct((rows, width), jnp.bfloat16),
-        ],
+            pltpu.VMEM((pairs * CAP, width), jnp.bfloat16),
+        ]
+        + [pltpu.VMEM((CAP, width), jnp.bfloat16)] * pairs,
         in_specs=[VMEM] * 4,
-        out_specs=[VMEM] * 3,
+        out_specs=[VMEM] * (3 + pairs),
         name="dispatch",
     )(tokens, ln_gain, choice, slot.reshape(1, count))
 
@@ -231,11 +250,18 @@
         size = lax.axis_size(axis)
         return lax.ppermute(block, axis, [(i, i ^ step) for i in range(size)])
 
-    each = experts // PARTS
-    received = lax.all_to_all(
-        buffer.reshape(experts, CAP, width), "expert", split_axis=0, concat_axis=0, tiled=True
-    ).reshape(rows, width)
-    homes = kernel(pack_kernel, [bf16(tall, width)] * PARTS, received)
+    partner = hop(odds, "expert", 1)
+    joined = kernel(
+        functools.partial(join_kernel, 1), [bf16(2 * CAP, width)] * (pairs - 1), partner, *evens[1:]
+    )
+    came = [hop(block, "expert", 2 * j + 2) for j, block in enumerate(joined)]
+    share = pairs // PARTS
+    homes = []
+    for part in range(PARTS):
+        blocks = came[max(part * share - 1, 0) : (part + 1) * share - 1]
+        if part == 0:
+            blocks = [evens[0], partner] + blocks
+        homes.append(kernel(functools.partial(pack_kernel, part == 0), bf16(tall, width), *blocks))
     beside = [hop(homes[part], "dp", 1) for part in range(PARTS)]
     visitors = {
         (step, part): hop(homes[part], "dp", step)
@@ -308,16 +334,28 @@
     back, extra = [], None
     for part in range(PARTS):
         far = [returned[step, part] for step in far_steps]
-        shapes = [bf16(CAP, full)] * each
+        shapes = [bf16(share * CAP, full)] + [bf16(CAP, full)] * share
         body = functools.partial(near_kernel, part, len(far))
         if part == 0:
-            out = kernel(body, [bf16(CAP, LANES)] + shapes, own, answer, b_out, *far, stats, shared)
-            extra, out = out[0], out[1:]
+            extra, odds, *evens = kernel(
+                body, [bf16(CAP, LANES)] + shapes, own, answer, b_out, *far, stats, shared
+            )
         else:
-            out = kernel(body, shapes, own, answer, b_out, *far, extra)
-        for place, slab in enumerate(out):
-            k = part * each + place
-            back.append(hop(slab, "expert", k) if k else slab)
+            odds, *evens = kernel(body, shapes, own, answer, b_out, *far, extra)
+        partner = hop(odds, "expert", 1)
+        lead = 1 if part == 0 else 0
+        if part == 0:
+            back += [evens[0], partner]
+        if share > lead:
+            joined = kernel(
+                functools.partial(join_kernel, lead),
+                [bf16(2 * CAP, full)] * (share - lead),
+                partner,
+                *evens[lead:],
+            )
+            for index, block in enumerate(joined):
+                k = 2 * (part * share + lead + index)
+                back.append(hop(block, "expert", k))
     return tuple(
         kernel(
             functools.partial(combine_kernel, experts),

time: 82.2 us -> 77 us (0.937)
  the two profiles are of different devices: /device:TPU:0 before, /device:TPU:8 now
where the time goes in v8:
time: 77 us; the launch traced here: 76.7 us
  waiting for transfers between devices  29.5 us (38%)
  Pallas kernels  23.5 us (31%)
  starting transfers between devices  19.3 us (25%)
  local copies, waits for them, and re-layouts  3.63 us (5%)
  between operations  0.78 us (1%)
    ppermute x20, waiting for transfers between devices, hop(): return lax.ppermute(block, axis, [(i, i ^ step) for i in range(size)])  29.5 us
    ppermute x20, starting transfers between devices, hop(): return lax.ppermute(block, axis, [(i, i ^ step) for i in range(size)])  19.3 us
    pallas_call x16, Pallas kernels, kernel(): pl.pallas_call(body, out_shape=shapes, in_specs=[VMEM] * len(operands), o...  18.1 us
    unnamed x16, local copies, waits for them, and re-layouts  3.63 us
    pallas_call x1, Pallas kernels, on_device(): hold(w_in.reshape(hidden, width), w_out.reshape(hidden, width))  2.96 us
    pallas_call x1, Pallas kernels, on_device(): pl.pallas_call(dispatch_kernel, out_shape=[jax.ShapeDtypeStruct((count, w...  2.43 us
  transfers between devices with their start and end apart: 20, of which 14 were waited for; matrix products, arithmetic and copies ran while one was open for 0% of the time, Pallas kernels for 26%

profile of v8, /device:TPU:8, one launch (start us, length us, event | category | flops | bytes accessed | tf_op | source)
XLA Modules:
  0.0 76.7 jit_solution(4178787178413264665)
XLA Ops:
  0.6 2.4 %dispatch.1 = (bf16[256,1280]{1,0:T(8,128)(2,1)}, s32[1,256]{1,0:T(1,128)}, bf16[64,1280]{1,0:T(8,128)(2,1)S(1)}, bf16[16,1280]{1,0:T(8,128)(2,1)S(1)}, bf16[16,...) custom-call(bf16[256,1280]{1,0:T(8,128)(2,1)} %tokens.1, f32[1280]{0:T(1024)} %gain.1, ...), custom_call_target="tpu_custom_call" | custom-call | tf_op jit(solution)/shard_map/dispatch/pallas_call | solution.py:218
  9.0 1.6 %collective-permute-start.7 = (bf16[64,1280]{1,0:T(8,128)(2,1)S(1)}, bf16[64,1280]{1,0:T(8,128)(2,1)}, u32[]{:S(2)}, u32[]{:S(2)}) collective-permute-start(bf16[64,1280]{1,0:T(8,128)(2,1)S(1)} %kernel.19.refs_0_), channel_id=1, source_target_pairs={{0,24},{8,16},{16,8},{24,0},{1,25},{9,17},{17,9},{25,1},{2,26},{10... | collective-permute-start | bytes 491528 | tf_op jit(solution)/shard_map/ppermute | solution.py:251
  11.3 1.6 %collective-permute-done.3.refs_1_ = bf16[32,1280]{1,0:T(8,128)(2,1)S(1)} collective-permute-done((bf16[32,1280]{1,0:T(8,128)(2,1)S(1)}, bf16[32,1280]{1,0:T(8,128)(2,1)S(1)}, u32[]{:S(2)}, u32[]{:S(2)}) %collective-permute-start.3) | collective-permute-done | bytes 81952 | tf_op jit(solution)/shard_map/ppermute | solution.py:251
  13.6 1.6 %collective-permute-start.8 = (bf16[64,1280]{1,0:T(8,128)(2,1)}, bf16[64,1280]{1,0:T(8,128)(2,1)}, u32[]{:S(2)}, u32[]{:S(2)}) collective-permute-start(bf16[64,1280]{1,0:T(8,128)(2,1)} %kernel.20.refs_1_), channel_id=1, source_target_pairs={{0,24},{8,16},{16,8},{24,0},{1,25},{9,17},{17,9},{25,1},{2,26},{10... | collective-permute-start | bytes 491528 | tf_op jit(solution)/shard_map/ppermute | solution.py:251
  15.1 2.5 %collective-permute-start.5 = (bf16[64,1280]{1,0:T(8,128)(2,1)}, bf16[64,1280]{1,0:T(8,128)(2,1)}, u32[]{:S(2)}, u32[]{:S(2)}) collective-permute-start(bf16[64,1280]{1,0:T(8,128)(2,1)} %kernel.20.refs_1_), channel_id=1, source_target_pairs={{0,8},{8,0},{16,24},{24,16},{1,9},{9,1},{17,25},{25,17},{2,10},{10... | collective-permute-start | bytes 491528 | tf_op jit(solution)/shard_map/ppermute | solution.py:251
  17.6 4.9 %collective-permute-done.7.refs_0_ = bf16[64,1280]{1,0:T(8,128)(2,1)} collective-permute-done((bf16[64,1280]{1,0:T(8,128)(2,1)S(1)}, bf16[64,1280]{1,0:T(8,128)(2,1)}, u32[]{:S(2)}, u32[]{:S(2)}) %collective-permute-start.7) | collective-permute-done | bytes 163872 | tf_op jit(solution)/shard_map/ppermute | solution.py:251
  22.6 2.6 %collective-permute-done.8.refs_1_ = bf16[64,1280]{1,0:T(8,128)(2,1)} collective-permute-done((bf16[64,1280]{1,0:T(8,128)(2,1)}, bf16[64,1280]{1,0:T(8,128)(2,1)}, u32[]{:S(2)}, u32[]{:S(2)}) %collective-permute-start.8) | collective-permute-done | bytes 163872 | tf_op jit(solution)/shard_map/ppermute | solution.py:251
  25.1 3.0 %kernel.21 = (bf16[1280,1280]{1,0:T(8,128)(2,1)S(1)}, bf16[1280,1280]{1,0:T(8,128)(2,1)S(1)}) custom-call(bf16[1280,1280]{1,0:T(8,128)(2,1)} %bitcast.6, bf16[1280,1280]{1,0:T(8,128)(2,1)} %bitcast.7), custom_call_target="tpu_custom_call" | custom-call | tf_op jit(solution)/shard_map/kernel/pallas_call | solution.py:289
  28.1 1.7 %copy-done = bf16[1280,1280]{1,0:T(8,128)(2,1)} copy-done((bf16[1280,1280]{1,0:T(8,128)(2,1)}, bf16[1280,1280]{1,0:T(8,128)(2,1)S(1)}, u32[]{:S(2)}) %copy-start) | copy-done | bytes 3276824
  29.8 2.1 %kernel.17 = (f32[8,256]{1,0:T(8,128)}, f32[8,128]{1,0:T(8,128)}) custom-call(bf16[256,1280]{1,0:T(8,128)(2,1)} %get-tuple-element.26.normed, bf16[8,1280]{1,0:T(8,128)(2,1)} %bitcast.8, s32[1,256]{1,0:T(1,128)} %bitcast.10, s32[1,256]{1,0:T(1,128)} %bitcast.12), custom_call_target="tpu_custom_call" | custom-call | tf_op jit(solution)/shard_map/kernel/pallas_call | solution.py:233
  32.0 1.9 %copy-done.1 = bf16[1280,1280]{1,0:T(8,128)(2,1)S(1)} copy-done((bf16[1280,1280]{1,0:T(8,128)(2,1)S(1)}, bf16[1280,1280]{1,0:T(8,128)(2,1)}, u32[]{:S(2)}) %copy-start.1) | copy-done | bytes 3276824
  33.9 2.9 %kernel.23 = bf16[128,1280]{1,0:T(8,128)(2,1)S(1)} custom-call(bf16[64,1280]{1,0:T(8,128)(2,1)} %collective-permute-done.4.refs_0_, bf16[64,1280]{1,0:T(8,128)(2,1)} %collective-permute-done.5.refs_1_, bf16[1280,1280]{1,0:T(8,128)(2,1)S(1)} %copy-done.1, bf16[1,1280]{1,0:T(2,128)(2,1)S(1)} %copy-done.3, bf16[1280,1280]{1,0:T(8,128)(2,1)S(1)} %get-tuple-element.37.refs_4_.refs_3_), custom_call_target="tpu_custom_call" | custom-call | flops 838860800 | bytes 7208960 | tf_op jit(solution)/shard_map/kernel/pallas_call | solution.py:233
  36.8 2.1 %collective-permute-start.6 = (bf16[128,1280]{1,0:T(8,128)(2,1)S(1)}, bf16[128,1280]{1,0:T(8,128)(2,1)S(1)}, u32[]{:S(2)}, u32[]{:S(2)}) collective-permute-start(bf16[128,1280]{1,0:T(8,128)(2,1)S(1)} %kernel.23), channel_id=1, source_target_pairs={{0,8},{8,0},{16,24},{24,16},{1,9},{9,1},{17,25},{25,17},{2,10},{10... | collective-permute-start | bytes 983048 | tf_op jit(solution)/shard_map/ppermute | solution.py:251
  38.9 2.7 %kernel.25 = bf16[64,1408]{1,0:T(8,128)(2,1)S(1)} custom-call(bf16[64,1280]{1,0:T(8,128)(2,1)} %collective-permute-done.9.refs_0_, bf16[1280,1280]{1,0:T(8,128)(2,1)S(1)} %copy-done.2, bf16[1,1280]{1,0:T(2,128)(2,1)S(1)} %copy-done.3, bf16[1280,1280]{1,0:T(8,128)(2,1)S(1)} %get-tuple-element.37.refs_4_.refs_3_, f32[8,128]{1,0:T(8,128)S(1)} %copy-done.4), custom_call_target="tpu_custom_call" | custom-call | flops 419430400 | bytes 6881280 | tf_op jit(solution)/shard_map/kernel/pallas_call | solution.py:233
  41.7 2.7 %kernel.29 = bf16[64,1280]{1,0:T(8,128)(2,1)S(1)} custom-call(bf16[64,1280]{1,0:T(8,128)(2,1)} %collective-permute-done.14.refs_0_, bf16[1280,1280]{1,0:T(8,128)(2,1)S(1)} %copy-done.2, bf16[1,1280]{1,0:T(2,128)(2,1)S(1)} %copy-done.3, bf16[1280,1280]{1,0:T(8,128)(2,1)S(1)} %get-tuple-element.37.refs_4_.refs_3_), custom_call_target="tpu_custom_call" | custom-call | flops 419430400 | bytes 6881280 | tf_op jit(solution)/shard_map/kernel/pallas_call | solution.py:233
  44.4 2.0 %collective-permute-start.15 = (bf16[64,1280]{1,0:T(8,128)(2,1)S(1)}, bf16[64,1280]{1,0:T(8,128)(2,1)S(1)}, u32[]{:S(2)}, u32[]{:S(2)}) collective-permute-start(bf16[64,1280]{1,0:T(8,128)(2,1)S(1)} %kernel.29), channel_id=1, source_target_pairs={{0,8},{8,0},{16,24},{24,16},{1,9},{9,1},{17,25},{25,17},{2,10},{10... | collective-permute-start | bytes 491528 | tf_op jit(solution)/shard_map/ppermute | solution.py:251
  46.4 2.8 %kernel.24.own = f32[128,1280]{1,0:T(8,128)S(1)} custom-call(bf16[64,1280]{1,0:T(8,128)(2,1)} %collective-permute-done.7.refs_0_, bf16[64,1280]{1,0:T(8,128)(2,1)} %collective-permute-done.8.refs_1_, bf16[1280,1280]{1,0:T(8,128)(2,1)S(1)} %copy-done.2, bf16[1,1280]{1,0:T(2,128)(2,1)S(1)} %copy-done.3, bf16[1280,1280]{1,0:T(8,128)(2,1)S(1)} %get-tuple-element.37.refs_4_.refs_3_), custom_call_target="tpu_custom_call" | custom-call | flops 838860800 | bytes 7208960 | tf_op jit(solution)/shard_map/kernel/pallas_call | solution.py:233
  49.2 2.1 %collective-permute-done.10.other.refs_1_.refs_2_ = bf16[64,1408]{1,0:T(8,128)(2,1)S(1)} collective-permute-done((bf16[64,1408]{1,0:T(8,128)(2,1)S(1)}, bf16[64,1408]{1,0:T(8,128)(2,1)S(1)}, u32[]{:S(2)}, u32[]{:S(2)}) %collective-permute-start.10) | collective-permute-done | bytes 180256 | tf_op jit(solution)/shard_map/ppermute | solution.py:251
  52.4 2.3 %collective-permute-done.15.other = bf16[64,1280]{1,0:T(8,128)(2,1)S(1)} collective-permute-done((bf16[64,1280]{1,0:T(8,128)(2,1)S(1)}, bf16[64,1280]{1,0:T(8,128)(2,1)S(1)}, u32[]{:S(2)}, u32[]{:S(2)}) %collective-permute-start.15) | collective-permute-done | bytes 163872 | tf_op jit(solution)/shard_map/ppermute | solution.py:251
  55.4 2.7 %kernel.22.own = f32[128,1280]{1,0:T(8,128)S(1)} custom-call(bf16[64,1280]{1,0:T(8,128)(2,1)S(1)} %kernel.19.refs_0_, bf16[64,1280]{1,0:T(8,128)(2,1)} %kernel.20.refs_1_, bf16[1280,1280]{1,0:T(8,128)(2,1)S(1)} %copy-done.2, bf16[1,1280]{1,0:T(2,128)(2,1)S(1)} %copy-done.3, bf16[1280,1280]{1,0:T(8,128)(2,1)S(1)} %get-tuple-element.37.refs_4_.refs_3_), custom_call_target="tpu_custom_call" | custom-call | flops 838860800 | bytes 7208960 | tf_op jit(solution)/shard_map/kernel/pallas_call | solution.py:233
  58.1 6.2 %collective-permute-done.11.refs_0_ = bf16[64,1408]{1,0:T(8,128)(2,1)S(1)} collective-permute-done((bf16[64,1408]{1,0:T(8,128)(2,1)S(1)}, bf16[64,1408]{1,0:T(8,128)(2,1)S(1)}, u32[]{:S(2)}, u32[]{:S(2)}) %collective-permute-start.11) | collective-permute-done | bytes 180256 | tf_op jit(solution)/shard_map/ppermute | solution.py:251
  64.4 1.7 %collective-permute-done.16.refs_0_ = bf16[64,1280]{1,0:T(8,128)(2,1)S(1)} collective-permute-done((bf16[64,1280]{1,0:T(8,128)(2,1)S(1)}, bf16[64,1280]{1,0:T(8,128)(2,1)S(1)}, u32[]{:S(2)}, u32[]{:S(2)}) %collective-permute-start.16) | collective-permute-done | bytes 163872 | tf_op jit(solution)/shard_map/ppermute | solution.py:251
  71.1 1.8 %collective-permute-done.18.refs_3_ = bf16[32,1408]{1,0:T(8,128)(2,1)S(1)} collective-permute-done((bf16[32,1408]{1,0:T(8,128)(2,1)S(1)}, bf16[32,1408]{1,0:T(8,128)(2,1)S(1)}, u32[]{:S(2)}, u32[]{:S(2)}) %collective-permute-start.18) | collective-permute-done | bytes 90144 | tf_op jit(solution)/shard_map/ppermute | solution.py:251
  72.9 2.3 %collective-permute-done.19.refs_4_ = bf16[32,1408]{1,0:T(8,128)(2,1)S(1)} collective-permute-done((bf16[32,1408]{1,0:T(8,128)(2,1)S(1)}, bf16[32,1408]{1,0:T(8,128)(2,1)S(1)}, u32[]{:S(2)}, u32[]{:S(2)}) %collective-permute-start.19) | collective-permute-done | bytes 90144 | tf_op jit(solution)/shard_map/ppermute | solution.py:251
  (50 shorter events, 15.8 us)
Async XLA Ops:
  3.1 1.4 %collective-permute-start = (bf16[64,1280]{1,0:T(8,128)(2,1)S(1)}, bf16[64,1280]{1,0:T(8,128)(2,1)S(1)}, u32[]{:S(2)}, u32[]{:S(2)}) collective-permute-start(bf16[64,1280]{1,0:T(8,128)(2,1)S(1)} %get-tuple-element.29), channel_id=1, source_target_pairs={{0,1},{1,0},{2,3},{3,2},{4,5},{5,4},{6,7},{7,6},{8,9},{9,8},{10,11... | collective-permute-start | bytes 491528 | tf_op jit(solution)/shard_map/ppermute | solution.py:251
  4.5 4.6 %collective-permute-start.1 = (bf16[32,1280]{1,0:T(8,128)(2,1)S(1)}, bf16[32,1280]{1,0:T(8,128)(2,1)S(1)}, u32[]{:S(2)}, u32[]{:S(2)}) collective-permute-start(bf16[32,1280]{1,0:T(8,128)(2,1)S(1)} %get-tuple-element.33), channel_id=1, source_target_pairs={{0,2},{1,3},{2,0},{3,1},{4,6},{5,7},{6,4},{7,5},{8,10},{9,11},{10,... | collective-permute-start | bytes 245768 | tf_op jit(solution)/shard_map/ppermute | solution.py:251
  6.0 5.3 %collective-permute-start.2 = (bf16[32,1280]{1,0:T(8,128)(2,1)S(1)}, bf16[32,1280]{1,0:T(8,128)(2,1)S(1)}, u32[]{:S(2)}, u32[]{:S(2)}) collective-permute-start(bf16[32,1280]{1,0:T(8,128)(2,1)S(1)} %get-tuple-element.34), channel_id=1, source_target_pairs={{0,4},{1,5},{2,6},{3,7},{4,0},{5,1},{6,2},{7,3},{8,12},{9,13},{10,... | collective-permute-start | bytes 245768 | tf_op jit(solution)/shard_map/ppermute | solution.py:251
  7.6 5.3 %collective-permute-start.3 = (bf16[32,1280]{1,0:T(8,128)(2,1)S(1)}, bf16[32,1280]{1,0:T(8,128)(2,1)S(1)}, u32[]{:S(2)}, u32[]{:S(2)}) collective-permute-start(bf16[32,1280]{1,0:T(8,128)(2,1)S(1)} %get-tuple-element.35), channel_id=1, source_target_pairs={{0,6},{1,7},{2,4},{3,5},{4,2},{5,3},{6,0},{7,1},{8,14},{9,15},{10,... | collective-permute-start | bytes 245768 | tf_op jit(solution)/shard_map/ppermute | solution.py:251
  9.0 13.5 %collective-permute-start.7 = (bf16[64,1280]{1,0:T(8,128)(2,1)S(1)}, bf16[64,1280]{1,0:T(8,128)(2,1)}, u32[]{:S(2)}, u32[]{:S(2)}) collective-permute-start(bf16[64,1280]{1,0:T(8,128)(2,1)S(1)} %kernel.19.refs_0_), channel_id=1, source_target_pairs={{0,24},{8,16},{16,8},{24,0},{1,25},{9,17},{17,9},{25,1},{2,26},{10... | collective-permute-start | bytes 491528 | tf_op jit(solution)/shard_map/ppermute | solution.py:251
  13.6 11.6 %collective-permute-start.8 = (bf16[64,1280]{1,0:T(8,128)(2,1)}, bf16[64,1280]{1,0:T(8,128)(2,1)}, u32[]{:S(2)}, u32[]{:S(2)}) collective-permute-start(bf16[64,1280]{1,0:T(8,128)(2,1)} %kernel.20.refs_1_), channel_id=1, source_target_pairs={{0,24},{8,16},{16,8},{24,0},{1,25},{9,17},{17,9},{25,1},{2,26},{10... | collective-permute-start | bytes 491528 | tf_op jit(solution)/shard_map/ppermute | solution.py:251
  15.1 16.8 %collective-permute-start.5 = (bf16[64,1280]{1,0:T(8,128)(2,1)}, bf16[64,1280]{1,0:T(8,128)(2,1)}, u32[]{:S(2)}, u32[]{:S(2)}) collective-permute-start(bf16[64,1280]{1,0:T(8,128)(2,1)} %kernel.20.refs_1_), channel_id=1, source_target_pairs={{0,8},{8,0},{16,24},{24,16},{1,9},{9,1},{17,25},{25,17},{2,10},{10... | collective-permute-start | bytes 491528 | tf_op jit(solution)/shard_map/ppermute | solution.py:251
  17.6 14.3 %collective-permute-start.4 = (bf16[64,1280]{1,0:T(8,128)(2,1)S(1)}, bf16[64,1280]{1,0:T(8,128)(2,1)}, u32[]{:S(2)}, u32[]{:S(2)}) collective-permute-start(bf16[64,1280]{1,0:T(8,128)(2,1)S(1)} %kernel.19.refs_0_), channel_id=1, source_target_pairs={{0,8},{8,0},{16,24},{24,16},{1,9},{9,1},{17,25},{25,17},{2,10},{10... | collective-permute-start | bytes 491528 | tf_op jit(solution)/shard_map/ppermute | solution.py:251
  22.6 16.3 %collective-permute-start.9 = (bf16[64,1280]{1,0:T(8,128)(2,1)}, bf16[64,1280]{1,0:T(8,128)(2,1)}, u32[]{:S(2)}, u32[]{:S(2)}) collective-permute-start(bf16[64,1280]{1,0:T(8,128)(2,1)} %collective-permute-done.7.refs_0_), channel_id=1, source_target_pairs={{0,8},{8,0},{16,24},{24,16},{1,9},{9,1},{17,25},{25,17},{2,10},{10... | collective-permute-start | bytes 491528 | tf_op jit(solution)/shard_map/ppermute | solution.py:251
  25.1 16.5 %collective-permute-start.14 = (bf16[64,1280]{1,0:T(8,128)(2,1)}, bf16[64,1280]{1,0:T(8,128)(2,1)}, u32[]{:S(2)}, u32[]{:S(2)}) collective-permute-start(bf16[64,1280]{1,0:T(8,128)(2,1)} %collective-permute-done.8.refs_1_), channel_id=1, source_target_pairs={{0,8},{8,0},{16,24},{24,16},{1,9},{9,1},{17,25},{25,17},{2,10},{10... | collective-permute-start | bytes 491528 | tf_op jit(solution)/shard_map/ppermute | solution.py:251
  25.1 6.8 %copy-start.3 = (bf16[1,1280]{1,0:T(2,128)(2,1)S(1)}, bf16[1,1280]{1,0:T(2,128)(2,1)}, u32[]{:S(2)}) copy-start(bf16[1,1280]{1,0:T(2,128)(2,1)} %refs_2_.3) | copy-start | bytes 7684
  36.8 21.2 %collective-permute-start.6 = (bf16[128,1280]{1,0:T(8,128)(2,1)S(1)}, bf16[128,1280]{1,0:T(8,128)(2,1)S(1)}, u32[]{:S(2)}, u32[]{:S(2)}) collective-permute-start(bf16[128,1280]{1,0:T(8,128)(2,1)S(1)} %kernel.23), channel_id=1, source_target_pairs={{0,8},{8,0},{16,24},{24,16},{1,9},{9,1},{17,25},{25,17},{2,10},{10... | collective-permute-start | bytes 983048 | tf_op jit(solution)/shard_map/ppermute | solution.py:251
  41.6 9.7 %collective-permute-start.10 = (bf16[64,1408]{1,0:T(8,128)(2,1)S(1)}, bf16[64,1408]{1,0:T(8,128)(2,1)S(1)}, u32[]{:S(2)}, u32[]{:S(2)}) collective-permute-start(bf16[64,1408]{1,0:T(8,128)(2,1)S(1)} %kernel.25), channel_id=1, source_target_pairs={{0,8},{8,0},{16,24},{24,16},{1,9},{9,1},{17,25},{25,17},{2,10},{10... | collective-permute-start | bytes 540680 | tf_op jit(solution)/shard_map/ppermute | solution.py:251
  44.4 10.3 %collective-permute-start.15 = (bf16[64,1280]{1,0:T(8,128)(2,1)S(1)}, bf16[64,1280]{1,0:T(8,128)(2,1)S(1)}, u32[]{:S(2)}, u32[]{:S(2)}) collective-permute-start(bf16[64,1280]{1,0:T(8,128)(2,1)S(1)} %kernel.29), channel_id=1, source_target_pairs={{0,8},{8,0},{16,24},{24,16},{1,9},{9,1},{17,25},{25,17},{2,10},{10... | collective-permute-start | bytes 491528 | tf_op jit(solution)/shard_map/ppermute | solution.py:251
  51.3 12.9 %collective-permute-start.11 = (bf16[64,1408]{1,0:T(8,128)(2,1)S(1)}, bf16[64,1408]{1,0:T(8,128)(2,1)S(1)}, u32[]{:S(2)}, u32[]{:S(2)}) collective-permute-start(bf16[64,1408]{1,0:T(8,128)(2,1)S(1)} %kernel.26), channel_id=1, source_target_pairs={{0,24},{8,16},{16,8},{24,0},{1,25},{9,17},{17,9},{25,1},{2,26},{10... | collective-permute-start | bytes 540680 | tf_op jit(solution)/shard_map/ppermute | solution.py:251
  54.7 9.5 %copy-start.5 = (bf16[1,1280]{1,0:T(2,128)(2,1)S(1)}, bf16[1,1280]{1,0:T(2,128)(2,1)}, u32[]{:S(2)}) copy-start(bf16[1,1280]{1,0:T(2,128)(2,1)} %bias.3) | copy-start | bytes 7684
  54.8 20.7 %copy-start.6 = (f32[8,256]{1,0:T(8,128)S(1)}, f32[8,256]{1,0:T(8,128)}, u32[]{:S(2)}) copy-start(f32[8,256]{1,0:T(8,128)} %get-tuple-element.27.gate) | copy-start | bytes 24580
  54.8 20.7 %copy-start.7 = (s32[1,256]{1,0:T(1,128)S(1)}, s32[1,256]{1,0:T(1,128)}, u32[]{:S(2)}) copy-start(s32[1,256]{1,0:T(1,128)} %get-tuple-element.25.target) | copy-start | bytes 3076
  54.8 11.2 %collective-permute-start.16 = (bf16[64,1280]{1,0:T(8,128)(2,1)S(1)}, bf16[64,1280]{1,0:T(8,128)(2,1)S(1)}, u32[]{:S(2)}, u32[]{:S(2)}) collective-permute-start(bf16[64,1280]{1,0:T(8,128)(2,1)S(1)} %kernel.30), channel_id=1, source_target_pairs={{0,24},{8,16},{16,8},{24,0},{1,25},{9,17},{17,9},{25,1},{2,26},{10... | collective-permute-start | bytes 491528 | tf_op jit(solution)/shard_map/ppermute | solution.py:251
  66.1 1.4 %collective-permute-start.17 = (bf16[32,1408]{1,0:T(8,128)(2,1)S(1)}, bf16[32,1408]{1,0:T(8,128)(2,1)S(1)}, u32[]{:S(2)}, u32[]{:S(2)}) collective-permute-start(bf16[32,1408]{1,0:T(8,128)(2,1)S(1)} %get-tuple-element.43), channel_id=1, source_target_pairs={{0,1},{1,0},{2,3},{3,2},{4,5},{5,4},{6,7},{7,6},{8,9},{9,8},{10,11... | collective-permute-start | bytes 270344 | tf_op jit(solution)/shard_map/ppermute | solution.py:251
  66.2 4.3 %collective-permute-start.12 = (bf16[32,1408]{1,0:T(8,128)(2,1)S(1)}, bf16[32,1408]{1,0:T(8,128)(2,1)S(1)}, u32[]{:S(2)}, u32[]{:S(2)}) collective-permute-start(bf16[32,1408]{1,0:T(8,128)(2,1)S(1)} %get-tuple-element.40), channel_id=1, source_target_pairs={{0,1},{1,0},{2,3},{3,2},{4,5},{5,4},{6,7},{7,6},{8,9},{9,8},{10,11... | collective-permute-start | bytes 270344 | tf_op jit(solution)/shard_map/ppermute | solution.py:251
  67.5 5.4 %collective-permute-start.18 = (bf16[32,1408]{1,0:T(8,128)(2,1)S(1)}, bf16[32,1408]{1,0:T(8,128)(2,1)S(1)}, u32[]{:S(2)}, u32[]{:S(2)}) collective-permute-start(bf16[32,1408]{1,0:T(8,128)(2,1)S(1)} %get-tuple-element.46), channel_id=1, source_target_pairs={{0,4},{1,5},{2,6},{3,7},{4,0},{5,1},{6,2},{7,3},{8,12},{9,13},{10,... | collective-permute-start | bytes 270344 | tf_op jit(solution)/shard_map/ppermute | solution.py:251
  69.0 6.2 %collective-permute-start.19 = (bf16[32,1408]{1,0:T(8,128)(2,1)S(1)}, bf16[32,1408]{1,0:T(8,128)(2,1)S(1)}, u32[]{:S(2)}, u32[]{:S(2)}) collective-permute-start(bf16[32,1408]{1,0:T(8,128)(2,1)S(1)} %get-tuple-element.47), channel_id=1, source_target_pairs={{0,6},{1,7},{2,4},{3,5},{4,2},{5,3},{6,0},{7,1},{8,14},{9,15},{10,... | collective-permute-start | bytes 270344 | tf_op jit(solution)/shard_map/ppermute | solution.py:251
  70.5 4.9 %collective-permute-start.13 = (bf16[32,1408]{1,0:T(8,128)(2,1)S(1)}, bf16[32,1408]{1,0:T(8,128)(2,1)S(1)}, u32[]{:S(2)}, u32[]{:S(2)}) collective-permute-start(bf16[32,1408]{1,0:T(8,128)(2,1)S(1)} %kernel.28), channel_id=1, source_target_pairs={{0,2},{1,3},{2,0},{3,1},{4,6},{5,7},{6,4},{7,5},{8,10},{9,11},{10,... | collective-permute-start | bytes 270344 | tf_op jit(solution)/shard_map/ppermute | solution.py:251
  (4 other events, 13.6 us)
